TPU v7x, 512 devices: a whole 4x4x16 slice. The times are simulated.
512 devices in a mesh: rows: 16 (over y_lo, x, core), cols: 32 (over y_hi, z).
Axes of the slice: x: 4, y: 4 (y_hi: 2, y_lo: 2; y = y_hi * 2 + y_lo), z: 16, core: 2. Of those that a mesh axis runs over, the one named last changes fastest.
Arguments:
- e_field: float32 [3, 128, 512, 128], P(None, 'rows', 'cols'), may hold values from -6 to 6
- h_field: float32 [3, 128, 512, 128], P(None, 'rows', 'cols'), may hold values from -6 to 6
- polar: float32 [3, 128, 512, 128], P(None, 'rows', 'cols'), may hold values from -4 to 4
- polar_rate: float32 [3, 128, 512, 128], P(None, 'rows', 'cols'), may hold values from -4 to 4
- material_id: int32 [128, 512, 128], P('rows', 'cols'), may hold values from 0 to 7
- eps_inf: float32 [8], replicated, may hold values from 1 to 6
- delta_eps: float32 [8], replicated, may hold values from 0.5 to 4
- pole_freq: float32 [8], replicated, may hold values from 0.1 to 0.6
- damping: float32 [8], replicated, may hold values from 0.02 to 0.3
- dft_acc: float32 [8, 128, 512, 128], P(None, 'rows', 'cols'), may hold values from -6 to 6
- plane_index: int32 [1], replicated, may hold values from 1 to 127
- direction_ids: int32 [256, 2], replicated, may hold values from 0 to 63
Outputs:
- e_out: float32 [3, 128, 512, 128], P(None, 'rows', 'cols')
- h_out: float32 [3, 128, 512, 128], P(None, 'rows', 'cols')
- polar_out: float32 [3, 128, 512, 128], P(None, 'rows', 'cols')
- rate_out: float32 [3, 128, 512, 128], P(None, 'rows', 'cols')
- dft_out: float32 [8, 128, 512, 128], P(None, 'rows', 'cols')
- far_field: float32 [8, 128, 256], P(None, 'rows', 'cols')
All inputs are finite; a program needn't handle non-finite values.
Results may differ from a plain program's by a relative error of at most 0.0002.
Values sent between devices are 32-bit elements; how exact they have to be, the bound alone decides.
No kernel may reach another device: no remote copies, remote signals or barrier semaphores. Data moves between devices by JAX's collectives and lax.ppermute only.
A program may use at most 64 MiB of HBM per device.

v0:
```python
import math

import jax
import jax.numpy as jnp
from jax import lax
from jax.sharding import PartitionSpec as P

STEPS = 8
F = 128
G = 64


COURANT = 0.5
OMEGA_LO = 2.0 * math.pi / 24.0
OMEGA_HI = 2.0 * math.pi / 12.0
SPREAD = 0.7
BEST_PRECISION = lax.Precision.HIGHEST


def passed_along(value, axis, steps):
    count = lax.axis_size(axis)
    initial, last = (max(0, -steps), min(count, count - steps))
    return lax.ppermute(value, axis, [(source, source + steps) for source in range(initial, last)])


def picked(shard, axis, root):
    return lax.dynamic_index_in_dim(lax.all_gather(shard, axis), root, 0, keepdims=False)


def cut_along(shard, dim, size):
    before, after = (shard.shape[:dim], shard.shape[dim + 1 :])
    return jnp.moveaxis(shard.reshape(*before, size, -1, *after), dim, 0)


def summed_on_arrival(shard, axis, dim):
    tiles = cut_along(shard, dim, lax.axis_size(axis))
    arrived = lax.all_to_all(tiles, axis, split_axis=0, concat_axis=0, tiled=True)
    return arrived.sum(axis=0)


def next_along(values, axis, rim):
    return jnp.concatenate([lax.slice_in_dim(values, 1, values.shape[axis], axis=axis), rim], axis)


def prev_along(values, axis, rim):
    return jnp.concatenate(
        [rim, lax.slice_in_dim(values, 0, values.shape[axis] - 1, axis=axis)], axis
    )


def zero_rim(values, axis):
    return jnp.zeros_like(lax.slice_in_dim(values, 0, 1, axis=axis))


def curl_forward(field_in, row_next, col_next):
    elec_x, elec_y, elec_z = (field_in[0], field_in[1], field_in[2])
    y_plus_x = next_along(elec_y, 0, row_next[0])
    z_plus_x = next_along(elec_z, 0, row_next[1])
    x_plus_y = next_along(elec_x, 1, col_next[0])
    z_plus_y = next_along(elec_z, 1, col_next[1])
    x_plus_z = next_along(elec_x, 2, zero_rim(elec_x, 2))
    y_plus_z = next_along(elec_y, 2, zero_rim(elec_y, 2))
    return jnp.stack(
        [
            z_plus_y - elec_z - (y_plus_z - elec_y),
            x_plus_z - elec_x - (z_plus_x - elec_z),
            y_plus_x - elec_y - (x_plus_y - elec_x),
        ]
    )


def curl_backward(field_in, row_prev, col_prev):
    magn_x, magn_y, magn_z = (field_in[0], field_in[1], field_in[2])
    y_minus_x = prev_along(magn_y, 0, row_prev[0])
    z_minus_x = prev_along(magn_z, 0, row_prev[1])
    x_minus_y = prev_along(magn_x, 1, col_prev[0])
    z_minus_y = prev_along(magn_z, 1, col_prev[1])
    x_minus_z = prev_along(magn_x, 2, zero_rim(magn_x, 2))
    y_minus_z = prev_along(magn_y, 2, zero_rim(magn_y, 2))
    return jnp.stack(
        [
            magn_z - z_minus_y - (magn_y - y_minus_z),
            magn_x - x_minus_z - (magn_z - z_minus_x),
            magn_y - y_minus_x - (magn_x - x_minus_y),
        ]
    )


def material_terms(material_id, eps_inf, delta_eps, pole_freq, damping):
    levels = jnp.arange(eps_inf.shape[0], dtype=jnp.int32)
    onehot = (material_id[None] == levels[:, None, None, None]).astype(eps_inf.dtype)

    def lookup(entries):
        return jnp.sum(onehot * entries[:, None, None, None], axis=0)

    half_damp = 0.5 * lookup(damping)
    pole = lookup(pole_freq)
    keep_rate = (1.0 - half_damp) / (1.0 + half_damp)
    drive_gain = pole * pole / COURANT / (1.0 + half_damp)
    return (keep_rate, drive_gain, lookup(delta_eps), COURANT / lookup(eps_inf))


def upper_rims(e_field):
    row_next = passed_along(e_field[1:3, :1], "rows", -1)
    col_next = passed_along(e_field[0:3:2, :, :1], "cols", -1)
    return (row_next, col_next)


def lower_rims(h_field):
    row_prev = passed_along(h_field[1:3, -1:], "rows", 1)
    col_prev = passed_along(h_field[0:3:2, :, -1:], "cols", 1)
    return (row_prev, col_prev)


def plane_sample(e_field, h_field, local_row):
    return jnp.concatenate(
        [
            lax.dynamic_index_in_dim(e_field[1:3], local_row, 1, keepdims=False),
            lax.dynamic_index_in_dim(h_field[1:3], local_row, 1, keepdims=False),
        ],
        0,
    )


def sample_times(count):
    return (jnp.arange(count).astype(jnp.float32) + 1.0) * COURANT


def update_dft(acc, angles, stacked):
    real_part = acc[:4] + jnp.einsum(
        "nf,ncyz->cfyz", jnp.cos(angles), stacked, precision=BEST_PRECISION
    )
    imag_part = acc[4:] - jnp.einsum(
        "nf,ncyz->cfyz", jnp.sin(angles), stacked, precision=BEST_PRECISION
    )
    return jnp.concatenate([real_part, imag_part], 0)


def currents(parts):
    return jnp.stack([-parts[3], parts[2], parts[1], -parts[0]])


def radiation(dft_block, omegas, plane_x, dir_x, dir_y, dir_z, pos_y):
    cur_real = currents(dft_block[:4])
    cur_imag = currents(dft_block[4:])
    pos_z = jnp.arange(dft_block.shape[3]).astype(jnp.float32)
    phase_z = omegas[:, None, None] * (pos_z[:, None] * dir_z[None, :])[None]
    phase_y = (
        omegas[:, None, None] * (pos_y[:, None] * dir_y[None, :] + plane_x * dir_x[None, :])[None]
    )
    cos_z, sin_z = (jnp.cos(phase_z), jnp.sin(phase_z))
    cos_y, sin_y = (jnp.cos(phase_y), jnp.sin(phase_y))
    part_real = jnp.einsum(
        "cfyz,fzd->cfyd", cur_real, cos_z, precision=BEST_PRECISION
    ) - jnp.einsum("cfyz,fzd->cfyd", cur_imag, sin_z, precision=BEST_PRECISION)
    part_imag = jnp.einsum(
        "cfyz,fzd->cfyd", cur_real, sin_z, precision=BEST_PRECISION
    ) + jnp.einsum("cfyz,fzd->cfyd", cur_imag, cos_z, precision=BEST_PRECISION)
    out_real = jnp.sum(part_real * cos_y[None] - part_imag * sin_y[None], axis=2)
    out_imag = jnp.sum(part_real * sin_y[None] + part_imag * cos_y[None], axis=2)
    return jnp.concatenate([out_real, out_imag], 0)


def local(
    e_field,
    h_field,
    polar,
    polar_rate,
    material_id,
    eps_inf,
    delta_eps,
    pole_freq,
    damping,
    dft_acc,
    plane_index,
    direction_ids,
):
    cells_x = e_field.shape[1]
    cells_y = e_field.shape[2]
    cells_z = e_field.shape[3]
    freq_block = dft_acc.shape[1]
    keep_rate, drive_gain, coupled, e_scale = material_terms(
        material_id, eps_inf, delta_eps, pole_freq, damping
    )
    plane_row = plane_index[0]
    root_row = plane_row // cells_x
    local_row = plane_row % cells_x
    freq_ids = lax.axis_index("rows") * freq_block + jnp.arange(freq_block, dtype=jnp.int32)
    omegas = OMEGA_LO + (OMEGA_HI - OMEGA_LO) * (freq_ids.astype(jnp.float32) / (F - 1))
    all_times = sample_times(STEPS)
    dft_out = dft_acc
    samples = []
    for step_index in range(STEPS):
        row_next, col_next = upper_rims(e_field)
        h_field = h_field - COURANT * curl_forward(e_field, row_next, col_next)
        rate_new = keep_rate * polar_rate + drive_gain * (coupled * e_field - polar)
        polar = polar + COURANT * rate_new
        row_prev, col_prev = lower_rims(h_field)
        e_field = e_field + e_scale * (curl_backward(h_field, row_prev, col_prev) - rate_new)
        polar_rate = rate_new
        sample = plane_sample(e_field, h_field, local_row)
        samples.append(sample)
    received = picked(jnp.stack(samples), "rows", root_row)
    angles = all_times[:, None] * omegas[None, :]
    dft_out = update_dft(dft_out, angles, received)
    ids_float = direction_ids.astype(jnp.float32)
    dir_y = SPREAD * (2.0 * ids_float[:, 0] / (G - 1) - 1.0)
    dir_z = SPREAD * (2.0 * ids_float[:, 1] / (G - 1) - 1.0)
    dir_x = jnp.sqrt(1.0 - dir_y * dir_y - dir_z * dir_z)
    pos_y = (lax.axis_index("cols") * cells_y + jnp.arange(cells_y, dtype=jnp.int32)).astype(
        jnp.float32
    )
    partial_value = radiation(
        dft_out, omegas, plane_row.astype(jnp.float32), dir_x, dir_y, dir_z, pos_y
    )
    total_y = lax.axis_size("cols") * cells_y
    far_field = summed_on_arrival(partial_value, "cols", 2) * (1.0 / math.sqrt(total_y * cells_z))
    return (e_field, h_field, polar, polar_rate, dft_out, far_field)


def solution(mesh):
    in_specs = (
        P(None, "rows", "cols", None),
        P(None, "rows", "cols", None),
        P(None, "rows", "cols", None),
        P(None, "rows", "cols", None),
        P("rows", "cols", None),
        P(),
        P(),
        P(),
        P(),
        P(None, "rows", "cols", None),
        P(),
        P(),
    )
    out_specs = (
        P(None, "rows", "cols", None),
        P(None, "rows", "cols", None),
        P(None, "rows", "cols", None),
        P(None, "rows", "cols", None),
        P(None, "rows", "cols", None),
        P(None, "rows", "cols"),
    )
    return jax.shard_map(local, mesh=mesh, in_specs=in_specs, out_specs=out_specs, check_vma=False)
```

profile of v0, /device:TPU:2, one launch (start us, length us, event | category | flops | bytes accessed | tf_op | source)
XLA Modules:
  0.0 283.7 jit_solution(11405190134189713704)
XLA Ops:
  8.1 1.9 collective-permute-start.1
  19.4 1.9 collective-permute-start.3
  21.4 4.4 %collective-permute-start.2 = (f32[2,8,1,128]{3,1,2,0:T(8,128)S(1)}, f32[2,8,1,128]{3,1,2,0:T(8,128)S(1)}, u32[]{:S(2)}, u32[]{:S(2)}) collective-permute-start(f32[2,8,1,128]{3,1,2,0:T(8,128)S(1)} %bitcast.629), channel_id=1, source_target_pairs={{0,1},{1,2},{2,3},{3,4},{4,5},{5,6},{6,7},{7,8},{8,9},{9,10},{10,1... | collective-permute-start | bytes 24584 | tf_op jit(solution)/shard_map/ppermute | solution.py:23
  25.8 1.3 collective-permute-done.2
  28.6 1.3 collective-permute-start.4
  30.0 5.3 %collective-permute-start.5 = (f32[2,1,16,128]{3,2,1,0:T(8,128)S(1)}, f32[2,1,16,128]{3,2,1,0:T(8,128)S(1)}, u32[]{:S(2)}, u32[]{:S(2)}) collective-permute-start(f32[2,1,16,128]{3,2,1,0:T(8,128)S(1)} %slice.1214), channel_id=1, source_target_pairs={{32,0},{64,32},{96,64},{128,96},{160,128},{192,160},{224,192},{256... | collective-permute-start | bytes 49160 | tf_op jit(solution)/shard_map/ppermute | solution.py:23
  35.3 1.4 collective-permute-done.5
  37.0 1.9 collective-permute-start.7
  39.0 4.5 %collective-permute-start.6 = (f32[2,8,1,128]{3,1,2,0:T(8,128)S(1)}, f32[2,8,1,128]{3,1,2,0:T(8,128)S(1)}, u32[]{:S(2)}, u32[]{:S(2)}) collective-permute-start(f32[2,8,1,128]{3,1,2,0:T(8,128)S(1)} %bitcast.630), channel_id=1, source_target_pairs={{0,1},{1,2},{2,3},{3,4},{4,5},{5,6},{6,7},{7,8},{8,9},{9,10},{10,1... | collective-permute-start | bytes 24584 | tf_op jit(solution)/shard_map/ppermute | solution.py:23
  43.5 1.3 collective-permute-done.6
  45.2 1.3 collective-permute-start.8
  46.6 2.8 collective-permute-start.9
  49.4 1.6 collective-permute-done.8
  51.3 1.9 collective-permute-start.11
  53.3 4.3 %collective-permute-start.10 = (f32[2,8,1,128]{3,1,2,0:T(8,128)S(1)}, f32[2,8,1,128]{3,1,2,0:T(8,128)S(1)}, u32[]{:S(2)}, u32[]{:S(2)}) collective-permute-start(f32[2,8,1,128]{3,1,2,0:T(8,128)S(1)} %bitcast.631), channel_id=1, source_target_pairs={{0,1},{1,2},{2,3},{3,4},{4,5},{5,6},{6,7},{7,8},{8,9},{9,10},{10,1... | collective-permute-start | bytes 24584 | tf_op jit(solution)/shard_map/ppermute | solution.py:23
  57.6 1.3 collective-permute-done.10
  60.7 2.8 collective-permute-start.13
  63.5 1.6 collective-permute-done.12
  65.5 5.4 %collective-permute-start.15 = (f32[2,1,16,128]{3,2,1,0:T(8,128)S(1)}, f32[2,1,16,128]{3,2,1,0:T(8,128)S(1)}, u32[]{:S(2)}, u32[]{:S(2)}) collective-permute-start(f32[2,1,16,128]{3,2,1,0:T(8,128)S(1)} %slice.1283), channel_id=1, source_target_pairs={{0,32},{32,64},{64,96},{96,128},{128,160},{160,192},{192,224},{224... | collective-permute-start | bytes 49160 | tf_op jit(solution)/shard_map/ppermute | solution.py:23
  71.0 4.8 %collective-permute-start.14 = (f32[2,8,1,128]{3,1,2,0:T(8,128)S(1)}, f32[2,8,1,128]{3,1,2,0:T(8,128)S(1)}, u32[]{:S(2)}, u32[]{:S(2)}) collective-permute-start(f32[2,8,1,128]{3,1,2,0:T(8,128)S(1)} %bitcast.632), channel_id=1, source_target_pairs={{0,1},{1,2},{2,3},{3,4},{4,5},{5,6},{6,7},{7,8},{8,9},{9,10},{10,1... | collective-permute-start | bytes 24584 | tf_op jit(solution)/shard_map/ppermute | solution.py:23
  75.8 1.3 collective-permute-done.14
  79.0 1.9 collective-permute-start.17
  80.9 3.3 %collective-permute-done.16 = f32[2,8,1,128]{3,2,1,0:T(1,128)S(1)} collective-permute-done((f32[2,8,1,128]{3,2,1,0:T(1,128)S(1)}, f32[2,8,1,128]{3,2,1,0:T(1,128)S(1)}, u32[]{:S(2)}, u32[]{:S(2)}) %collective-permute-start.16) | collective-permute-done | bytes 8224 | tf_op jit(solution)/shard_map/ppermute | solution.py:23
  84.5 3.1 %collective-permute-start.19 = (f32[2,1,16,128]{3,2,1,0:T(8,128)S(1)}, f32[2,1,16,128]{3,2,1,0:T(8,128)S(1)}, u32[]{:S(2)}, u32[]{:S(2)}) collective-permute-start(f32[2,1,16,128]{3,2,1,0:T(8,128)S(1)} %slice.1311), channel_id=1, source_target_pairs={{0,32},{32,64},{64,96},{96,128},{128,160},{160,192},{192,224},{224... | collective-permute-start | bytes 49160 | tf_op jit(solution)/shard_map/ppermute | solution.py:23
  87.6 5.6 %collective-permute-start.18 = (f32[2,8,1,128]{3,1,2,0:T(8,128)S(1)}, f32[2,8,1,128]{3,1,2,0:T(8,128)S(1)}, u32[]{:S(2)}, u32[]{:S(2)}) collective-permute-start(f32[2,8,1,128]{3,1,2,0:T(8,128)S(1)} %bitcast.633), channel_id=1, source_target_pairs={{0,1},{1,2},{2,3},{3,4},{4,5},{5,6},{6,7},{7,8},{8,9},{9,10},{10,1... | collective-permute-start | bytes 24584 | tf_op jit(solution)/shard_map/ppermute | solution.py:23
  93.2 1.3 collective-permute-done.18
  96.4 1.9 collective-permute-start.21
  98.3 3.6 %collective-permute-done.20 = f32[2,8,1,128]{3,2,1,0:T(1,128)S(1)} collective-permute-done((f32[2,8,1,128]{3,2,1,0:T(1,128)S(1)}, f32[2,8,1,128]{3,2,1,0:T(1,128)S(1)}, u32[]{:S(2)}, u32[]{:S(2)}) %collective-permute-start.20) | collective-permute-done | bytes 8224 | tf_op jit(solution)/shard_map/ppermute | solution.py:23
  102.3 2.7 collective-permute-start.23
  105.0 5.7 %collective-permute-start.22 = (f32[2,8,1,128]{3,1,2,0:T(8,128)S(1)}, f32[2,8,1,128]{3,1,2,0:T(8,128)S(1)}, u32[]{:S(2)}, u32[]{:S(2)}) collective-permute-start(f32[2,8,1,128]{3,1,2,0:T(8,128)S(1)} %bitcast.634), channel_id=1, source_target_pairs={{0,1},{1,2},{2,3},{3,4},{4,5},{5,6},{6,7},{7,8},{8,9},{9,10},{10,1... | collective-permute-start | bytes 24584 | tf_op jit(solution)/shard_map/ppermute | solution.py:23
  110.8 1.3 collective-permute-done.22
  113.8 1.9 collective-permute-start.25
  115.8 3.4 %collective-permute-done.24 = f32[2,8,1,128]{3,1,2,0:T(8,128)S(1)} collective-permute-done((f32[2,8,1,128]{3,1,2,0:T(8,128)S(1)}, f32[2,8,1,128]{3,1,2,0:T(8,128)S(1)}, u32[]{:S(2)}, u32[]{:S(2)}) %collective-permute-start.24) | collective-permute-done | bytes 8224 | tf_op jit(solution)/shard_map/ppermute | solution.py:23
  119.6 2.9 %collective-permute-start.27 = (f32[2,1,16,128]{3,2,1,0:T(8,128)S(1)}, f32[2,1,16,128]{3,2,1,0:T(8,128)S(1)}, u32[]{:S(2)}, u32[]{:S(2)}) collective-permute-start(f32[2,1,16,128]{3,2,1,0:T(8,128)S(1)} %slice.1367), channel_id=1, source_target_pairs={{0,32},{32,64},{64,96},{96,128},{128,160},{160,192},{192,224},{224... | collective-permute-start | bytes 49160 | tf_op jit(solution)/shard_map/ppermute | solution.py:23
  122.5 5.7 %collective-permute-start.26 = (f32[2,8,1,128]{3,1,2,0:T(8,128)S(1)}, f32[2,8,1,128]{3,1,2,0:T(8,128)S(1)}, u32[]{:S(2)}, u32[]{:S(2)}) collective-permute-start(f32[2,8,1,128]{3,1,2,0:T(8,128)S(1)} %bitcast.635), channel_id=1, source_target_pairs={{0,1},{1,2},{2,3},{3,4},{4,5},{5,6},{6,7},{7,8},{8,9},{9,10},{10,1... | collective-permute-start | bytes 24584 | tf_op jit(solution)/shard_map/ppermute | solution.py:23
  128.2 1.3 collective-permute-done.26
  130.7 1.4 collective-permute-start.28
  132.2 1.9 collective-permute-start.29
  134.1 3.4 %collective-permute-done.28 = f32[2,8,1,128]{3,1,2,0:T(8,128)S(1)} collective-permute-done((f32[2,8,1,128]{3,1,2,0:T(8,128)S(1)}, f32[2,8,1,128]{3,1,2,0:T(8,128)S(1)}, u32[]{:S(2)}, u32[]{:S(2)}) %collective-permute-start.28) | collective-permute-done | bytes 8224 | tf_op jit(solution)/shard_map/ppermute | solution.py:23
  138.0 2.9 %collective-permute-start.31 = (f32[2,1,16,128]{3,2,1,0:T(8,128)S(1)}, f32[2,1,16,128]{3,2,1,0:T(8,128)S(1)}, u32[]{:S(2)}, u32[]{:S(2)}) collective-permute-start(f32[2,1,16,128]{3,2,1,0:T(8,128)S(1)} %slice.1395), channel_id=1, source_target_pairs={{0,32},{32,64},{64,96},{96,128},{128,160},{160,192},{192,224},{224... | collective-permute-start | bytes 49160 | tf_op jit(solution)/shard_map/ppermute | solution.py:23
  140.9 5.9 %collective-permute-start.30 = (f32[2,8,1,128]{3,1,2,0:T(8,128)S(1)}, f32[2,8,1,128]{3,1,2,0:T(8,128)S(1)}, u32[]{:S(2)}, u32[]{:S(2)}) collective-permute-start(f32[2,8,1,128]{3,1,2,0:T(8,128)S(1)} %bitcast.636), channel_id=1, source_target_pairs={{0,1},{1,2},{2,3},{3,4},{4,5},{5,6},{6,7},{7,8},{8,9},{9,10},{10,1... | collective-permute-start | bytes 24584 | tf_op jit(solution)/shard_map/ppermute | solution.py:23
  149.9 70.9 %all-gather.3.cloned.1.call-done = f32[128,4,16,128]{3,2,1,0:T(8,128)} async-done(((f32[8,4,16,128]{3,2,1,0:T(8,128)}), f32[128,4,16,128]{3,2,1,0:T(8,128)}) %all-gather.3.cloned.1.call-update) | async-done | bytes 4194320 | tf_op jit(solution)/shard_map/all_gather | solution.py:27
  222.5 4.1 %fusion.6 = f32[8,256,4,16]{1,3,2,0:T(8,128)S(1)} fusion(f32[128,256]{1,0:T(8,128)S(1)} %broadcast_multiply_fusion, f32[8]{0:T(128)S(1)} %get-tuple-element.239, f32[4,8,16,128]{3,1,2,0:T(8,128)S(1)} %pad_maximum_fusion.1), kind=kOutput, calls=%fused_computation.11 | convolution fusion | flops 201588736 | bytes 917536 | tf_op jit(solution)/shard_map/cfyz,fzd->cfyd/dot_general | solution.py:153
  226.6 4.2 %fusion.9 = f32[8,256,4,16]{1,3,2,0:T(8,128)S(1)} fusion(f32[128,256]{1,0:T(8,128)S(1)} %broadcast_multiply_fusion, f32[8]{0:T(128)S(1)} %get-tuple-element.239, f32[4,8,16,128]{3,1,2,0:T(8,128)S(1)} %pad_maximum_fusion.1), kind=kOutput, calls=%fused_computation.13 | convolution fusion | flops 201588736 | bytes 917536 | tf_op jit(solution)/shard_map/cfyz,fzd->cfyd/dot_general | solution.py:156
  231.4 4.4 %fusion.1 = f32[4,8,16,256]{3,2,0,1:T(8,128)S(1)} fusion(f32[8,256,4,16]{1,3,2,0:T(8,128)S(1)} %fusion.6, f32[128,256]{1,0:T(8,128)S(1)} %broadcast_multiply_fusion, f32[8]{0:T(128)S(1)} %get-tuple-element.239, f32[4,8,16,128]{3,1,2,0:T(8,128)S(1)} %pad_maximum_fusion.2), kind=kOutput, calls=%fused_computation.5 | convolution fusion | flops 201719808 | bytes 1441824 | tf_op jit(solution)/shard_map/cfyz,fzd->cfyd/dot_general | solution.py:155
  235.8 4.9 %subtract_reduce_fusion = (f32[4,8,256]{2,0,1:T(4,128)S(1)}, f32[4,8,256]{2,0,1:T(4,128)S(1)}) fusion(f32[4,8,16,256]{3,2,0,1:T(8,128)S(1)} %fusion.1, f32[8,16,256]{2,1,0:T(8,128)S(1)} %get-tuple-element.171, f32[8,16,256]{2,1,0:T(8,128)S(1)} %get-tuple-element.170, f32[8,256,4,16]{1,3,2,0:T(8,128)S(1)} %fusion.9, ...), kind=kOutput, calls=%fused_computation.16 | convolution fusion | flops 202752000 | bytes 1769504 | tf_op jit(solution)/shard_map/cfyz,fzd->cfyd/dot_general | solution.py:158
  243.2 14.9 %all-to-all-start = ((f32[32,1,512]{2,1,0:T(1,128)}), f32[32,1,512]{2,1,0:T(1,128)S(1)}, u32[]{:S(2)}, u32[]{:S(2)}) async-start(f32[32,1,512]{2,1,0:T(1,128)} %reshape.327), calls=%async_computation | async-start | bytes 131072 | tf_op jit(solution)/shard_map/all_to_all | solution.py:37
  259.0 15.3 %all-to-all-done = f32[32,1,512]{2,1,0:T(1,128)S(1)} async-done(((f32[32,1,512]{2,1,0:T(1,128)}), f32[32,1,512]{2,1,0:T(1,128)S(1)}, u32[]{:S(2)}, u32[]{:S(2)}) %all-to-all-start) | async-done | bytes 65568 | tf_op jit(solution)/shard_map/all_to_all | solution.py:37
  (300 shorter events, 32.5 us)
Async XLA Ops:
  7.2 21.2 %copy-start.3 = (f32[3,8,16,128]{3,2,1,0:T(8,128)S(1)}, f32[3,8,16,128]{3,2,1,0:T(8,128)}, u32[]{:S(2)}) copy-start(f32[3,8,16,128]{3,2,1,0:T(8,128)} %param.12) | copy-start | bytes 589828
  7.2 21.2 %copy-start.1 = (f32[3,8,16,128]{3,2,1,0:T(8,128)S(1)}, f32[3,8,16,128]{3,2,1,0:T(8,128)}, u32[]{:S(2)}) copy-start(f32[3,8,16,128]{3,2,1,0:T(8,128)} %param.14) | copy-start | bytes 589828
  7.2 21.2 %copy-start.8 = (f32[3,8,16,128]{3,2,1,0:T(8,128)S(1)}, f32[3,8,16,128]{3,2,1,0:T(8,128)}, u32[]{:S(2)}) copy-start(f32[3,8,16,128]{3,2,1,0:T(8,128)} %param.15) | copy-start | bytes 589828
  7.2 213.6 %all-gather.3.cloned.1.call-start = ((), (), s32[]{:S(2)}) async-start(), calls=%async_computation.1 | async-start | bytes 4456448 | tf_op jit(solution)/shard_map/all_gather | solution.py:27
  8.1 8.3 %collective-permute-start.1 = (f32[2,1,16,128]{3,2,1,0:T(8,128)S(1)}, f32[2,1,16,128]{3,2,1,0:T(8,128)S(1)}, u32[]{:S(2)}, u32[]{:S(2)}) collective-permute-start(f32[2,1,16,128]{3,2,1,0:T(8,128)S(1)} %slice.910), channel_id=1, source_target_pairs={{32,0},{64,32},{96,64},{128,96},{160,128},{192,160},{224,192},{256... | collective-permute-start | bytes 49160 | tf_op jit(solution)/shard_map/ppermute | solution.py:23
  10.9 5.5 %collective-permute-start = (f32[2,8,1,128]{3,2,1,0:T(1,128)S(1)}, f32[2,8,1,128]{3,2,1,0:T(1,128)S(1)}, u32[]{:S(2)}, u32[]{:S(2)}) collective-permute-start(f32[2,8,1,128]{3,2,1,0:T(1,128)S(1)} %slice.902), channel_id=1, source_target_pairs={{1,0},{2,1},{3,2},{4,3},{5,4},{6,5},{7,6},{8,7},{9,8},{10,9},{11,1... | collective-permute-start | bytes 24584 | tf_op jit(solution)/shard_map/ppermute | solution.py:23
  14.2 22.7 %copy-start = (f32[3,8,16,128]{3,2,1,0:T(8,128)S(1)}, f32[3,8,16,128]{3,2,1,0:T(8,128)}, u32[]{:S(2)}) copy-start(f32[3,8,16,128]{3,2,1,0:T(8,128)} %param.13) | copy-start | bytes 589828
  19.4 8.8 %collective-permute-start.3 = (f32[2,1,16,128]{3,2,1,0:T(8,128)S(1)}, f32[2,1,16,128]{3,2,1,0:T(8,128)S(1)}, u32[]{:S(2)}, u32[]{:S(2)}) collective-permute-start(f32[2,1,16,128]{3,2,1,0:T(8,128)S(1)} %slice.1199), channel_id=1, source_target_pairs={{0,32},{32,64},{64,96},{96,128},{128,160},{160,192},{192,224},{224... | collective-permute-start | bytes 49160 | tf_op jit(solution)/shard_map/ppermute | solution.py:23
  21.4 5.8 %collective-permute-start.2 = (f32[2,8,1,128]{3,1,2,0:T(8,128)S(1)}, f32[2,8,1,128]{3,1,2,0:T(8,128)S(1)}, u32[]{:S(2)}, u32[]{:S(2)}) collective-permute-start(f32[2,8,1,128]{3,1,2,0:T(8,128)S(1)} %bitcast.629), channel_id=1, source_target_pairs={{0,1},{1,2},{2,3},{3,4},{4,5},{5,6},{6,7},{7,8},{8,9},{9,10},{10,1... | collective-permute-start | bytes 24584 | tf_op jit(solution)/shard_map/ppermute | solution.py:23
  28.6 6.7 %collective-permute-start.4 = (f32[2,8,1,128]{3,2,1,0:T(1,128)S(1)}, f32[2,8,1,128]{3,2,1,0:T(1,128)S(1)}, u32[]{:S(2)}, u32[]{:S(2)}) collective-permute-start(f32[2,8,1,128]{3,2,1,0:T(1,128)S(1)} %slice.934), channel_id=1, source_target_pairs={{1,0},{2,1},{3,2},{4,3},{5,4},{6,5},{7,6},{8,7},{9,8},{10,9},{11,1... | collective-permute-start | bytes 24584 | tf_op jit(solution)/shard_map/ppermute | solution.py:23
  30.0 6.7 %collective-permute-start.5 = (f32[2,1,16,128]{3,2,1,0:T(8,128)S(1)}, f32[2,1,16,128]{3,2,1,0:T(8,128)S(1)}, u32[]{:S(2)}, u32[]{:S(2)}) collective-permute-start(f32[2,1,16,128]{3,2,1,0:T(8,128)S(1)} %slice.1214), channel_id=1, source_target_pairs={{32,0},{64,32},{96,64},{128,96},{160,128},{192,160},{224,192},{256... | collective-permute-start | bytes 49160 | tf_op jit(solution)/shard_map/ppermute | solution.py:23
  37.0 7.8 %collective-permute-start.7 = (f32[2,1,16,128]{3,2,1,0:T(8,128)S(1)}, f32[2,1,16,128]{3,2,1,0:T(8,128)S(1)}, u32[]{:S(2)}, u32[]{:S(2)}) collective-permute-start(f32[2,1,16,128]{3,2,1,0:T(8,128)S(1)} %slice.1227), channel_id=1, source_target_pairs={{0,32},{32,64},{64,96},{96,128},{128,160},{160,192},{192,224},{224... | collective-permute-start | bytes 49160 | tf_op jit(solution)/shard_map/ppermute | solution.py:23
  39.0 5.9 %collective-permute-start.6 = (f32[2,8,1,128]{3,1,2,0:T(8,128)S(1)}, f32[2,8,1,128]{3,1,2,0:T(8,128)S(1)}, u32[]{:S(2)}, u32[]{:S(2)}) collective-permute-start(f32[2,8,1,128]{3,1,2,0:T(8,128)S(1)} %bitcast.630), channel_id=1, source_target_pairs={{0,1},{1,2},{2,3},{3,4},{4,5},{5,6},{6,7},{7,8},{8,9},{9,10},{10,1... | collective-permute-start | bytes 24584 | tf_op jit(solution)/shard_map/ppermute | solution.py:23
  45.2 5.8 %collective-permute-start.8 = (f32[2,8,1,128]{3,2,1,0:T(1,128)S(1)}, f32[2,8,1,128]{3,2,1,0:T(1,128)S(1)}, u32[]{:S(2)}, u32[]{:S(2)}) collective-permute-start(f32[2,8,1,128]{3,2,1,0:T(1,128)S(1)} %slice.966), channel_id=1, source_target_pairs={{1,0},{2,1},{3,2},{4,3},{5,4},{6,5},{7,6},{8,7},{9,8},{10,9},{11,1... | collective-permute-start | bytes 24584 | tf_op jit(solution)/shard_map/ppermute | solution.py:23
  46.6 4.4 %collective-permute-start.9 = (f32[2,1,16,128]{3,2,1,0:T(8,128)S(1)}, f32[2,1,16,128]{3,2,1,0:T(8,128)S(1)}, u32[]{:S(2)}, u32[]{:S(2)}) collective-permute-start(f32[2,1,16,128]{3,2,1,0:T(8,128)S(1)} %slice.1242), channel_id=1, source_target_pairs={{32,0},{64,32},{96,64},{128,96},{160,128},{192,160},{224,192},{256... | collective-permute-start | bytes 49160 | tf_op jit(solution)/shard_map/ppermute | solution.py:23
  51.3 7.6 %collective-permute-start.11 = (f32[2,1,16,128]{3,2,1,0:T(8,128)S(1)}, f32[2,1,16,128]{3,2,1,0:T(8,128)S(1)}, u32[]{:S(2)}, u32[]{:S(2)}) collective-permute-start(f32[2,1,16,128]{3,2,1,0:T(8,128)S(1)} %slice.1255), channel_id=1, source_target_pairs={{0,32},{32,64},{64,96},{96,128},{128,160},{160,192},{192,224},{224... | collective-permute-start | bytes 49160 | tf_op jit(solution)/shard_map/ppermute | solution.py:23
  53.3 5.7 %collective-permute-start.10 = (f32[2,8,1,128]{3,1,2,0:T(8,128)S(1)}, f32[2,8,1,128]{3,1,2,0:T(8,128)S(1)}, u32[]{:S(2)}, u32[]{:S(2)}) collective-permute-start(f32[2,8,1,128]{3,1,2,0:T(8,128)S(1)} %bitcast.631), channel_id=1, source_target_pairs={{0,1},{1,2},{2,3},{3,4},{4,5},{5,6},{6,7},{7,8},{8,9},{9,10},{10,1... | collective-permute-start | bytes 24584 | tf_op jit(solution)/shard_map/ppermute | solution.py:23
  59.3 5.8 %collective-permute-start.12 = (f32[2,8,1,128]{3,2,1,0:T(1,128)S(1)}, f32[2,8,1,128]{3,2,1,0:T(1,128)S(1)}, u32[]{:S(2)}, u32[]{:S(2)}) collective-permute-start(f32[2,8,1,128]{3,2,1,0:T(1,128)S(1)} %slice.998), channel_id=1, source_target_pairs={{1,0},{2,1},{3,2},{4,3},{5,4},{6,5},{7,6},{8,7},{9,8},{10,9},{11,1... | collective-permute-start | bytes 24584 | tf_op jit(solution)/shard_map/ppermute | solution.py:23
  60.7 4.4 %collective-permute-start.13 = (f32[2,1,16,128]{3,2,1,0:T(8,128)S(1)}, f32[2,1,16,128]{3,2,1,0:T(8,128)S(1)}, u32[]{:S(2)}, u32[]{:S(2)}) collective-permute-start(f32[2,1,16,128]{3,2,1,0:T(8,128)S(1)} %slice.1270), channel_id=1, source_target_pairs={{32,0},{64,32},{96,64},{128,96},{160,128},{192,160},{224,192},{256... | collective-permute-start | bytes 49160 | tf_op jit(solution)/shard_map/ppermute | solution.py:23
  65.5 11.6 %collective-permute-start.15 = (f32[2,1,16,128]{3,2,1,0:T(8,128)S(1)}, f32[2,1,16,128]{3,2,1,0:T(8,128)S(1)}, u32[]{:S(2)}, u32[]{:S(2)}) collective-permute-start(f32[2,1,16,128]{3,2,1,0:T(8,128)S(1)} %slice.1283), channel_id=1, source_target_pairs={{0,32},{32,64},{64,96},{96,128},{128,160},{160,192},{192,224},{224... | collective-permute-start | bytes 49160 | tf_op jit(solution)/shard_map/ppermute | solution.py:23
  71.0 6.2 %collective-permute-start.14 = (f32[2,8,1,128]{3,1,2,0:T(8,128)S(1)}, f32[2,8,1,128]{3,1,2,0:T(8,128)S(1)}, u32[]{:S(2)}, u32[]{:S(2)}) collective-permute-start(f32[2,8,1,128]{3,1,2,0:T(8,128)S(1)} %bitcast.632), channel_id=1, source_target_pairs={{0,1},{1,2},{2,3},{3,4},{4,5},{5,6},{6,7},{7,8},{8,9},{9,10},{10,1... | collective-permute-start | bytes 24584 | tf_op jit(solution)/shard_map/ppermute | solution.py:23
  77.6 6.6 %collective-permute-start.16 = (f32[2,8,1,128]{3,2,1,0:T(1,128)S(1)}, f32[2,8,1,128]{3,2,1,0:T(1,128)S(1)}, u32[]{:S(2)}, u32[]{:S(2)}) collective-permute-start(f32[2,8,1,128]{3,2,1,0:T(1,128)S(1)} %slice.1030), channel_id=1, source_target_pairs={{1,0},{2,1},{3,2},{4,3},{5,4},{6,5},{7,6},{8,7},{9,8},{10,9},{11,1... | collective-permute-start | bytes 24584 | tf_op jit(solution)/shard_map/ppermute | solution.py:23
  79.0 5.2 %collective-permute-start.17 = (f32[2,1,16,128]{3,2,1,0:T(8,128)S(1)}, f32[2,1,16,128]{3,2,1,0:T(8,128)S(1)}, u32[]{:S(2)}, u32[]{:S(2)}) collective-permute-start(f32[2,1,16,128]{3,2,1,0:T(8,128)S(1)} %slice.1298), channel_id=1, source_target_pairs={{32,0},{64,32},{96,64},{128,96},{160,128},{192,160},{224,192},{256... | collective-permute-start | bytes 49160 | tf_op jit(solution)/shard_map/ppermute | solution.py:23
  84.5 10.0 %collective-permute-start.19 = (f32[2,1,16,128]{3,2,1,0:T(8,128)S(1)}, f32[2,1,16,128]{3,2,1,0:T(8,128)S(1)}, u32[]{:S(2)}, u32[]{:S(2)}) collective-permute-start(f32[2,1,16,128]{3,2,1,0:T(8,128)S(1)} %slice.1311), channel_id=1, source_target_pairs={{0,32},{32,64},{64,96},{96,128},{128,160},{160,192},{192,224},{224... | collective-permute-start | bytes 49160 | tf_op jit(solution)/shard_map/ppermute | solution.py:23
  87.6 6.9 %collective-permute-start.18 = (f32[2,8,1,128]{3,1,2,0:T(8,128)S(1)}, f32[2,8,1,128]{3,1,2,0:T(8,128)S(1)}, u32[]{:S(2)}, u32[]{:S(2)}) collective-permute-start(f32[2,8,1,128]{3,1,2,0:T(8,128)S(1)} %bitcast.633), channel_id=1, source_target_pairs={{0,1},{1,2},{2,3},{3,4},{4,5},{5,6},{6,7},{7,8},{8,9},{9,10},{10,1... | collective-permute-start | bytes 24584 | tf_op jit(solution)/shard_map/ppermute | solution.py:23
  95.0 6.9 %collective-permute-start.20 = (f32[2,8,1,128]{3,2,1,0:T(1,128)S(1)}, f32[2,8,1,128]{3,2,1,0:T(1,128)S(1)}, u32[]{:S(2)}, u32[]{:S(2)}) collective-permute-start(f32[2,8,1,128]{3,2,1,0:T(1,128)S(1)} %slice.1062), channel_id=1, source_target_pairs={{1,0},{2,1},{3,2},{4,3},{5,4},{6,5},{7,6},{8,7},{9,8},{10,9},{11,1... | collective-permute-start | bytes 24584 | tf_op jit(solution)/shard_map/ppermute | solution.py:23
  96.4 5.5 %collective-permute-start.21 = (f32[2,1,16,128]{3,2,1,0:T(8,128)S(1)}, f32[2,1,16,128]{3,2,1,0:T(8,128)S(1)}, u32[]{:S(2)}, u32[]{:S(2)}) collective-permute-start(f32[2,1,16,128]{3,2,1,0:T(8,128)S(1)} %slice.1326), channel_id=1, source_target_pairs={{32,0},{64,32},{96,64},{128,96},{160,128},{192,160},{224,192},{256... | collective-permute-start | bytes 49160 | tf_op jit(solution)/shard_map/ppermute | solution.py:23
  102.3 9.8 %collective-permute-start.23 = (f32[2,1,16,128]{3,2,1,0:T(8,128)S(1)}, f32[2,1,16,128]{3,2,1,0:T(8,128)S(1)}, u32[]{:S(2)}, u32[]{:S(2)}) collective-permute-start(f32[2,1,16,128]{3,2,1,0:T(8,128)S(1)} %slice.1339), channel_id=1, source_target_pairs={{0,32},{32,64},{64,96},{96,128},{128,160},{160,192},{192,224},{224... | collective-permute-start | bytes 49160 | tf_op jit(solution)/shard_map/ppermute | solution.py:23
  105.0 7.1 %collective-permute-start.22 = (f32[2,8,1,128]{3,1,2,0:T(8,128)S(1)}, f32[2,8,1,128]{3,1,2,0:T(8,128)S(1)}, u32[]{:S(2)}, u32[]{:S(2)}) collective-permute-start(f32[2,8,1,128]{3,1,2,0:T(8,128)S(1)} %bitcast.634), channel_id=1, source_target_pairs={{0,1},{1,2},{2,3},{3,4},{4,5},{5,6},{6,7},{7,8},{8,9},{9,10},{10,1... | collective-permute-start | bytes 24584 | tf_op jit(solution)/shard_map/ppermute | solution.py:23
  112.4 6.7 %collective-permute-start.24 = (f32[2,8,1,128]{3,1,2,0:T(8,128)S(1)}, f32[2,8,1,128]{3,1,2,0:T(8,128)S(1)}, u32[]{:S(2)}, u32[]{:S(2)}) collective-permute-start(f32[2,8,1,128]{3,1,2,0:T(8,128)S(1)} %bitcast.627), channel_id=1, source_target_pairs={{1,0},{2,1},{3,2},{4,3},{5,4},{6,5},{7,6},{8,7},{9,8},{10,9},{11,1... | collective-permute-start | bytes 24584 | tf_op jit(solution)/shard_map/ppermute | solution.py:23
  113.8 5.3 %collective-permute-start.25 = (f32[2,1,16,128]{3,2,1,0:T(8,128)S(1)}, f32[2,1,16,128]{3,2,1,0:T(8,128)S(1)}, u32[]{:S(2)}, u32[]{:S(2)}) collective-permute-start(f32[2,1,16,128]{3,2,1,0:T(8,128)S(1)} %slice.1354), channel_id=1, source_target_pairs={{32,0},{64,32},{96,64},{128,96},{160,128},{192,160},{224,192},{256... | collective-permute-start | bytes 49160 | tf_op jit(solution)/shard_map/ppermute | solution.py:23
  119.6 10.0 %collective-permute-start.27 = (f32[2,1,16,128]{3,2,1,0:T(8,128)S(1)}, f32[2,1,16,128]{3,2,1,0:T(8,128)S(1)}, u32[]{:S(2)}, u32[]{:S(2)}) collective-permute-start(f32[2,1,16,128]{3,2,1,0:T(8,128)S(1)} %slice.1367), channel_id=1, source_target_pairs={{0,32},{32,64},{64,96},{96,128},{128,160},{160,192},{192,224},{224... | collective-permute-start | bytes 49160 | tf_op jit(solution)/shard_map/ppermute | solution.py:23
  122.5 7.1 %collective-permute-start.26 = (f32[2,8,1,128]{3,1,2,0:T(8,128)S(1)}, f32[2,8,1,128]{3,1,2,0:T(8,128)S(1)}, u32[]{:S(2)}, u32[]{:S(2)}) collective-permute-start(f32[2,8,1,128]{3,1,2,0:T(8,128)S(1)} %bitcast.635), channel_id=1, source_target_pairs={{0,1},{1,2},{2,3},{3,4},{4,5},{5,6},{6,7},{7,8},{8,9},{9,10},{10,1... | collective-permute-start | bytes 24584 | tf_op jit(solution)/shard_map/ppermute | solution.py:23
  130.6 19.2 %copy-start.4 = (f32[3,8,16,128]{3,2,1,0:T(8,128)}, f32[3,8,16,128]{3,2,1,0:T(8,128)S(1)}, u32[]{:S(2)}) copy-start(f32[3,8,16,128]{3,2,1,0:T(8,128)S(1)} %get-tuple-element.37) | copy-start | bytes 589828
  130.6 18.4 %copy-start.9 = (s32[256,2]{0,1:T(2,128)S(1)}, s32[256,2]{0,1:T(2,128)}, u32[]{:S(2)}) copy-start(s32[256,2]{0,1:T(2,128)} %param.23) | copy-start | bytes 6148
  130.6 19.2 %copy-start.6 = (f32[8,8,16,128]{3,2,1,0:T(8,128)S(1)}, f32[8,8,16,128]{3,2,1,0:T(8,128)}, u32[]{:S(2)}) copy-start(f32[8,8,16,128]{3,2,1,0:T(8,128)} %param.21) | copy-start | bytes 1572868
  130.7 6.9 %collective-permute-start.28 = (f32[2,8,1,128]{3,1,2,0:T(8,128)S(1)}, f32[2,8,1,128]{3,1,2,0:T(8,128)S(1)}, u32[]{:S(2)}, u32[]{:S(2)}) collective-permute-start(f32[2,8,1,128]{3,1,2,0:T(8,128)S(1)} %bitcast.628), channel_id=1, source_target_pairs={{1,0},{2,1},{3,2},{4,3},{5,4},{6,5},{7,6},{8,7},{9,8},{10,9},{11,1... | collective-permute-start | bytes 24584 | tf_op jit(solution)/shard_map/ppermute | solution.py:23
  132.2 5.3 %collective-permute-start.29 = (f32[2,1,16,128]{3,2,1,0:T(8,128)S(1)}, f32[2,1,16,128]{3,2,1,0:T(8,128)S(1)}, u32[]{:S(2)}, u32[]{:S(2)}) collective-permute-start(f32[2,1,16,128]{3,2,1,0:T(8,128)S(1)} %slice.1382), channel_id=1, source_target_pairs={{32,0},{64,32},{96,64},{128,96},{160,128},{192,160},{224,192},{256... | collective-permute-start | bytes 49160 | tf_op jit(solution)/shard_map/ppermute | solution.py:23
  137.9 88.7 %copy-start.2 = (f32[3,8,16,128]{3,2,1,0:T(8,128)}, f32[3,8,16,128]{3,2,1,0:T(8,128)S(1)}, u32[]{:S(2)}) copy-start(f32[3,8,16,128]{3,2,1,0:T(8,128)S(1)} %fusion.49) | copy-start | bytes 589828
  138.0 10.0 %collective-permute-start.31 = (f32[2,1,16,128]{3,2,1,0:T(8,128)S(1)}, f32[2,1,16,128]{3,2,1,0:T(8,128)S(1)}, u32[]{:S(2)}, u32[]{:S(2)}) collective-permute-start(f32[2,1,16,128]{3,2,1,0:T(8,128)S(1)} %slice.1395), channel_id=1, source_target_pairs={{0,32},{32,64},{64,96},{96,128},{128,160},{160,192},{192,224},{224... | collective-permute-start | bytes 49160 | tf_op jit(solution)/shard_map/ppermute | solution.py:23
  140.9 7.1 %collective-permute-start.30 = (f32[2,8,1,128]{3,1,2,0:T(8,128)S(1)}, f32[2,8,1,128]{3,1,2,0:T(8,128)S(1)}, u32[]{:S(2)}, u32[]{:S(2)}) collective-permute-start(f32[2,8,1,128]{3,1,2,0:T(8,128)S(1)} %bitcast.636), channel_id=1, source_target_pairs={{0,1},{1,2},{2,3},{3,4},{4,5},{5,6},{6,7},{7,8},{8,9},{9,10},{10,1... | collective-permute-start | bytes 24584 | tf_op jit(solution)/shard_map/ppermute | solution.py:23
  148.2 87.6 %copy-start.5 = (f32[3,8,16,128]{3,2,1,0:T(8,128)}, f32[3,8,16,128]{3,2,1,0:T(8,128)S(1)}, u32[]{:S(2)}) copy-start(f32[3,8,16,128]{3,2,1,0:T(8,128)S(1)} %fusion.51) | copy-start | bytes 589828
  148.2 0.7 copy-start.7
  243.2 31.1 %all-to-all-start = ((f32[32,1,512]{2,1,0:T(1,128)}), f32[32,1,512]{2,1,0:T(1,128)S(1)}, u32[]{:S(2)}, u32[]{:S(2)}) async-start(f32[32,1,512]{2,1,0:T(1,128)} %reshape.327), calls=%async_computation | async-start | bytes 131072 | tf_op jit(solution)/shard_map/all_to_all | solution.py:37
Sparse Core Ops, SparseCore 0:
  149.1 71.6 all-gather.2
where the time goes:
time: 285 us; the launch traced here: 284 us
  waiting for transfers between devices  117 us (41%)
  starting transfers between devices  110 us (39%)
  matrix products  18.8 us (7%)
  between operations  16.6 us (6%)
  local copies, waits for them, and re-layouts  11.8 us (4%)
  other arithmetic  10.3 us (4%)
    ppermute x32, starting transfers between devices, passed_along(): lax.ppermute(value, axis, [(source, source + steps) for source in range(i...  94.7 us
    all_gather x1, waiting for transfers between devices, picked(): lax.all_gather(shard, axis)  70.9 us
    ppermute x32, waiting for transfers between devices, passed_along(): lax.ppermute(value, axis, [(source, source + steps) for source in range(i...  30.4 us
    all_to_all x1, waiting for transfers between devices, summed_on_arrival(): lax.all_to_all(tiles, axis, split_axis=0, concat_axis=0, tiled=True)  15.3 us
    all_to_all x1, starting transfers between devices, summed_on_arrival(): lax.all_to_all(tiles, axis, split_axis=0, concat_axis=0, tiled=True)  14.9 us
  transfers between devices with their start and end apart: 34, of which 19 were waited for; matrix products, arithmetic and copies ran while one was open for 2% of the time, Pallas kernels for 0%

commit v1 on v0

v1 whole, which is shorter than its diff:
```python
import math

import jax
import jax.numpy as jnp
from jax import lax
from jax.experimental import pallas as pl
from jax.experimental.pallas import tpu as pltpu
from jax.sharding import PartitionSpec as P

STEPS = 8
HALO = 8
G = 64
FINE = 16

COURANT = 0.5
OMEGA_LO = 2.0 * math.pi / 24.0
OMEGA_HI = 2.0 * math.pi / 12.0
SPREAD = 0.7

VMEM = pl.BlockSpec(memory_space=pltpu.VMEM)
SMEM = pl.BlockSpec(memory_space=pltpu.SMEM)


def shifted(value, axis, steps):
    count = lax.axis_size(axis)
    first, last = (max(0, -steps), min(count, count - steps))
    return lax.ppermute(value, axis, [(source, source + steps) for source in range(first, last)])


def material_table(eps_inf, delta_eps, pole_freq, damping):
    half_damp = 0.5 * damping
    keep = (1.0 - half_damp) / (1.0 + half_damp)
    drive = pole_freq * pole_freq / COURANT / (1.0 + half_damp)
    return jnp.stack([keep, drive, delta_eps, COURANT / eps_inf])


def yee_kernel(
    where_ref, table_ref, own_ref, ylo_ref, yhi_ref, xlo_ref, xhi_ref, clo_ref, chi_ref,
    e_out, h_out, p_out, j_out, sample_out, state, coef,
):
    cells_x, cells_y, cells_z = own_ref.shape[1:]
    wide_x = cells_x + 2 * HALO
    wide_y = cells_y + 2 * HALO
    inner_x, inner_y = (HALO, HALO + cells_x), (HALO, HALO + cells_y)
    x_spans = ((0, HALO), inner_x, (inner_x[1], wide_x))
    y_spans = ((0, HALO), inner_y, (inner_y[1], wide_y))
    parts = (
        ((clo_ref, 0), (xlo_ref, None), (clo_ref, 1)),
        ((ylo_ref, None), (own_ref, None), (yhi_ref, None)),
        ((chi_ref, 0), (xhi_ref, None), (chi_ref, 1)),
    )
    levels = table_ref.shape[1]
    for i, (x0, x1) in enumerate(x_spans):
        for k, (y0, y1) in enumerate(y_spans):
            ref, lead = parts[i][k]
            part = ref if lead is None else ref.at[lead]
            inside = jnp.float32(1.0)
            if i != 1:
                inside = inside * where_ref[0, i // 2]
            if k != 1:
                inside = inside * where_ref[1, k // 2]

            def fill(x, carry, part=part, inside=inside, x0=x0, y0=y0, y1=y1):
                for comp in range(12):
                    state[comp, x0 + x, y0:y1, :] = part[comp, x]
                ids = part[12, x]
                values = [jnp.zeros_like(ids)] * 4
                for level in range(levels):
                    hit = ids == jnp.float32(level)
                    values = [jnp.where(hit, table_ref[c, level], v) for c, v in enumerate(values)]
                coef[0, x0 + x, y0:y1, :] = values[0]
                coef[1, x0 + x, y0:y1, :] = values[1]
                coef[2, x0 + x, y0:y1, :] = values[2]
                coef[3, x0 + x, y0:y1, :] = values[3] * inside
                coef[4, x0 + x, y0:y1, :] = jnp.full_like(ids, COURANT) * inside
                return carry

            lax.fori_loop(0, x1 - x0, fill, 0)

    lane = lax.broadcasted_iota(jnp.int32, (wide_y, cells_z), 1)
    not_last = lane < cells_z - 1
    not_first = lane > 0

    def z_next(v):
        return jnp.where(not_last, pltpu.roll(v, cells_z - 1, 1), 0.0)

    def z_prev(v):
        return jnp.where(not_first, pltpu.roll(v, 1, 1), 0.0)

    def y_next(v):
        return pltpu.roll(v, wide_y - 1, 0)

    def y_prev(v):
        return pltpu.roll(v, 1, 0)

    def magnetic(x):
        ex, ey, ez = (state[c, x] for c in range(3))
        ey_x, ez_x = (state[1, x + 1], state[2, x + 1])
        gain = coef[4, x]
        hx = state[3, x] - gain * ((y_next(ez) - ez) - (z_next(ey) - ey))
        hy = state[4, x] - gain * ((z_next(ex) - ex) - (ez_x - ez))
        hz = state[5, x] - gain * ((ey_x - ey) - (y_next(ex) - ex))
        state[3, x] = hx
        state[4, x] = hy
        state[5, x] = hz
        return hx, hy, hz

    def both(x, carry):
        hy_x, hz_x = (state[4, x - 1], state[5, x - 1])
        fields = [state[c, x] for c in range(3)]
        hx, hy, hz = magnetic(x)
        curl = (
            (hz - y_prev(hz)) - (hy - z_prev(hy)),
            (hx - z_prev(hx)) - (hz - hz_x),
            (hy - hy_x) - (hx - y_prev(hx)),
        )
        keep, drive, coupled, scale = (coef[c, x] for c in range(4))
        for c in range(3):
            polar = state[6 + c, x]
            rate = keep * state[9 + c, x] + drive * (coupled * fields[c] - polar)
            state[6 + c, x] = polar + COURANT * rate
            state[9 + c, x] = rate
            state[c, x] = fields[c] + scale * (curl[c] - rate)
        return carry

    plane = HALO + where_ref_row(where_ref)
    for step in range(STEPS):
        magnetic(step)
        lax.fori_loop(step + 1, wide_x - 1 - step, both, 0, unroll=2)
        for slot, comp in enumerate((1, 2, 4, 5)):
            sample_out[step, slot] = state[comp, plane, inner_y[0] : inner_y[1], :]
    for c in range(3):
        for base, out in ((0, e_out), (3, h_out), (6, p_out), (9, j_out)):
            out[c] = state[base + c, inner_x[0] : inner_x[1], inner_y[0] : inner_y[1], :]


def where_ref_row(where_ref):
    return where_ref[2, 0].astype(jnp.int32)


def yee_steps(where, table, own, ylo, yhi, xlo, xhi, clo, chi):
    cells = own.shape[1:]
    block = jax.ShapeDtypeStruct((3,) + cells, jnp.float32)
    wide = (cells[0] + 2 * HALO, cells[1] + 2 * HALO, cells[2])
    return pl.pallas_call(
        yee_kernel,
        out_shape=[block] * 4 + [jax.ShapeDtypeStruct((STEPS, 4) + cells[1:], jnp.float32)],
        in_specs=[SMEM, SMEM] + [VMEM] * 7,
        out_specs=[VMEM] * 5,
        scratch_shapes=[
            pltpu.VMEM((12,) + wide, jnp.float32),
            pltpu.VMEM((5,) + wide, jnp.float32),
        ],
        compiler_params=pltpu.CompilerParams(vmem_limit_bytes=40 * 1024 * 1024),
        name="yee_steps",
    )(where, table, own, ylo, yhi, xlo, xhi, clo, chi)


def halves(value):
    high = value.astype(jnp.bfloat16)
    return high, (value - high.astype(jnp.float32)).astype(jnp.bfloat16)


def phase_kernel(coarse_c, coarse_s, fine_c, fine_s, high_out, low_out):
    freqs, coarse, count = coarse_c.shape

    def one(f, carry):
        fc, fs = fine_c[f], fine_s[f]
        for a in range(coarse):
            cc, cs = coarse_c[f, a : a + 1], coarse_s[f, a : a + 1]
            rows = slice(a * FINE, (a + 1) * FINE)
            cos_high, cos_low = halves(cc * fc - cs * fs)
            sin_high, sin_low = halves(cs * fc + cc * fs)
            high_out[f, rows, :count] = cos_high
            high_out[f, rows, count:] = sin_high
            low_out[f, rows, :count] = cos_low
            low_out[f, rows, count:] = sin_low
        return carry

    lax.fori_loop(0, freqs, one, 0)


def z_phases(omegas, dir_z, cells_z):
    coarse = cells_z // FINE
    base = omegas[:, None, None] * (
        (FINE * jnp.arange(coarse)).astype(jnp.float32)[:, None] * dir_z[None, :]
    )
    fine = omegas[:, None, None] * (jnp.arange(FINE).astype(jnp.float32)[:, None] * dir_z[None, :])
    out = jax.ShapeDtypeStruct(
        (omegas.shape[0], cells_z, 2 * dir_z.shape[0]), jnp.bfloat16
    )
    return pl.pallas_call(
        phase_kernel,
        out_shape=[out, out],
        in_specs=[VMEM] * 4,
        out_specs=[VMEM] * 2,
        cost_estimate=pl.CostEstimate(flops=8000000, bytes_accessed=3000000, transcendentals=0),
        name="z_phases",
    )(jnp.cos(base), jnp.sin(base), jnp.cos(fine), jnp.sin(fine))


def radiation_kernel(
    cos_ref, sin_ref, sample_ref, acc_ref, high_ref, low_ref, cosy_ref, siny_ref,
    dft_out, part_out, rows_ref,
):
    freqs, cells_y, cells_z = acc_ref.shape[1:]
    steps = sample_ref.shape[0]
    count = cosy_ref.shape[2]
    half = 4 * cells_y

    def one(f, carry):
        reals, imags = [], []
        for c in range(4):
            real = acc_ref[c, f]
            imag = acc_ref[4 + c, f]
            for n in range(steps):
                sample = sample_ref[n, c]
                real = real + cos_ref[n, f] * sample
                imag = imag - sin_ref[n, f] * sample
            dft_out[c, f] = real
            dft_out[4 + c, f] = imag
            reals.append(real)
            imags.append(imag)
        left_high, left_low = halves(jnp.concatenate(reals + imags, axis=0))
        high, low = high_ref[f], low_ref[f]

        def mul(a, b):
            return jnp.dot(a, b, preferred_element_type=jnp.float32)

        table = mul(left_high, high) + (mul(left_high, low) + mul(left_low, high))
        part_real = table[:half, :count] - table[half:, count:]
        part_imag = table[:half, count:] + table[half:, :count]
        cos_y, sin_y = cosy_ref[f], siny_ref[f]
        for c, (source, sign) in enumerate(((3, -1.0), (2, 1.0), (1, 1.0), (0, -1.0))):
            pr = part_real[source * cells_y : (source + 1) * cells_y]
            pi = part_imag[source * cells_y : (source + 1) * cells_y]
            out_real = jnp.sum(pr * cos_y - pi * sin_y, axis=0, keepdims=True)
            out_imag = jnp.sum(pr * sin_y + pi * cos_y, axis=0, keepdims=True)
            rows_ref[c, pl.ds(f, 1), :] = sign * out_real
            rows_ref[4 + c, pl.ds(f, 1), :] = sign * out_imag
        return carry

    lax.fori_loop(0, freqs, one, 0)
    rows = jnp.concatenate([rows_ref[c] for c in range(8)] * 2, axis=0)
    part_out[...] = rows.T


def radiate(cos_a, sin_a, samples, acc, high, low, cos_y, sin_y):
    count = cos_y.shape[2]
    freqs = acc.shape[1]
    return pl.pallas_call(
        radiation_kernel,
        out_shape=[
            jax.ShapeDtypeStruct(acc.shape, jnp.float32),
            jax.ShapeDtypeStruct((count, 16 * freqs), jnp.float32),
        ],
        in_specs=[SMEM, SMEM] + [VMEM] * 6,
        out_specs=[VMEM] * 2,
        scratch_shapes=[pltpu.VMEM((8, freqs, count), jnp.float32)],
        compiler_params=pltpu.CompilerParams(vmem_limit_bytes=40 * 1024 * 1024),
        name="radiate",
    )(cos_a, sin_a, samples, acc, high, low, cos_y, sin_y)


def spread_rows(samples, root):
    count = lax.axis_size("rows")
    pieces = samples.reshape(count, -1, samples.shape[-1])
    arrived = lax.all_to_all(pieces, "rows", split_axis=0, concat_axis=0, tiled=True)
    mine = lax.dynamic_index_in_dim(arrived, root, 0, keepdims=True)
    copies = jnp.broadcast_to(mine, pieces.shape)
    gathered = lax.all_to_all(copies, "rows", split_axis=0, concat_axis=0, tiled=True)
    return gathered.reshape(samples.shape)


def local(
    e_field, h_field, polar, polar_rate, material_id, eps_inf, delta_eps, pole_freq, damping,
    dft_acc, plane_index, direction_ids,
):
    cells_x, cells_y, cells_z = e_field.shape[1:]
    freq_block = dft_acc.shape[1]
    row, col = lax.axis_index("rows"), lax.axis_index("cols")
    rows, cols = lax.axis_size("rows"), lax.axis_size("cols")

    mats = material_id.astype(jnp.float32)[None]
    fields = (e_field, h_field, polar, polar_rate, mats)
    own = jnp.concatenate(fields, 0)
    first = jnp.concatenate([v[:, :, :HALO] for v in fields], 0)
    final = jnp.concatenate([v[:, :, -HALO:] for v in fields], 0)
    yhi = shifted(first, "cols", -1)
    ylo = shifted(final, "cols", 1)
    xhi = shifted(own, "rows", -1)
    xlo = shifted(own, "rows", 1)
    sides = jnp.stack([ylo, yhi])
    chi = shifted(sides, "rows", -1)
    clo = shifted(sides, "rows", 1)

    plane_row = plane_index[0]
    root_row = plane_row // cells_x
    local_row = plane_row % cells_x
    table = material_table(eps_inf, delta_eps, pole_freq, damping)
    where = jnp.stack(
        [row > 0, row < rows - 1, col > 0, col < cols - 1, local_row, local_row]
    ).astype(jnp.float32).reshape(3, 2)
    e_out, h_out, p_out, j_out, samples = yee_steps(
        where, table, own, ylo, yhi, xlo, xhi, clo, chi
    )

    total_f = rows * freq_block
    freq_ids = row * freq_block + jnp.arange(freq_block, dtype=jnp.int32)
    omegas = OMEGA_LO + (OMEGA_HI - OMEGA_LO) * (freq_ids.astype(jnp.float32) / (total_f - 1))
    times = (jnp.arange(STEPS).astype(jnp.float32) + 1.0) * COURANT
    angles = times[:, None] * omegas[None, :]
    ids_float = direction_ids.astype(jnp.float32)
    dir_y = SPREAD * (2.0 * ids_float[:, 0] / (G - 1) - 1.0)
    dir_z = SPREAD * (2.0 * ids_float[:, 1] / (G - 1) - 1.0)
    dir_x = jnp.sqrt(1.0 - dir_y * dir_y - dir_z * dir_z)
    pos_y = (col * cells_y + jnp.arange(cells_y, dtype=jnp.int32)).astype(jnp.float32)
    plane_x = plane_row.astype(jnp.float32)
    phase_y = (
        omegas[:, None, None] * (pos_y[:, None] * dir_y[None, :] + plane_x * dir_x[None, :])[None]
    )
    high, low = z_phases(omegas, dir_z, cells_z)

    received = spread_rows(samples, root_row)
    dft_out, partial_sum = radiate(
        jnp.cos(angles), jnp.sin(angles), received, dft_acc, high, low,
        jnp.cos(phase_y), jnp.sin(phase_y),
    )
    pieces = partial_sum.reshape(cols, -1, partial_sum.shape[-1])
    arrived = lax.all_to_all(pieces, "cols", split_axis=0, concat_axis=0, tiled=True)
    scale = 1.0 / math.sqrt(cols * cells_y * cells_z)
    far = jnp.sum(arrived, axis=0) * scale
    far_field = far[:, : 8 * freq_block].T.reshape(8, freq_block, -1)
    return (e_out, h_out, p_out, j_out, dft_out, far_field)


def solution(mesh):
    grid = P(None, "rows", "cols", None)
    in_specs = (
        grid, grid, grid, grid, P("rows", "cols", None), P(), P(), P(), P(), grid, P(), P(),
    )
    out_specs = (grid, grid, grid, grid, grid, P(None, "rows", "cols"))
    return jax.shard_map(local, mesh=mesh, in_specs=in_specs, out_specs=out_specs, check_vma=False)
```

time: 285 us -> 132 us (0.46)
  waiting for transfers between devices: 117 us -> 23.8 us
  starting transfers between devices: 110 us -> 30.3 us
  blocking collectives: 0 us -> 36.8 us
  Pallas kernels: 0 us -> 21 us
  matrix products: 18.8 us -> 0 us
  between operations: 16.6 us -> 1.51 us
  other arithmetic: 10.3 us -> 3.18 us
    ppermute x32 -> x6, starting transfers between devices: 94.7 us -> 16.2 us  [shifted(): lax.ppermute(value, axis, [(source, source + steps) for source in range(f...]
    all_gather x1 -> x0, waiting for transfers between devices: 70.9 us -> none  [picked(): lax.all_gather(shard, axis)]
    all_to_all x0 -> x1, blocking collectives: none -> 36.8 us  [local(): lax.all_to_all(pieces, 'cols', split_axis=0, concat_axis=0, tiled=True)]
    pallas_call x0 -> x3, Pallas kernels: none -> 21 us  [the longest x1 14.5 us: yee_steps(): pl.pallas_call(yee_kernel, out_shape=[block] * 4 + [jax.ShapeDtypeStruct(...]
    dot_general x6 -> x0, matrix products: 18.8 us -> none  [the longest x1 4.91 us: radiation(): jnp.einsum('cfyz,fzd->cfyd', cur_imag, cos_z, precision=BEST_PRECISION)]
    ppermute x32 -> x6, waiting for transfers between devices: 30.4 us -> 18.8 us  [shifted(): lax.ppermute(value, axis, [(source, source + steps) for source in range(f...]
    all_to_all x1 -> x2, waiting for transfers between devices: 15.3 us -> 5.07 us  [the longest x1 3.56 us: spread_rows(): lax.all_to_all(pieces, 'rows', split_axis=0, concat_axis=0, tiled=True)]
    unnamed x23 -> x37, local copies, waits for them, and re-layouts: 3.37 us -> 12.9 us
  transfers between devices with their start and end apart: 34 -> 8, of which waited for: 19 -> 6; matrix products, arithmetic and copies ran while one was open for 2% -> 5% of each run, Pallas kernels for 0% -> 2%
where the time goes in v1:
time: 132 us; the launch traced here: 131 us
  blocking collectives  36.8 us (28%)
  starting transfers between devices  30.3 us (23%)
  waiting for transfers between devices  23.8 us (18%)
  Pallas kernels  21 us (16%)
  local copies, waits for them, and re-layouts  14.4 us (11%)
  other arithmetic  3.18 us (2%)
  between operations  1.51 us (1%)
    all_to_all x1, blocking collectives, local(): lax.all_to_all(pieces, 'cols', split_axis=0, concat_axis=0, tiled=True)  36.8 us
    ppermute x6, waiting for transfers between devices, shifted(): lax.ppermute(value, axis, [(source, source + steps) for source in range(f...  18.8 us
    ppermute x6, starting transfers between devices, shifted(): lax.ppermute(value, axis, [(source, source + steps) for source in range(f...  16.2 us
    pallas_call x1, Pallas kernels, yee_steps(): pl.pallas_call(yee_kernel, out_shape=[block] * 4 + [jax.ShapeDtypeStruct(...  14.5 us
    unnamed x37, local copies, waits for them, and re-layouts  12.9 us
    all_to_all x1, starting transfers between devices, spread_rows(): lax.all_to_all(pieces, 'rows', split_axis=0, concat_axis=0, tiled=True)  8.06 us
    all_to_all x1, starting transfers between devices, spread_rows(): lax.all_to_all(copies, 'rows', split_axis=0, concat_axis=0, tiled=True)  6.03 us
    pallas_call x1, Pallas kernels, radiate(): pl.pallas_call(radiation_kernel, out_shape=[jax.ShapeDtypeStruct(acc.shap...  3.64 us
  transfers between devices with their start and end apart: 8, of which 6 were waited for; matrix products, arithmetic and copies ran while one was open for 5% of the time, Pallas kernels for 2%

profile of v1, /device:TPU:2, one launch (start us, length us, event | category | flops | bytes accessed | tf_op | source)
XLA Modules:
  0.0 131.0 jit_solution(11937281855815258867)
XLA Ops:
  0.6 1.0 constant_dynamic-update-slice_fusion.4
  1.6 0.0 copy-done.5
  1.7 0.9 copy-done.6
  2.6 0.9 copy-done.7
  3.5 0.8 copy-done.8
  4.4 1.9 %collective-permute-start.2 = (f32[13,8,16,128]{3,2,1,0:T(8,128)S(1)}, f32[13,8,16,128]{3,2,1,0:T(8,128)S(1)}, u32[]{:S(2)}, u32[]{:S(2)}) collective-permute-start(f32[13,8,16,128]{3,2,1,0:T(8,128)S(1)} %constant_dynamic-update-slice_fusion.own_ref), channel_id=1, source_target_pairs={{0,32},{32,64},{64,96},{96,128},{128,160},{160,192},{192,224},{224... | collective-permute-start | bytes 2555912 | tf_op jit(solution)/shard_map/ppermute | solution.py:27
  6.3 3.6 %collective-permute-start.3 = (f32[13,8,16,128]{3,2,1,0:T(8,128)S(1)}, f32[13,8,16,128]{3,2,1,0:T(8,128)S(1)}, u32[]{:S(2)}, u32[]{:S(2)}) collective-permute-start(f32[13,8,16,128]{3,2,1,0:T(8,128)S(1)} %constant_dynamic-update-slice_fusion.own_ref), channel_id=1, source_target_pairs={{32,0},{64,32},{96,64},{128,96},{160,128},{192,160},{224,192},{256... | collective-permute-start | bytes 2555912 | tf_op jit(solution)/shard_map/ppermute | solution.py:27
  9.9 0.7 slice_dynamic-update-slice_fusion.3
  10.6 0.7 slice_dynamic-update-slice_fusion.2
  11.3 0.7 slice_dynamic-update-slice_fusion.1
  12.0 0.7 slice_dynamic-update-slice_fusion
  12.7 0.6 slice_dynamic-update-slice_fusion.8
  13.3 3.8 %collective-permute-start = (f32[13,8,8,128]{3,2,1,0:T(8,128)}, f32[13,8,8,128]{3,2,1,0:T(8,128)S(1)}, u32[]{:S(2)}, u32[]{:S(2)}) collective-permute-start(f32[13,8,8,128]{3,2,1,0:T(8,128)} %get-tuple-element.39), channel_id=1, source_target_pairs={{0,1},{1,2},{2,3},{3,4},{4,5},{5,6},{6,7},{7,8},{8,9},{9,10},{10,1... | collective-permute-start | bytes 1277960 | tf_op jit(solution)/shard_map/ppermute | solution.py:27
  17.1 1.3 collective-permute-start.1
  19.2 0.1 stack.64
  19.3 0.1 convert_element_type.60.where_ref
  19.3 0.6 copy-done.13
  19.9 0.7 copy-done.9
  20.6 0.6 copy-done.10
  21.3 0.0 copy-done.11
  21.3 0.7 copy-done.12
  22.0 4.6 %collective-permute-done.ylo_ref = f32[13,8,8,128]{3,2,1,0:T(8,128)S(1)} collective-permute-done((f32[13,8,8,128]{3,2,1,0:T(8,128)}, f32[13,8,8,128]{3,2,1,0:T(8,128)S(1)}, u32[]{:S(2)}, u32[]{:S(2)}) %collective-permute-start) | collective-permute-done | bytes 426016 | tf_op jit(solution)/shard_map/ppermute | solution.py:27
  26.5 4.2 %collective-permute-done.1.yhi_ref = f32[13,8,8,128]{3,2,1,0:T(8,128)S(1)} collective-permute-done((f32[13,8,8,128]{3,2,1,0:T(8,128)}, f32[13,8,8,128]{3,2,1,0:T(8,128)S(1)}, u32[]{:S(2)}, u32[]{:S(2)}) %collective-permute-start.1) | collective-permute-done | bytes 426016 | tf_op jit(solution)/shard_map/ppermute | solution.py:27
  30.7 0.1 pad_maximum_fusion
  30.8 1.9 %collective-permute-start.4 = (f32[2,13,8,8,128]{4,3,2,1,0:T(8,128)S(1)}, f32[2,13,8,8,128]{4,3,2,1,0:T(8,128)S(1)}, u32[]{:S(2)}, u32[]{:S(2)}) collective-permute-start(f32[2,13,8,8,128]{4,3,2,1,0:T(8,128)S(1)} %pad_maximum_fusion), channel_id=1, source_target_pairs={{0,32},{32,64},{64,96},{96,128},{128,160},{160,192},{192,224},{224... | collective-permute-start | bytes 2555912 | tf_op jit(solution)/shard_map/ppermute | solution.py:27
  32.7 3.6 %collective-permute-start.5 = (f32[2,13,8,8,128]{4,3,2,1,0:T(8,128)S(1)}, f32[2,13,8,8,128]{4,3,2,1,0:T(8,128)S(1)}, u32[]{:S(2)}, u32[]{:S(2)}) collective-permute-start(f32[2,13,8,8,128]{4,3,2,1,0:T(8,128)S(1)} %pad_maximum_fusion), channel_id=1, source_target_pairs={{32,0},{64,32},{96,64},{128,96},{160,128},{192,160},{224,192},{256... | collective-permute-start | bytes 2555912 | tf_op jit(solution)/shard_map/ppermute | solution.py:27
  36.4 0.1 broadcast_multiply_fusion.1
  36.5 0.1 multiply_add_fusion
  36.5 0.0 collective-permute-done.2.xlo_ref
  36.5 0.0 collective-permute-done.3.xhi_ref
  36.6 8.2 %collective-permute-done.4.clo_ref = f32[2,13,8,8,128]{4,3,2,1,0:T(8,128)S(1)} collective-permute-done((f32[2,13,8,8,128]{4,3,2,1,0:T(8,128)S(1)}, f32[2,13,8,8,128]{4,3,2,1,0:T(8,128)S(1)}, u32[]{:S(2)}, u32[]{:S(2)}) %collective-permute-start.4) | collective-permute-done | bytes 852000 | tf_op jit(solution)/shard_map/ppermute | solution.py:27
  44.8 1.8 %collective-permute-done.5.chi_ref = f32[2,13,8,8,128]{4,3,2,1,0:T(8,128)S(1)} collective-permute-done((f32[2,13,8,8,128]{4,3,2,1,0:T(8,128)S(1)}, f32[2,13,8,8,128]{4,3,2,1,0:T(8,128)S(1)}, u32[]{:S(2)}, u32[]{:S(2)}) %collective-permute-start.5) | collective-permute-done | bytes 852000 | tf_op jit(solution)/shard_map/ppermute | solution.py:27
  46.6 14.5 %yee_steps.1 = (f32[3,8,16,128]{3,2,1,0:T(8,128)}, f32[3,8,16,128]{3,2,1,0:T(8,128)}, f32[3,8,16,128]{3,2,1,0:T(8,128)}, f32[3,8,16,128]{3,2,1,0:T(8,128)}, f32[8,4,16,128]{3,2,1,0:T(8,128)S(1)}) custom-call(f32[3,2]{1,0:T(4,128)S(1)} %convert_element_type.60.where_ref, f32[4,8]{1,0:T(4,128)S(1)} %pad_maximum_fusion.1.table_ref, ...), custom_call_target="tpu_custom_call" | custom-call | tf_op jit(solution)/shard_map/yee_steps/pallas_call | solution.py:145
  61.0 0.7 copy-done.3
  61.7 8.1 %all-to-all-start = ((f32[16,32,128]{2,1,0:T(8,128)}), f32[16,32,128]{2,1,0:T(8,128)S(1)}, u32[]{:S(2)}, u32[]{:S(2)}) async-start(f32[16,32,128]{2,1,0:T(8,128)} %bitcast.37), calls=%async_computation | async-start | bytes 524288 | tf_op jit(solution)/shard_map/all_to_all | solution.py:268
  69.8 1.8 %multiply_sine_fusion = (f32[8,16,256]{2,1,0:T(8,128)S(1)}, f32[8,16,256]{2,1,0:T(8,128)S(1)}, f32[8,16,256]{2,1,0:T(8,128)}, f32[8,16,256]{2,1,0:T(8,128)}) fusion(f32[16,256]{1,0:T(8,128)S(1)} %get-tuple-element.56, f32[8]{0:T(128)S(1)} %get-tuple-element.54, f32[16,256]{1,0:T(8,128)S(1)} %get-tuple-element.57), kind=kLoop, calls=%fused_computation.1 | loop fusion | flops 65536 | bytes 557088 | tf_op jit(solution)/shard_map/sin | solution.py:327
  71.6 3.6 %all-to-all-done = f32[16,32,128]{2,1,0:T(8,128)S(1)} async-done(((f32[16,32,128]{2,1,0:T(8,128)}), f32[16,32,128]{2,1,0:T(8,128)S(1)}, u32[]{:S(2)}, u32[]{:S(2)}) %all-to-all-start) | async-done | bytes 262176 | tf_op jit(solution)/shard_map/all_to_all | solution.py:268
  75.2 0.7 broadcast_in_dim.8
  75.9 6.0 %all-to-all-start.1 = ((f32[16,32,128]{2,1,0:T(8,128)}), f32[16,32,128]{2,1,0:T(8,128)S(1)}, u32[]{:S(2)}, u32[]{:S(2)}) async-start(f32[16,32,128]{2,1,0:T(8,128)} %broadcast_in_dim.8), calls=%async_computation.1 | async-start | bytes 524288 | tf_op jit(solution)/shard_map/all_to_all | solution.py:271
  81.9 1.0 multiply_sine_fusion.2
  82.9 2.9 %z_phases.1 = (bf16[8,128,512]{2,1,0:T(8,128)(2,1)}, bf16[8,128,512]{2,1,0:T(8,128)(2,1)}) custom-call(f32[8,8,256]{2,1,0:T(8,128)} %get-tuple-element.45.coarse_c, f32[8,8,256]{2,1,0:T(8,128)} %get-tuple-element.44.coarse_s, f32[8,16,256]{2,1,0:T(8,128)} %get-tuple-element.50.fine_c, f32[8,16,256]{2,1,0:T(8,128)} %get-tuple-element.51.fine_s), custom_call_target="tpu_custom_call" | custom-call | flops 8000000 | bytes 3000000 | tf_op jit(solution)/shard_map/z_phases/pallas_call | solution.py:192
  85.8 0.1 multiply_sine_fusion.3
  85.9 1.5 %all-to-all-done.1 = f32[16,32,128]{2,1,0:T(8,128)S(1)} async-done(((f32[16,32,128]{2,1,0:T(8,128)}), f32[16,32,128]{2,1,0:T(8,128)S(1)}, u32[]{:S(2)}, u32[]{:S(2)}) %all-to-all-start.1) | async-done | bytes 262176 | tf_op jit(solution)/shard_map/all_to_all | solution.py:271
  87.4 1.2 copy-done
  88.6 1.2 copy-done.1
  89.8 3.6 %radiate.1 = (f32[8,8,16,128]{3,2,1,0:T(8,128)}, f32[256,128]{1,0:T(8,128)S(1)}) custom-call(f32[8,8]{1,0:T(8,128)S(1)} %get-tuple-element.49.cos_ref, f32[8,8]{1,0:T(8,128)S(1)} %get-tuple-element.48.sin_ref, f32[8,4,16,128]{3,2,1,0:T(8,128)S(1)} %bitcast.36, f32[8,8,16,128]{3,2,1,0:T(8,128)S(1)} %copy-done.2, bf16[8,128,512]{2,1,0:T(8,128)(2,1)S(1)} %copy-done, ...), custom_call_target="tpu_custom_call" | custom-call | tf_op jit(solution)/shard_map/radiate/pallas_call | solution.py:251
  93.5 36.8 %all_to_all.15 = f32[32,8,128]{2,1,0:T(8,128)S(1)} all-to-all(f32[32,8,128]{2,1,0:T(8,128)S(1)} %bitcast.38), channel_id=1, replica_groups=mesh['rows'=16,'cols'=32] {'cols'}, dimensions={0} | all-to-all | bytes 262144 | tf_op jit(solution)/shard_map/all_to_all | solution.py:330
  130.3 0.7 copy.19
  (36 shorter events, 0.2 us)
Async XLA Ops:
  0.6 1.0 copy-start.5
  1.7 0.9 copy-start.6
  2.6 0.9 copy-start.7
  3.5 0.8 copy-start.8
  3.5 6.4 %copy-start.4 = (f32[3,8,16,128]{3,2,1,0:T(8,128)S(1)}, f32[3,8,16,128]{3,2,1,0:T(8,128)}, u32[]{:S(2)}) copy-start(f32[3,8,16,128]{3,2,1,0:T(8,128)} %param.12) | copy-start | bytes 589828
  4.4 32.2 %collective-permute-start.2 = (f32[13,8,16,128]{3,2,1,0:T(8,128)S(1)}, f32[13,8,16,128]{3,2,1,0:T(8,128)S(1)}, u32[]{:S(2)}, u32[]{:S(2)}) collective-permute-start(f32[13,8,16,128]{3,2,1,0:T(8,128)S(1)} %constant_dynamic-update-slice_fusion.own_ref), channel_id=1, source_target_pairs={{0,32},{32,64},{64,96},{96,128},{128,160},{160,192},{192,224},{224... | collective-permute-start | bytes 2555912 | tf_op jit(solution)/shard_map/ppermute | solution.py:27
  6.3 30.3 %collective-permute-start.3 = (f32[13,8,16,128]{3,2,1,0:T(8,128)S(1)}, f32[13,8,16,128]{3,2,1,0:T(8,128)S(1)}, u32[]{:S(2)}, u32[]{:S(2)}) collective-permute-start(f32[13,8,16,128]{3,2,1,0:T(8,128)S(1)} %constant_dynamic-update-slice_fusion.own_ref), channel_id=1, source_target_pairs={{32,0},{64,32},{96,64},{128,96},{160,128},{192,160},{224,192},{256... | collective-permute-start | bytes 2555912 | tf_op jit(solution)/shard_map/ppermute | solution.py:27
  13.3 13.2 %collective-permute-start = (f32[13,8,8,128]{3,2,1,0:T(8,128)}, f32[13,8,8,128]{3,2,1,0:T(8,128)S(1)}, u32[]{:S(2)}, u32[]{:S(2)}) collective-permute-start(f32[13,8,8,128]{3,2,1,0:T(8,128)} %get-tuple-element.39), channel_id=1, source_target_pairs={{0,1},{1,2},{2,3},{3,4},{4,5},{5,6},{6,7},{7,8},{8,9},{9,10},{10,1... | collective-permute-start | bytes 1277960 | tf_op jit(solution)/shard_map/ppermute | solution.py:27
  17.1 13.6 %collective-permute-start.1 = (f32[13,8,8,128]{3,2,1,0:T(8,128)}, f32[13,8,8,128]{3,2,1,0:T(8,128)S(1)}, u32[]{:S(2)}, u32[]{:S(2)}) collective-permute-start(f32[13,8,8,128]{3,2,1,0:T(8,128)} %get-tuple-element.38), channel_id=1, source_target_pairs={{1,0},{2,1},{3,2},{4,3},{5,4},{6,5},{7,6},{8,7},{9,8},{10,9},{11,1... | collective-permute-start | bytes 1277960 | tf_op jit(solution)/shard_map/ppermute | solution.py:27
  19.3 0.7 copy-start.13
  19.9 0.7 copy-start.9
  20.6 0.7 copy-start.10
  20.6 0.7 copy-start.11
  21.3 0.7 copy-start.12
  30.8 14.0 %collective-permute-start.4 = (f32[2,13,8,8,128]{4,3,2,1,0:T(8,128)S(1)}, f32[2,13,8,8,128]{4,3,2,1,0:T(8,128)S(1)}, u32[]{:S(2)}, u32[]{:S(2)}) collective-permute-start(f32[2,13,8,8,128]{4,3,2,1,0:T(8,128)S(1)} %pad_maximum_fusion), channel_id=1, source_target_pairs={{0,32},{32,64},{64,96},{96,128},{128,160},{160,192},{192,224},{224... | collective-permute-start | bytes 2555912 | tf_op jit(solution)/shard_map/ppermute | solution.py:27
  32.7 13.8 %collective-permute-start.5 = (f32[2,13,8,8,128]{4,3,2,1,0:T(8,128)S(1)}, f32[2,13,8,8,128]{4,3,2,1,0:T(8,128)S(1)}, u32[]{:S(2)}, u32[]{:S(2)}) collective-permute-start(f32[2,13,8,8,128]{4,3,2,1,0:T(8,128)S(1)} %pad_maximum_fusion), channel_id=1, source_target_pairs={{32,0},{64,32},{96,64},{128,96},{160,128},{192,160},{224,192},{256... | collective-permute-start | bytes 2555912 | tf_op jit(solution)/shard_map/ppermute | solution.py:27
  61.0 0.7 copy-start.3
  61.7 13.4 %all-to-all-start = ((f32[16,32,128]{2,1,0:T(8,128)}), f32[16,32,128]{2,1,0:T(8,128)S(1)}, u32[]{:S(2)}, u32[]{:S(2)}) async-start(f32[16,32,128]{2,1,0:T(8,128)} %bitcast.37), calls=%async_computation | async-start | bytes 524288 | tf_op jit(solution)/shard_map/all_to_all | solution.py:268
  75.9 11.5 %copy-start.2 = (f32[8,8,16,128]{3,2,1,0:T(8,128)S(1)}, f32[8,8,16,128]{3,2,1,0:T(8,128)}, u32[]{:S(2)}) copy-start(f32[8,8,16,128]{3,2,1,0:T(8,128)} %acc_ref.1) | copy-start | bytes 1572868
  75.9 11.5 %all-to-all-start.1 = ((f32[16,32,128]{2,1,0:T(8,128)}), f32[16,32,128]{2,1,0:T(8,128)S(1)}, u32[]{:S(2)}, u32[]{:S(2)}) async-start(f32[16,32,128]{2,1,0:T(8,128)} %broadcast_in_dim.8), calls=%async_computation.1 | async-start | bytes 524288 | tf_op jit(solution)/shard_map/all_to_all | solution.py:271
  87.4 1.2 copy-start
  88.6 1.2 copy-start.1

commit v2 on v1

--- a/solution.py
+++ b/solution.py
@@ -7,6 +7,7 @@
 from jax.experimental.pallas import tpu as pltpu
 from jax.sharding import PartitionSpec as P
 
+
 STEPS = 8
 HALO = 8
 G = 64
@@ -31,12 +32,63 @@
     half_damp = 0.5 * damping
     keep = (1.0 - half_damp) / (1.0 + half_damp)
     drive = pole_freq * pole_freq / COURANT / (1.0 + half_damp)
-    return jnp.stack([keep, drive, delta_eps, COURANT / eps_inf])
+    table = jnp.stack([keep, 0.5 * drive, 4.0 * delta_eps, 0.5 * (COURANT / eps_inf)])
+    return jnp.broadcast_to(
+        jnp.pad(table, ((0, 0), (0, 128 - table.shape[1])))[:, None, :], (4, 8, 128)
+    )
+
+
+def pack_kernel(e_ref, h_ref, p_ref, j_ref, m_ref, own, first, final, mats, sems):
+    cells_y = e_ref.shape[2]
+    spans = ((own, 0, cells_y), (first, 0, HALO), (final, cells_y - HALO, HALO))
+    copies = [pltpu.make_async_copy(m_ref, mats, sems.at[0])]
+    for i, ref in enumerate((e_ref, h_ref, p_ref, j_ref)):
+        for k, (out, start, size) in enumerate(spans):
+            copies.append(
+                pltpu.make_async_copy(
+                    ref.at[:, :, pl.ds(start, size), :],
+                    out.at[pl.ds(3 * i, 3)],
+                    sems.at[1 + 3 * i + k],
+                )
+            )
+    for copy in copies:
+        copy.start()
+    copies[0].wait()
+    ids = mats[...].astype(jnp.float32)
+    own[12] = ids
+    first[12] = ids[:, :HALO]
+    final[12] = ids[:, cells_y - HALO :]
+    for copy in copies[1:]:
+        copy.wait()
+
+
+def pack(e_field, h_field, polar, polar_rate, material_id):
+    cells_x, cells_y, cells_z = material_id.shape
+    strip = jax.ShapeDtypeStruct((13, cells_x, HALO, cells_z), jnp.float32)
+    return pl.pallas_call(
+        pack_kernel,
+        out_shape=[
+            jax.ShapeDtypeStruct((13, cells_x, cells_y, cells_z), jnp.float32), strip, strip,
+        ],
+        in_specs=[pl.BlockSpec(memory_space=pltpu.HBM)] * 5,
+        out_specs=[VMEM] * 3,
+        scratch_shapes=[
+            pltpu.VMEM(material_id.shape, jnp.int32),
+            pltpu.SemaphoreType.DMA((13,)),
+        ],
+        compiler_params=pltpu.CompilerParams(vmem_limit_bytes=8 * 1024 * 1024),
+        name="pack",
+    )(
+        *(
+            pltpu.with_memory_space_constraint(v, pltpu.HBM)
+            for v in (e_field, h_field, polar, polar_rate, material_id)
+        )
+    )
 
 
 def yee_kernel(
     where_ref, table_ref, own_ref, ylo_ref, yhi_ref, xlo_ref, xhi_ref, clo_ref, chi_ref,
-    e_out, h_out, p_out, j_out, sample_out, state, coef,
+    e_out, h_out, p_out, j_out, sample_out, even, odd, coef,
 ):
     cells_x, cells_y, cells_z = own_ref.shape[1:]
     wide_x = cells_x + 2 * HALO
@@ -49,37 +101,42 @@
         ((ylo_ref, None), (own_ref, None), (yhi_ref, None)),
         ((chi_ref, 0), (xhi_ref, None), (chi_ref, 1)),
     )
-    levels = table_ref.shape[1]
+    gains = (1.0, 2.0, 4.0, 2.0)
+    whole = slice(0, wide_y)
+    zeros = jnp.zeros((HALO, cells_z), jnp.float32)
+    tables = [table_ref[c] for c in range(4)]
     for i, (x0, x1) in enumerate(x_spans):
         for k, (y0, y1) in enumerate(y_spans):
             ref, lead = parts[i][k]
             part = ref if lead is None else ref.at[lead]
             inside = jnp.float32(1.0)
             if i != 1:
-                inside = inside * where_ref[0, i // 2]
+                inside = inside * where_ref[0, i // 2].astype(jnp.float32)
             if k != 1:
-                inside = inside * where_ref[1, k // 2]
+                inside = inside * where_ref[1, k // 2].astype(jnp.float32)
 
             def fill(x, carry, part=part, inside=inside, x0=x0, y0=y0, y1=y1):
                 for comp in range(12):
-                    state[comp, x0 + x, y0:y1, :] = part[comp, x]
-                ids = part[12, x]
-                values = [jnp.zeros_like(ids)] * 4
-                for level in range(levels):
-                    hit = ids == jnp.float32(level)
-                    values = [jnp.where(hit, table_ref[c, level], v) for c, v in enumerate(values)]
-                coef[0, x0 + x, y0:y1, :] = values[0]
-                coef[1, x0 + x, y0:y1, :] = values[1]
-                coef[2, x0 + x, y0:y1, :] = values[2]
-                coef[3, x0 + x, y0:y1, :] = values[3] * inside
-                coef[4, x0 + x, y0:y1, :] = jnp.full_like(ids, COURANT) * inside
+                    even[comp, x0 + x, y0:y1, :] = part[comp, x] * gains[comp // 3]
+                for y in range(y0, y1, 8):
+                    ids = part[12, x, y - y0 : y - y0 + 8, :].astype(jnp.int32)
+                    for c in range(4):
+                        value = jnp.take_along_axis(tables[c], ids, axis=1)
+                        coef[c, x0 + x, y : y + 8, :] = value * inside if c == 3 else value
                 return carry
 
-            lax.fori_loop(0, x1 - x0, fill, 0)
+            lax.fori_loop(0, x1 - x0, fill, 0, unroll=2)
+    for buffer in (even, odd):
+        for comp in (0, 2):
+            for x in range(wide_x):
+                buffer[comp, x, wide_y:, :] = zeros
 
     lane = lax.broadcasted_iota(jnp.int32, (wide_y, cells_z), 1)
     not_last = lane < cells_z - 1
     not_first = lane > 0
+    x_edge = where_ref[0, 0].astype(jnp.float32)
+    y_edge = where_ref[1, 0].astype(jnp.float32)
+    plane = HALO + where_ref[2, 0]
 
     def z_next(v):
         return jnp.where(not_last, pltpu.roll(v, cells_z - 1, 1), 0.0)
@@ -87,71 +144,79 @@
     def z_prev(v):
         return jnp.where(not_first, pltpu.roll(v, 1, 1), 0.0)
 
-    def y_next(v):
-        return pltpu.roll(v, wide_y - 1, 0)
-
     def y_prev(v):
-        return pltpu.roll(v, 1, 0)
-
-    def magnetic(x):
-        ex, ey, ez = (state[c, x] for c in range(3))
-        ey_x, ez_x = (state[1, x + 1], state[2, x + 1])
-        gain = coef[4, x]
-        hx = state[3, x] - gain * ((y_next(ez) - ez) - (z_next(ey) - ey))
-        hy = state[4, x] - gain * ((z_next(ex) - ex) - (ez_x - ez))
-        hz = state[5, x] - gain * ((ey_x - ey) - (y_next(ex) - ex))
-        state[3, x] = hx
-        state[4, x] = hy
-        state[5, x] = hz
-        return hx, hy, hz
-
-    def both(x, carry):
-        hy_x, hz_x = (state[4, x - 1], state[5, x - 1])
-        fields = [state[c, x] for c in range(3)]
-        hx, hy, hz = magnetic(x)
-        curl = (
-            (hz - y_prev(hz)) - (hy - z_prev(hy)),
-            (hx - z_prev(hx)) - (hz - hz_x),
-            (hy - hy_x) - (hx - y_prev(hx)),
-        )
-        keep, drive, coupled, scale = (coef[c, x] for c in range(4))
+        return pltpu.roll(jnp.concatenate([v[:HALO] * y_edge, v[HALO:]], axis=0), 1, 0)
+
+    for step in range(STEPS):
+        old, new = (even, odd) if step % 2 == 0 else (odd, even)
+
+        def magnetic(x, old=old):
+            ex, ey, ez = (old[c, x, whole] for c in range(3))
+            ey_x, ez_x = (old[1, x + 1, whole], old[2, x + 1, whole])
+            ex_y, ez_y = (old[0, x, 1 : wide_y + 1], old[2, x, 1 : wide_y + 1])
+            hx = old[3, x, whole] - ((ez_y - ez) - (z_next(ey) - ey))
+            hy = old[4, x, whole] - ((z_next(ex) - ex) - (ez_x - ez))
+            hz = old[5, x, whole] - ((ey_x - ey) - (ex_y - ex))
+            return hx, hy, hz
+
+        def electric(x, old=old, new=new):
+            edge = jnp.where(x == HALO, x_edge, 1.0)
+            hx, hy, hz = (new[3 + c, x, whole] for c in range(3))
+            hy_x, hz_x = (new[c, x - 1, whole] * edge for c in (4, 5))
+            curl = (
+                (hz - y_prev(hz)) - (hy - z_prev(hy)),
+                (hx - z_prev(hx)) - (hz - hz_x),
+                (hy - hy_x) - (hx - y_prev(hx)),
+            )
+            keep, drive, coupled, scale = (coef[c, x] for c in range(4))
+            for c in range(3):
+                polar = old[6 + c, x, whole]
+                field = old[c, x, whole]
+                rate = keep * old[9 + c, x, whole] + drive * (coupled * field - polar)
+                new[6 + c, x, whole] = polar + rate
+                new[9 + c, x, whole] = rate
+                new[c, x, whole] = field + scale * (curl[c] - rate)
+
+        def put(x, values, new=new):
+            for c in range(3):
+                new[3 + c, x, whole] = values[c]
+
+        def both(x, carry, magnetic=magnetic, electric=electric, put=put):
+            after = magnetic(x + 1)
+            electric(x)
+            put(x + 1, after)
+            return carry
+
+        put(step, magnetic(step))
+        put(step + 1, magnetic(step + 1))
+        lax.fori_loop(step + 1, wide_x - 2 - step, both, 0)
+        electric(wide_x - 2 - step)
+        for slot, (comp, gain) in enumerate(((1, 1.0), (2, 1.0), (4, 0.5), (5, 0.5))):
+            sample_out[step, slot] = new[comp, plane, inner_y[0] : inner_y[1], :] * gain
+
+    final = even if STEPS % 2 == 0 else odd
+
+    def emit(x, carry):
         for c in range(3):
-            polar = state[6 + c, x]
-            rate = keep * state[9 + c, x] + drive * (coupled * fields[c] - polar)
-            state[6 + c, x] = polar + COURANT * rate
-            state[9 + c, x] = rate
-            state[c, x] = fields[c] + scale * (curl[c] - rate)
+            for base, out, gain in ((0, e_out, 1.0), (3, h_out, 0.5), (6, p_out, 0.25), (9, j_out, 0.5)):
+                out[c, x] = final[base + c, HALO + x, inner_y[0] : inner_y[1], :] * gain
         return carry
 
-    plane = HALO + where_ref_row(where_ref)
-    for step in range(STEPS):
-        magnetic(step)
-        lax.fori_loop(step + 1, wide_x - 1 - step, both, 0, unroll=2)
-        for slot, comp in enumerate((1, 2, 4, 5)):
-            sample_out[step, slot] = state[comp, plane, inner_y[0] : inner_y[1], :]
-    for c in range(3):
-        for base, out in ((0, e_out), (3, h_out), (6, p_out), (9, j_out)):
-            out[c] = state[base + c, inner_x[0] : inner_x[1], inner_y[0] : inner_y[1], :]
-
-
-def where_ref_row(where_ref):
-    return where_ref[2, 0].astype(jnp.int32)
+    lax.fori_loop(0, cells_x, emit, 0, unroll=2)
 
 
 def yee_steps(where, table, own, ylo, yhi, xlo, xhi, clo, chi):
     cells = own.shape[1:]
     block = jax.ShapeDtypeStruct((3,) + cells, jnp.float32)
     wide = (cells[0] + 2 * HALO, cells[1] + 2 * HALO, cells[2])
+    state = pltpu.VMEM((12, wide[0], wide[1] + 8, wide[2]), jnp.float32)
     return pl.pallas_call(
         yee_kernel,
         out_shape=[block] * 4 + [jax.ShapeDtypeStruct((STEPS, 4) + cells[1:], jnp.float32)],
-        in_specs=[SMEM, SMEM] + [VMEM] * 7,
+        in_specs=[SMEM, VMEM] + [VMEM] * 7,
         out_specs=[VMEM] * 5,
-        scratch_shapes=[
-            pltpu.VMEM((12,) + wide, jnp.float32),
-            pltpu.VMEM((5,) + wide, jnp.float32),
-        ],
-        compiler_params=pltpu.CompilerParams(vmem_limit_bytes=40 * 1024 * 1024),
+        scratch_shapes=[state, state, pltpu.VMEM((4,) + wide, jnp.float32)],
+        compiler_params=pltpu.CompilerParams(vmem_limit_bytes=20 * 1024 * 1024),
         name="yee_steps",
     )(where, table, own, ylo, yhi, xlo, xhi, clo, chi)
 
@@ -194,6 +259,7 @@
         out_shape=[out, out],
         in_specs=[VMEM] * 4,
         out_specs=[VMEM] * 2,
+        compiler_params=pltpu.CompilerParams(vmem_limit_bytes=8 * 1024 * 1024),
         cost_estimate=pl.CostEstimate(flops=8000000, bytes_accessed=3000000, transcendentals=0),
         name="z_phases",
     )(jnp.cos(base), jnp.sin(base), jnp.cos(fine), jnp.sin(fine))
@@ -203,7 +269,7 @@
     cos_ref, sin_ref, sample_ref, acc_ref, high_ref, low_ref, cosy_ref, siny_ref,
     dft_out, part_out, rows_ref,
 ):
-    freqs, cells_y, cells_z = acc_ref.shape[1:]
+    freqs, cells_y, _ = acc_ref.shape[1:]
     steps = sample_ref.shape[0]
     count = cosy_ref.shape[2]
     half = 4 * cells_y
@@ -241,7 +307,11 @@
         return carry
 
     lax.fori_loop(0, freqs, one, 0)
-    rows = jnp.concatenate([rows_ref[c] for c in range(8)] * 2, axis=0)
+    half_count = count // 2
+    rows = jnp.concatenate(
+        [rows_ref[c, :, k * half_count : (k + 1) * half_count] for k in range(2) for c in range(8)],
+        axis=0,
+    )
     part_out[...] = rows.T
 
 
@@ -252,14 +322,33 @@
         radiation_kernel,
         out_shape=[
             jax.ShapeDtypeStruct(acc.shape, jnp.float32),
-            jax.ShapeDtypeStruct((count, 16 * freqs), jnp.float32),
+            jax.ShapeDtypeStruct((count // 2, 16 * freqs), jnp.float32),
         ],
         in_specs=[SMEM, SMEM] + [VMEM] * 6,
         out_specs=[VMEM] * 2,
         scratch_shapes=[pltpu.VMEM((8, freqs, count), jnp.float32)],
-        compiler_params=pltpu.CompilerParams(vmem_limit_bytes=40 * 1024 * 1024),
+        compiler_params=pltpu.CompilerParams(vmem_limit_bytes=16 * 1024 * 1024),
         name="radiate",
     )(cos_a, sin_a, samples, acc, high, low, cos_y, sin_y)
+
+
+def finish(arrived, scale, freqs):
+    share = 2 * arrived.shape[1]
+
+    def finish_kernel(in_ref, out_ref):
+        total = jnp.sum(in_ref[...], axis=0) * scale
+        half = total.shape[1] // 2
+        both = jnp.concatenate([total, pltpu.roll(total, half, 1)], axis=0)
+        out_ref[...] = both.T[:half].reshape(out_ref.shape)
+
+    return pl.pallas_call(
+        finish_kernel,
+        out_shape=jax.ShapeDtypeStruct((8, freqs, share), jnp.float32),
+        in_specs=[VMEM],
+        out_specs=VMEM,
+        compiler_params=pltpu.CompilerParams(vmem_limit_bytes=4 * 1024 * 1024),
+        name="finish",
+    )(arrived)
 
 
 def spread_rows(samples, root):
@@ -281,11 +370,7 @@
     row, col = lax.axis_index("rows"), lax.axis_index("cols")
     rows, cols = lax.axis_size("rows"), lax.axis_size("cols")
 
-    mats = material_id.astype(jnp.float32)[None]
-    fields = (e_field, h_field, polar, polar_rate, mats)
-    own = jnp.concatenate(fields, 0)
-    first = jnp.concatenate([v[:, :, :HALO] for v in fields], 0)
-    final = jnp.concatenate([v[:, :, -HALO:] for v in fields], 0)
+    own, first, final = pack(e_field, h_field, polar, polar_rate, material_id)
     yhi = shifted(first, "cols", -1)
     ylo = shifted(final, "cols", 1)
     xhi = shifted(own, "rows", -1)
@@ -300,17 +385,17 @@
     table = material_table(eps_inf, delta_eps, pole_freq, damping)
     where = jnp.stack(
         [row > 0, row < rows - 1, col > 0, col < cols - 1, local_row, local_row]
-    ).astype(jnp.float32).reshape(3, 2)
-    e_out, h_out, p_out, j_out, samples = yee_steps(
-        where, table, own, ylo, yhi, xlo, xhi, clo, chi
-    )
+    ).astype(jnp.int32).reshape(3, 2)
 
     total_f = rows * freq_block
     freq_ids = row * freq_block + jnp.arange(freq_block, dtype=jnp.int32)
     omegas = OMEGA_LO + (OMEGA_HI - OMEGA_LO) * (freq_ids.astype(jnp.float32) / (total_f - 1))
     times = (jnp.arange(STEPS).astype(jnp.float32) + 1.0) * COURANT
     angles = times[:, None] * omegas[None, :]
-    ids_float = direction_ids.astype(jnp.float32)
+    count = direction_ids.shape[0]
+    share = count // cols
+    pairs = direction_ids.reshape(cols, 2, share // 2, 2).transpose(1, 0, 2, 3)
+    ids_float = pairs.reshape(count, 2).astype(jnp.float32)
     dir_y = SPREAD * (2.0 * ids_float[:, 0] / (G - 1) - 1.0)
     dir_z = SPREAD * (2.0 * ids_float[:, 1] / (G - 1) - 1.0)
     dir_x = jnp.sqrt(1.0 - dir_y * dir_y - dir_z * dir_z)
@@ -320,17 +405,21 @@
         omegas[:, None, None] * (pos_y[:, None] * dir_y[None, :] + plane_x * dir_x[None, :])[None]
     )
     high, low = z_phases(omegas, dir_z, cells_z)
-
+    waves = (
+        high, low, jnp.cos(phase_y), jnp.sin(phase_y), jnp.cos(angles), jnp.sin(angles), where, table,
+    )
+    waves, (xlo, xhi, clo, chi) = lax.optimization_barrier((waves, (xlo, xhi, clo, chi)))
+    high, low, cos_y, sin_y, cos_a, sin_a, where, table = waves
+    e_out, h_out, p_out, j_out, samples = yee_steps(
+        where, table, own, ylo, yhi, xlo, xhi, clo, chi
+    )
     received = spread_rows(samples, root_row)
     dft_out, partial_sum = radiate(
-        jnp.cos(angles), jnp.sin(angles), received, dft_acc, high, low,
-        jnp.cos(phase_y), jnp.sin(phase_y),
+        cos_a, sin_a, received, dft_acc, high, low, cos_y, sin_y,
     )
     pieces = partial_sum.reshape(cols, -1, partial_sum.shape[-1])
     arrived = lax.all_to_all(pieces, "cols", split_axis=0, concat_axis=0, tiled=True)
-    scale = 1.0 / math.sqrt(cols * cells_y * cells_z)
-    far = jnp.sum(arrived, axis=0) * scale
-    far_field = far[:, : 8 * freq_block].T.reshape(8, freq_block, -1)
+    far_field = finish(arrived, 1.0 / math.sqrt(cols * cells_y * cells_z), freq_block)
     return (e_out, h_out, p_out, j_out, dft_out, far_field)
 
 

time: 132 us -> 125 us (0.947)
  the two profiles are of different devices: /device:TPU:2 before, /device:TPU:1 now
where the time goes in v2:
time: 125 us; the launch traced here: 124 us
  blocking collectives  42.6 us (34%)
  starting transfers between devices  27 us (22%)
  Pallas kernels  25.6 us (20%)
  waiting for transfers between devices  21.4 us (17%)
  other arithmetic  3.23 us (3%)
  local copies, waits for them, and re-layouts  2.79 us (2%)
  between operations  1.51 us (1%)
    all_to_all x1, blocking collectives, local(): lax.all_to_all(pieces, 'cols', split_axis=0, concat_axis=0, tiled=True)  32.2 us
    ppermute x6, starting transfers between devices, shifted(): lax.ppermute(value, axis, [(source, source + steps) for source in range(f...  19.4 us
    pallas_call x1, Pallas kernels, yee_steps(): pl.pallas_call(yee_kernel, out_shape=[block] * 4 + [jax.ShapeDtypeStruct(...  18.2 us
    ppermute x6, waiting for transfers between devices, shifted(): lax.ppermute(value, axis, [(source, source + steps) for source in range(f...  14.2 us
    all_to_all x1, blocking collectives, spread_rows(): lax.all_to_all(copies, 'rows', split_axis=0, concat_axis=0, tiled=True)  10.4 us
    all_to_all x1, starting transfers between devices, spread_rows(): lax.all_to_all(pieces, 'rows', split_axis=0, concat_axis=0, tiled=True)  7.66 us
    all_to_all x1, waiting for transfers between devices, spread_rows(): lax.all_to_all(pieces, 'rows', split_axis=0, concat_axis=0, tiled=True)  7.16 us
    pallas_call x1, Pallas kernels, radiate(): pl.pallas_call(radiation_kernel, out_shape=[jax.ShapeDtypeStruct(acc.shap...  3.63 us
  transfers between devices with their start and end apart: 7, of which 5 were waited for; matrix products, arithmetic and copies ran while one was open for 3% of the time, Pallas kernels for 0%

profile of v2, /device:TPU:1, one launch (start us, length us, event | category | flops | bytes accessed | tf_op | source)
XLA Modules:
  0.0 124.2 jit_solution(14875044051262178912)
XLA Ops:
  0.6 2.5 %pack.1 = (f32[13,8,16,128]{3,2,1,0:T(8,128)}, f32[13,8,8,128]{3,2,1,0:T(8,128)S(1)}, f32[13,8,8,128]{3,2,1,0:T(8,128)S(1)}) custom-call(f32[3,8,16,128]{3,2,1,0:T(8,128)} %e_ref.1, f32[3,8,16,128]{3,2,1,0:T(8,128)} %h_ref.1, f32[3,8,16,128]{3,2,1,0:T(8,128)} %p_ref.1, f32[3,8,16,128]{3,2,1,0:T(8,128)} %j_ref.1, s32[8,16,128]{2,1,0:T(8,128)} %m_ref.1), custom_call_target="tpu_custom_call" | custom-call | tf_op jit(solution)/shard_map/pack/pallas_call | solution.py:68
  3.2 8.7 %collective-permute-start.1 = (f32[13,8,16,128]{3,2,1,0:T(8,128)}, f32[13,8,16,128]{3,2,1,0:T(8,128)}, u32[]{:S(2)}, u32[]{:S(2)}) collective-permute-start(f32[13,8,16,128]{3,2,1,0:T(8,128)} %get-tuple-element.32.own_ref), channel_id=1, source_target_pairs={{32,0},{64,32},{96,64},{128,96},{160,128},{192,160},{224,192},{256... | collective-permute-start | bytes 2555912 | tf_op jit(solution)/shard_map/ppermute | solution.py:28
  11.9 1.9 %collective-permute-start = (f32[13,8,16,128]{3,2,1,0:T(8,128)}, f32[13,8,16,128]{3,2,1,0:T(8,128)}, u32[]{:S(2)}, u32[]{:S(2)}) collective-permute-start(f32[13,8,16,128]{3,2,1,0:T(8,128)} %get-tuple-element.32.own_ref), channel_id=1, source_target_pairs={{0,32},{32,64},{64,96},{96,128},{128,160},{160,192},{192,224},{224... | collective-permute-start | bytes 2555912 | tf_op jit(solution)/shard_map/ppermute | solution.py:28
  13.8 1.3 %collective-permute-start.2 = (f32[13,8,8,128]{3,2,1,0:T(8,128)S(1)}, f32[13,8,8,128]{3,2,1,0:T(8,128)S(1)}, u32[]{:S(2)}, u32[]{:S(2)}) collective-permute-start(f32[13,8,8,128]{3,2,1,0:T(8,128)S(1)} %get-tuple-element.33), channel_id=1, source_target_pairs={{0,1},{1,2},{2,3},{3,4},{4,5},{5,6},{6,7},{7,8},{8,9},{9,10},{10,1... | collective-permute-start | bytes 1277960 | tf_op jit(solution)/shard_map/ppermute | solution.py:28
  15.2 1.3 %collective-permute-start.3 = (f32[13,8,8,128]{3,2,1,0:T(8,128)S(1)}, f32[13,8,8,128]{3,2,1,0:T(8,128)S(1)}, u32[]{:S(2)}, u32[]{:S(2)}) collective-permute-start(f32[13,8,8,128]{3,2,1,0:T(8,128)S(1)} %get-tuple-element.34), channel_id=1, source_target_pairs={{1,0},{2,1},{3,2},{4,3},{5,4},{6,5},{7,6},{8,7},{9,8},{10,9},{11,1... | collective-permute-start | bytes 1277960 | tf_op jit(solution)/shard_map/ppermute | solution.py:28
  17.2 0.0 copy-start.2
  17.2 0.7 copy-done.2
  17.9 0.1 convert_element_type.63
  18.0 0.1 convert_element_type.65
  18.2 0.1 multiply_add_fusion
  18.2 0.1 broadcast_multiply_fusion.1
  18.3 1.0 multiply_sine_fusion
  19.3 3.9 %collective-permute-done.2.ylo_ref = f32[13,8,8,128]{3,2,1,0:T(8,128)S(1)} collective-permute-done((f32[13,8,8,128]{3,2,1,0:T(8,128)S(1)}, f32[13,8,8,128]{3,2,1,0:T(8,128)S(1)}, u32[]{:S(2)}, u32[]{:S(2)}) %collective-permute-start.2) | collective-permute-done | bytes 426016 | tf_op jit(solution)/shard_map/ppermute | solution.py:28
  23.2 3.9 %collective-permute-done.3.yhi_ref = f32[13,8,8,128]{3,2,1,0:T(8,128)S(1)} collective-permute-done((f32[13,8,8,128]{3,2,1,0:T(8,128)S(1)}, f32[13,8,8,128]{3,2,1,0:T(8,128)S(1)}, u32[]{:S(2)}, u32[]{:S(2)}) %collective-permute-start.3) | collective-permute-done | bytes 426016 | tf_op jit(solution)/shard_map/ppermute | solution.py:28
  27.0 1.0 pad_maximum_fusion
  28.0 4.2 %collective-permute-start.5 = (f32[2,13,8,8,128]{4,3,2,1,0:T(8,128)}, f32[2,13,8,8,128]{4,3,2,1,0:T(8,128)}, u32[]{:S(2)}, u32[]{:S(2)}) collective-permute-start(f32[2,13,8,8,128]{4,3,2,1,0:T(8,128)} %pad_maximum_fusion), channel_id=1, source_target_pairs={{32,0},{64,32},{96,64},{128,96},{160,128},{192,160},{224,192},{256... | collective-permute-start | bytes 2555912 | tf_op jit(solution)/shard_map/ppermute | solution.py:28
  32.2 1.9 %collective-permute-start.4 = (f32[2,13,8,8,128]{4,3,2,1,0:T(8,128)}, f32[2,13,8,8,128]{4,3,2,1,0:T(8,128)}, u32[]{:S(2)}, u32[]{:S(2)}) collective-permute-start(f32[2,13,8,8,128]{4,3,2,1,0:T(8,128)} %pad_maximum_fusion), channel_id=1, source_target_pairs={{0,32},{32,64},{64,96},{96,128},{128,160},{160,192},{192,224},{224... | collective-permute-start | bytes 2555912 | tf_op jit(solution)/shard_map/ppermute | solution.py:28
  34.1 0.9 multiply_sine_fusion.2
  35.0 0.1 stack.64
  35.1 0.1 reshape.198.where_ref
  35.2 0.0 copy-start.1
  35.2 0.8 copy-done.1
  36.1 0.0 copy-start.3
  36.1 0.0 copy-start.4
  36.1 0.5 z_phases.1
  36.6 0.2 copy-done.3
  36.7 0.0 copy-done.4
  36.7 0.0 copy-start.5
  36.7 0.0 copy-start.6
  36.7 0.6 copy-done.5
  37.4 0.0 copy-done.6
  37.4 0.1 multiply_sine_fusion.3
  37.5 0.0 collective-permute-done.1.xhi_ref
  37.5 0.0 collective-permute-done.xlo_ref
  37.6 4.7 %collective-permute-done.5.chi_ref = f32[2,13,8,8,128]{4,3,2,1,0:T(8,128)} collective-permute-done((f32[2,13,8,8,128]{4,3,2,1,0:T(8,128)}, f32[2,13,8,8,128]{4,3,2,1,0:T(8,128)}, u32[]{:S(2)}, u32[]{:S(2)}) %collective-permute-start.5) | collective-permute-done | bytes 852000 | tf_op jit(solution)/shard_map/ppermute | solution.py:28
  42.3 1.7 %collective-permute-done.4.clo_ref = f32[2,13,8,8,128]{4,3,2,1,0:T(8,128)} collective-permute-done((f32[2,13,8,8,128]{4,3,2,1,0:T(8,128)}, f32[2,13,8,8,128]{4,3,2,1,0:T(8,128)}, u32[]{:S(2)}, u32[]{:S(2)}) %collective-permute-start.4) | collective-permute-done | bytes 852000 | tf_op jit(solution)/shard_map/ppermute | solution.py:28
  44.0 18.2 %yee_steps.1 = (f32[3,8,16,128]{3,2,1,0:T(8,128)}, f32[3,8,16,128]{3,2,1,0:T(8,128)}, f32[3,8,16,128]{3,2,1,0:T(8,128)}, f32[3,8,16,128]{3,2,1,0:T(8,128)}, f32[8,4,16,128]{3,2,1,0:T(8,128)}) custom-call(s32[3,2]{1,0:T(4,128)S(1)} %reshape.198.where_ref, f32[4,8,128]{2,1,0:T(8,128)S(1)} %broadcast_in_dim.6.table_ref, ...), custom_call_target="tpu_custom_call" | custom-call | tf_op jit(solution)/shard_map/yee_steps/pallas_call | solution.py:213
  62.2 7.7 %all-to-all-start = ((f32[16,32,128]{2,1,0:T(8,128)}), f32[16,32,128]{2,1,0:T(8,128)S(1)}, u32[]{:S(2)}, u32[]{:S(2)}) async-start(f32[16,32,128]{2,1,0:T(8,128)} %bitcast.15), calls=%async_computation | async-start | bytes 524288 | tf_op jit(solution)/shard_map/all_to_all | solution.py:357
  69.9 0.0 copy-start
  69.9 7.2 %all-to-all-done = f32[16,32,128]{2,1,0:T(8,128)S(1)} async-done(((f32[16,32,128]{2,1,0:T(8,128)}), f32[16,32,128]{2,1,0:T(8,128)S(1)}, u32[]{:S(2)}, u32[]{:S(2)}) %all-to-all-start) | async-done | bytes 262176 | tf_op jit(solution)/shard_map/all_to_all | solution.py:357
  77.1 10.4 %all_to_all.15 = f32[16,32,128]{2,1,0:T(8,128)S(1)} all-to-all(f32[16,32,128]{2,1,0:T(8,128)S(1)} %broadcast_in_dim.8), channel_id=1, replica_groups=mesh['rows'=16,'cols'=32] {'rows'}, dimensions={0} | all-to-all | bytes 524288 | tf_op jit(solution)/shard_map/all_to_all | solution.py:360
  87.5 0.0 copy-done
  87.6 3.6 %radiate.1 = (f32[8,8,16,128]{3,2,1,0:T(8,128)}, f32[128,128]{1,0:T(8,128)S(1)}) custom-call(f32[8,8]{1,0:T(8,128)S(1)} %get-tuple-element.45.cos_ref, f32[8,8]{1,0:T(8,128)S(1)} %get-tuple-element.46.sin_ref, f32[8,4,16,128]{3,2,1,0:T(8,128)S(1)} %bitcast.37, f32[8,8,16,128]{3,2,1,0:T(8,128)S(1)} %copy-done, ...), custom_call_target="tpu_custom_call" | custom-call | tf_op jit(solution)/shard_map/radiate/pallas_call | solution.py:321
  91.2 32.2 %all_to_all.16.in_ref = f32[32,4,128]{2,1,0:T(4,128)S(1)} all-to-all(f32[32,4,128]{2,1,0:T(4,128)S(1)} %bitcast.38), channel_id=1, replica_groups=mesh['rows'=16,'cols'=32] {'cols'}, dimensions={0} | all-to-all | bytes 131072 | tf_op jit(solution)/shard_map/all_to_all | solution.py:421
  123.4 0.8 finish.1
  (14 shorter events, 0.1 us)
Async XLA Ops:
  3.2 34.4 %collective-permute-start.1 = (f32[13,8,16,128]{3,2,1,0:T(8,128)}, f32[13,8,16,128]{3,2,1,0:T(8,128)}, u32[]{:S(2)}, u32[]{:S(2)}) collective-permute-start(f32[13,8,16,128]{3,2,1,0:T(8,128)} %get-tuple-element.32.own_ref), channel_id=1, source_target_pairs={{32,0},{64,32},{96,64},{128,96},{160,128},{192,160},{224,192},{256... | collective-permute-start | bytes 2555912 | tf_op jit(solution)/shard_map/ppermute | solution.py:28
  11.9 25.6 %collective-permute-start = (f32[13,8,16,128]{3,2,1,0:T(8,128)}, f32[13,8,16,128]{3,2,1,0:T(8,128)}, u32[]{:S(2)}, u32[]{:S(2)}) collective-permute-start(f32[13,8,16,128]{3,2,1,0:T(8,128)} %get-tuple-element.32.own_ref), channel_id=1, source_target_pairs={{0,32},{32,64},{64,96},{96,128},{128,160},{160,192},{192,224},{224... | collective-permute-start | bytes 2555912 | tf_op jit(solution)/shard_map/ppermute | solution.py:28
  13.8 9.3 %collective-permute-start.2 = (f32[13,8,8,128]{3,2,1,0:T(8,128)S(1)}, f32[13,8,8,128]{3,2,1,0:T(8,128)S(1)}, u32[]{:S(2)}, u32[]{:S(2)}) collective-permute-start(f32[13,8,8,128]{3,2,1,0:T(8,128)S(1)} %get-tuple-element.33), channel_id=1, source_target_pairs={{0,1},{1,2},{2,3},{3,4},{4,5},{5,6},{6,7},{7,8},{8,9},{9,10},{10,1... | collective-permute-start | bytes 1277960 | tf_op jit(solution)/shard_map/ppermute | solution.py:28
  15.2 11.8 %collective-permute-start.3 = (f32[13,8,8,128]{3,2,1,0:T(8,128)S(1)}, f32[13,8,8,128]{3,2,1,0:T(8,128)S(1)}, u32[]{:S(2)}, u32[]{:S(2)}) collective-permute-start(f32[13,8,8,128]{3,2,1,0:T(8,128)S(1)} %get-tuple-element.34), channel_id=1, source_target_pairs={{1,0},{2,1},{3,2},{4,3},{5,4},{6,5},{7,6},{8,7},{9,8},{10,9},{11,1... | collective-permute-start | bytes 1277960 | tf_op jit(solution)/shard_map/ppermute | solution.py:28
  17.2 0.7 copy-start.2
  28.0 14.3 %collective-permute-start.5 = (f32[2,13,8,8,128]{4,3,2,1,0:T(8,128)}, f32[2,13,8,8,128]{4,3,2,1,0:T(8,128)}, u32[]{:S(2)}, u32[]{:S(2)}) collective-permute-start(f32[2,13,8,8,128]{4,3,2,1,0:T(8,128)} %pad_maximum_fusion), channel_id=1, source_target_pairs={{32,0},{64,32},{96,64},{128,96},{160,128},{192,160},{224,192},{256... | collective-permute-start | bytes 2555912 | tf_op jit(solution)/shard_map/ppermute | solution.py:28
  32.2 11.9 %collective-permute-start.4 = (f32[2,13,8,8,128]{4,3,2,1,0:T(8,128)}, f32[2,13,8,8,128]{4,3,2,1,0:T(8,128)}, u32[]{:S(2)}, u32[]{:S(2)}) collective-permute-start(f32[2,13,8,8,128]{4,3,2,1,0:T(8,128)} %pad_maximum_fusion), channel_id=1, source_target_pairs={{0,32},{32,64},{64,96},{96,128},{128,160},{160,192},{192,224},{224... | collective-permute-start | bytes 2555912 | tf_op jit(solution)/shard_map/ppermute | solution.py:28
  35.2 0.8 copy-start.1
  36.1 0.7 copy-start.3
  36.1 0.7 copy-start.4
  36.7 0.7 copy-start.5
  36.7 0.7 copy-start.6
  62.2 14.9 %all-to-all-start = ((f32[16,32,128]{2,1,0:T(8,128)}), f32[16,32,128]{2,1,0:T(8,128)S(1)}, u32[]{:S(2)}, u32[]{:S(2)}) async-start(f32[16,32,128]{2,1,0:T(8,128)} %bitcast.15), calls=%async_computation | async-start | bytes 524288 | tf_op jit(solution)/shard_map/all_to_all | solution.py:357
  69.9 17.7 %copy-start = (f32[8,8,16,128]{3,2,1,0:T(8,128)S(1)}, f32[8,8,16,128]{3,2,1,0:T(8,128)}, u32[]{:S(2)}) copy-start(f32[8,8,16,128]{3,2,1,0:T(8,128)} %acc_ref.1) | copy-start | bytes 1572868

commit v3 on v2

--- a/solution.py
+++ b/solution.py
@@ -87,7 +87,7 @@
 
 
 def yee_kernel(
-    where_ref, table_ref, own_ref, ylo_ref, yhi_ref, xlo_ref, xhi_ref, clo_ref, chi_ref,
+    where_ref, table_ref, own_ref, ylo_ref, yhi_ref, xlo_ref, xhi_ref, ll_ref, lh_ref, hl_ref, hh_ref,
     e_out, h_out, p_out, j_out, sample_out, even, odd, coef,
 ):
     cells_x, cells_y, cells_z = own_ref.shape[1:]
@@ -97,9 +97,9 @@
     x_spans = ((0, HALO), inner_x, (inner_x[1], wide_x))
     y_spans = ((0, HALO), inner_y, (inner_y[1], wide_y))
     parts = (
-        ((clo_ref, 0), (xlo_ref, None), (clo_ref, 1)),
-        ((ylo_ref, None), (own_ref, None), (yhi_ref, None)),
-        ((chi_ref, 0), (xhi_ref, None), (chi_ref, 1)),
+        (ll_ref, xlo_ref, lh_ref),
+        (ylo_ref, own_ref, yhi_ref),
+        (hl_ref, xhi_ref, hh_ref),
     )
     gains = (1.0, 2.0, 4.0, 2.0)
     whole = slice(0, wide_y)
@@ -107,8 +107,7 @@
     tables = [table_ref[c] for c in range(4)]
     for i, (x0, x1) in enumerate(x_spans):
         for k, (y0, y1) in enumerate(y_spans):
-            ref, lead = parts[i][k]
-            part = ref if lead is None else ref.at[lead]
+            part = parts[i][k]
             inside = jnp.float32(1.0)
             if i != 1:
                 inside = inside * where_ref[0, i // 2].astype(jnp.float32)
@@ -205,20 +204,20 @@
     lax.fori_loop(0, cells_x, emit, 0, unroll=2)
 
 
-def yee_steps(where, table, own, ylo, yhi, xlo, xhi, clo, chi):
-    cells = own.shape[1:]
+def yee_steps(where, table, *blocks):
+    cells = blocks[0].shape[1:]
     block = jax.ShapeDtypeStruct((3,) + cells, jnp.float32)
     wide = (cells[0] + 2 * HALO, cells[1] + 2 * HALO, cells[2])
     state = pltpu.VMEM((12, wide[0], wide[1] + 8, wide[2]), jnp.float32)
     return pl.pallas_call(
         yee_kernel,
         out_shape=[block] * 4 + [jax.ShapeDtypeStruct((STEPS, 4) + cells[1:], jnp.float32)],
-        in_specs=[SMEM, VMEM] + [VMEM] * 7,
+        in_specs=[SMEM, VMEM] + [VMEM] * len(blocks),
         out_specs=[VMEM] * 5,
         scratch_shapes=[state, state, pltpu.VMEM((4,) + wide, jnp.float32)],
         compiler_params=pltpu.CompilerParams(vmem_limit_bytes=20 * 1024 * 1024),
         name="yee_steps",
-    )(where, table, own, ylo, yhi, xlo, xhi, clo, chi)
+    )(where, table, *blocks)
 
 
 def halves(value):
@@ -371,13 +370,14 @@
     rows, cols = lax.axis_size("rows"), lax.axis_size("cols")
 
     own, first, final = pack(e_field, h_field, polar, polar_rate, material_id)
+    ylo = shifted(final, "cols", 1)
     yhi = shifted(first, "cols", -1)
-    ylo = shifted(final, "cols", 1)
     xhi = shifted(own, "rows", -1)
     xlo = shifted(own, "rows", 1)
-    sides = jnp.stack([ylo, yhi])
-    chi = shifted(sides, "rows", -1)
-    clo = shifted(sides, "rows", 1)
+    corner_hl = shifted(ylo, "rows", -1)
+    corner_ll = shifted(ylo, "rows", 1)
+    corner_hh = shifted(yhi, "rows", -1)
+    corner_lh = shifted(yhi, "rows", 1)
 
     plane_row = plane_index[0]
     root_row = plane_row // cells_x
@@ -406,12 +406,11 @@
     )
     high, low = z_phases(omegas, dir_z, cells_z)
     waves = (
-        high, low, jnp.cos(phase_y), jnp.sin(phase_y), jnp.cos(angles), jnp.sin(angles), where, table,
-    )
-    waves, (xlo, xhi, clo, chi) = lax.optimization_barrier((waves, (xlo, xhi, clo, chi)))
-    high, low, cos_y, sin_y, cos_a, sin_a, where, table = waves
+        jnp.cos(phase_y), jnp.sin(phase_y), jnp.cos(angles), jnp.sin(angles),
+    )
+    cos_y, sin_y, cos_a, sin_a = waves
     e_out, h_out, p_out, j_out, samples = yee_steps(
-        where, table, own, ylo, yhi, xlo, xhi, clo, chi
+        where, table, own, ylo, yhi, xlo, xhi, corner_ll, corner_lh, corner_hl, corner_hh
     )
     received = spread_rows(samples, root_row)
     dft_out, partial_sum = radiate(

time: 125 us -> 125 us (level)
  blocking collectives: 42.6 us -> 33.7 us
  starting transfers between devices: 27 us -> 35 us
  waiting for transfers between devices: 21.4 us -> 25 us
  Pallas kernels: 25.6 us -> 23.9 us
  other arithmetic: 3.23 us -> 1.62 us
    all_to_all x1 -> x0, blocking collectives: 10.4 us -> none  [spread_rows(): lax.all_to_all(copies, 'rows', split_axis=0, concat_axis=0, tiled=True)]
    all_to_all x0 -> x1, waiting for transfers between devices: none -> 6.35 us  [spread_rows(): lax.all_to_all(copies, 'rows', split_axis=0, concat_axis=0, tiled=True)]
    all_to_all x0 -> x1, starting transfers between devices: none -> 4.2 us  [spread_rows(): lax.all_to_all(copies, 'rows', split_axis=0, concat_axis=0, tiled=True)]
    ppermute x6 -> x8, starting transfers between devices: 19.4 us -> 22.6 us  [shifted(): lax.ppermute(value, axis, [(source, source + steps) for source in range(f...]
    ppermute x6 -> x8, waiting for transfers between devices: 14.2 us -> 12.5 us  [shifted(): lax.ppermute(value, axis, [(source, source + steps) for source in range(f...]
    pallas_call x1, Pallas kernels: 18.2 us -> 16.5 us  [yee_steps(): pl.pallas_call(yee_kernel, out_shape=[block] * 4 + [jax.ShapeDtypeStruct(...]
    all_to_all x1, blocking collectives: 32.2 us -> 33.7 us  [local(): lax.all_to_all(pieces, 'cols', split_axis=0, concat_axis=0, tiled=True)]
  transfers between devices with their start and end apart: 7 -> 10, of which waited for: 5 -> 5; matrix products, arithmetic and copies ran while one was open for 3% -> 2% of each run, Pallas kernels for 0% -> 0%
where the time goes in v3:
time: 125 us
  starting transfers between devices  35 us (28%)
  blocking collectives  33.7 us (27%)
  waiting for transfers between devices  25 us (20%)
  Pallas kernels  23.9 us (19%)
  local copies, waits for them, and re-layouts  3.86 us (3%)
  other arithmetic  1.62 us (1%)
  between operations  1.57 us (1%)
    all_to_all x1, blocking collectives, local(): lax.all_to_all(pieces, 'cols', split_axis=0, concat_axis=0, tiled=True)  33.7 us
    ppermute x8, starting transfers between devices, shifted(): lax.ppermute(value, axis, [(source, source + steps) for source in range(f...  22.6 us
    pallas_call x1, Pallas kernels, yee_steps(): pl.pallas_call(yee_kernel, out_shape=[block] * 4 + [jax.ShapeDtypeStruct(...  16.5 us
    ppermute x8, waiting for transfers between devices, shifted(): lax.ppermute(value, axis, [(source, source + steps) for source in range(f...  12.5 us
    all_to_all x1, starting transfers between devices, spread_rows(): lax.all_to_all(pieces, 'rows', split_axis=0, concat_axis=0, tiled=True)  8.27 us
    all_to_all x1, waiting for transfers between devices, spread_rows(): lax.all_to_all(copies, 'rows', split_axis=0, concat_axis=0, tiled=True)  6.35 us
    all_to_all x1, waiting for transfers between devices, spread_rows(): lax.all_to_all(pieces, 'rows', split_axis=0, concat_axis=0, tiled=True)  6.17 us
    all_to_all x1, starting transfers between devices, spread_rows(): lax.all_to_all(copies, 'rows', split_axis=0, concat_axis=0, tiled=True)  4.2 us
  transfers between devices with their start and end apart: 10, of which 5 were waited for; matrix products, arithmetic and copies ran while one was open for 2% of the time, Pallas kernels for 0%

profile of v3, /device:TPU:1, one launch (start us, length us, event | category | flops | bytes accessed | tf_op | source)
XLA Modules:
  0.0 124.7 jit_solution(3603943714539040220)
XLA Ops:
  0.6 2.5 %pack.1 = (f32[13,8,16,128]{3,2,1,0:T(8,128)S(1)}, f32[13,8,8,128]{3,2,1,0:T(8,128)}, f32[13,8,8,128]{3,2,1,0:T(8,128)}) custom-call(f32[3,8,16,128]{3,2,1,0:T(8,128)} %e_ref.1, f32[3,8,16,128]{3,2,1,0:T(8,128)} %h_ref.1, f32[3,8,16,128]{3,2,1,0:T(8,128)} %p_ref.1, f32[3,8,16,128]{3,2,1,0:T(8,128)} %j_ref.1, s32[8,16,128]{2,1,0:T(8,128)} %m_ref.1), custom_call_target="tpu_custom_call" | custom-call | tf_op jit(solution)/shard_map/pack/pallas_call | solution.py:68
  3.1 4.5 %collective-permute-start.2 = (f32[13,8,16,128]{3,2,1,0:T(8,128)S(1)}, f32[13,8,16,128]{3,2,1,0:T(8,128)S(1)}, u32[]{:S(2)}, u32[]{:S(2)}) collective-permute-start(f32[13,8,16,128]{3,2,1,0:T(8,128)S(1)} %get-tuple-element.18.own_ref), channel_id=1, source_target_pairs={{0,32},{32,64},{64,96},{96,128},{128,160},{160,192},{192,224},{224... | collective-permute-start | bytes 2555912 | tf_op jit(solution)/shard_map/ppermute | solution.py:28
  7.7 5.6 %collective-permute-start.3 = (f32[13,8,16,128]{3,2,1,0:T(8,128)S(1)}, f32[13,8,16,128]{3,2,1,0:T(8,128)S(1)}, u32[]{:S(2)}, u32[]{:S(2)}) collective-permute-start(f32[13,8,16,128]{3,2,1,0:T(8,128)S(1)} %get-tuple-element.18.own_ref), channel_id=1, source_target_pairs={{32,0},{64,32},{96,64},{128,96},{160,128},{192,160},{224,192},{256... | collective-permute-start | bytes 2555912 | tf_op jit(solution)/shard_map/ppermute | solution.py:28
  13.3 1.3 %collective-permute-start = (f32[13,8,8,128]{3,2,1,0:T(8,128)}, f32[13,8,8,128]{3,2,1,0:T(8,128)S(1)}, u32[]{:S(2)}, u32[]{:S(2)}) collective-permute-start(f32[13,8,8,128]{3,2,1,0:T(8,128)} %get-tuple-element.19), channel_id=1, source_target_pairs={{0,1},{1,2},{2,3},{3,4},{4,5},{5,6},{6,7},{7,8},{8,9},{9,10},{10,1... | collective-permute-start | bytes 1277960 | tf_op jit(solution)/shard_map/ppermute | solution.py:28
  14.6 1.3 %collective-permute-start.1 = (f32[13,8,8,128]{3,2,1,0:T(8,128)}, f32[13,8,8,128]{3,2,1,0:T(8,128)S(1)}, u32[]{:S(2)}, u32[]{:S(2)}) collective-permute-start(f32[13,8,8,128]{3,2,1,0:T(8,128)} %get-tuple-element.20), channel_id=1, source_target_pairs={{1,0},{2,1},{3,2},{4,3},{5,4},{6,5},{7,6},{8,7},{9,8},{10,9},{11,1... | collective-permute-start | bytes 1277960 | tf_op jit(solution)/shard_map/ppermute | solution.py:28
  16.6 0.1 stack.55
  16.7 0.1 reshape.198.where_ref
  16.8 0.0 copy-start.2
  16.8 0.7 copy-done.2
  17.5 0.1 convert_element_type.64
  17.6 0.1 convert_element_type.66
  17.7 0.0 copy-start.3
  17.7 0.0 copy-start.4
  17.8 0.6 copy-done.3
  18.4 0.0 copy-done.4
  18.4 0.0 copy-start.6
  18.4 0.6 copy-done.5
  19.1 0.0 copy-done.6
  19.1 4.9 %collective-permute-done.ylo_ref = f32[13,8,8,128]{3,2,1,0:T(8,128)S(1)} collective-permute-done((f32[13,8,8,128]{3,2,1,0:T(8,128)}, f32[13,8,8,128]{3,2,1,0:T(8,128)S(1)}, u32[]{:S(2)}, u32[]{:S(2)}) %collective-permute-start) | collective-permute-done | bytes 426016 | tf_op jit(solution)/shard_map/ppermute | solution.py:28
  24.0 2.4 %collective-permute-start.4 = (f32[13,8,8,128]{3,2,1,0:T(8,128)S(1)}, f32[13,8,8,128]{3,2,1,0:T(8,128)S(1)}, u32[]{:S(2)}, u32[]{:S(2)}) collective-permute-start(f32[13,8,8,128]{3,2,1,0:T(8,128)S(1)} %collective-permute-done.ylo_ref), channel_id=1, source_target_pairs={{0,32},{32,64},{64,96},{96,128},{128,160},{160,192},{192,224},{224... | collective-permute-start | bytes 1277960 | tf_op jit(solution)/shard_map/ppermute | solution.py:28
  26.5 0.1 broadcast_multiply_fusion.1
  26.5 1.9 %collective-permute-start.6 = (f32[13,8,8,128]{3,2,1,0:T(8,128)S(1)}, f32[13,8,8,128]{3,2,1,0:T(8,128)S(1)}, u32[]{:S(2)}, u32[]{:S(2)}) collective-permute-start(f32[13,8,8,128]{3,2,1,0:T(8,128)S(1)} %collective-permute-done.ylo_ref), channel_id=1, source_target_pairs={{32,0},{64,32},{96,64},{128,96},{160,128},{192,160},{224,192},{256... | collective-permute-start | bytes 1277960 | tf_op jit(solution)/shard_map/ppermute | solution.py:28
  28.5 0.0 collective-permute-done.1.yhi_ref
  28.5 3.6 %collective-permute-start.5 = (f32[13,8,8,128]{3,2,1,0:T(8,128)S(1)}, f32[13,8,8,128]{3,2,1,0:T(8,128)S(1)}, u32[]{:S(2)}, u32[]{:S(2)}) collective-permute-start(f32[13,8,8,128]{3,2,1,0:T(8,128)S(1)} %collective-permute-done.1.yhi_ref), channel_id=1, source_target_pairs={{0,32},{32,64},{64,96},{96,128},{128,160},{160,192},{192,224},{224... | collective-permute-start | bytes 1277960 | tf_op jit(solution)/shard_map/ppermute | solution.py:28
  32.1 0.0 collective-permute-done.4.ll_ref
  32.1 1.9 %collective-permute-start.7 = (f32[13,8,8,128]{3,2,1,0:T(8,128)S(1)}, f32[13,8,8,128]{3,2,1,0:T(8,128)S(1)}, u32[]{:S(2)}, u32[]{:S(2)}) collective-permute-start(f32[13,8,8,128]{3,2,1,0:T(8,128)S(1)} %collective-permute-done.1.yhi_ref), channel_id=1, source_target_pairs={{32,0},{64,32},{96,64},{128,96},{160,128},{192,160},{224,192},{256... | collective-permute-start | bytes 1277960 | tf_op jit(solution)/shard_map/ppermute | solution.py:28
  34.1 0.1 multiply_add_fusion
  34.2 3.0 %collective-permute-done.5.lh_ref = f32[13,8,8,128]{3,2,1,0:T(8,128)S(1)} collective-permute-done((f32[13,8,8,128]{3,2,1,0:T(8,128)S(1)}, f32[13,8,8,128]{3,2,1,0:T(8,128)S(1)}, u32[]{:S(2)}, u32[]{:S(2)}) %collective-permute-start.5) | collective-permute-done | bytes 426016 | tf_op jit(solution)/shard_map/ppermute | solution.py:28
  37.2 0.0 collective-permute-done.6.hl_ref
  37.2 4.5 %collective-permute-done.7.hh_ref = f32[13,8,8,128]{3,2,1,0:T(8,128)S(1)} collective-permute-done((f32[13,8,8,128]{3,2,1,0:T(8,128)S(1)}, f32[13,8,8,128]{3,2,1,0:T(8,128)S(1)}, u32[]{:S(2)}, u32[]{:S(2)}) %collective-permute-start.7) | collective-permute-done | bytes 426016 | tf_op jit(solution)/shard_map/ppermute | solution.py:28
  41.7 0.0 collective-permute-done.2.xlo_ref
  41.7 0.0 collective-permute-done.3.xhi_ref
  41.7 16.5 %yee_steps.1 = (f32[3,8,16,128]{3,2,1,0:T(8,128)}, f32[3,8,16,128]{3,2,1,0:T(8,128)}, f32[3,8,16,128]{3,2,1,0:T(8,128)}, f32[3,8,16,128]{3,2,1,0:T(8,128)}, f32[8,4,16,128]{3,2,1,0:T(8,128)S(1)}) custom-call(s32[3,2]{1,0:T(4,128)S(1)} %reshape.198.where_ref, f32[4,8,128]{2,1,0:T(8,128)S(1)} %broadcast_in_dim.6.table_ref, ...), custom_call_target="tpu_custom_call" | custom-call | tf_op jit(solution)/shard_map/yee_steps/pallas_call | solution.py:212
  58.2 0.0 copy-start.1
  58.2 0.7 copy-done.1
  58.9 8.3 %all-to-all-start = ((f32[16,32,128]{2,1,0:T(8,128)}), f32[16,32,128]{2,1,0:T(8,128)S(1)}, u32[]{:S(2)}, u32[]{:S(2)}) async-start(f32[16,32,128]{2,1,0:T(8,128)} %bitcast.34), calls=%async_computation | async-start | bytes 524288 | tf_op jit(solution)/shard_map/all_to_all | solution.py:356
  67.2 1.0 multiply_sine_fusion
  68.2 6.2 %all-to-all-done = f32[16,32,128]{2,1,0:T(8,128)S(1)} async-done(((f32[16,32,128]{2,1,0:T(8,128)}), f32[16,32,128]{2,1,0:T(8,128)S(1)}, u32[]{:S(2)}, u32[]{:S(2)}) %all-to-all-start) | async-done | bytes 262176 | tf_op jit(solution)/shard_map/all_to_all | solution.py:356
  74.4 0.7 broadcast_in_dim.8
  75.1 4.2 %all-to-all-start.1 = ((f32[16,32,128]{2,1,0:T(8,128)}), f32[16,32,128]{2,1,0:T(8,128)S(1)}, u32[]{:S(2)}, u32[]{:S(2)}) async-start(f32[16,32,128]{2,1,0:T(8,128)} %broadcast_in_dim.8), calls=%async_computation.1 | async-start | bytes 524288 | tf_op jit(solution)/shard_map/all_to_all | solution.py:359
  79.3 0.3 multiply_sine_fusion.2
  79.6 0.5 z_phases.1
  80.1 0.1 multiply_sine_fusion.3
  80.2 6.3 %all-to-all-done.1 = f32[16,32,128]{2,1,0:T(8,128)S(1)} async-done(((f32[16,32,128]{2,1,0:T(8,128)}), f32[16,32,128]{2,1,0:T(8,128)S(1)}, u32[]{:S(2)}, u32[]{:S(2)}) %all-to-all-start.1) | async-done | bytes 262176 | tf_op jit(solution)/shard_map/all_to_all | solution.py:359
  86.6 0.0 copy-done
  86.6 3.6 %radiate.1 = (f32[8,8,16,128]{3,2,1,0:T(8,128)}, f32[128,128]{1,0:T(8,128)S(1)}) custom-call(f32[8,8]{1,0:T(8,128)S(1)} %get-tuple-element.39.cos_ref, f32[8,8]{1,0:T(8,128)S(1)} %get-tuple-element.38.sin_ref, f32[8,4,16,128]{3,2,1,0:T(8,128)S(1)} %bitcast.33, f32[8,8,16,128]{3,2,1,0:T(8,128)S(1)} %copy-done, ...), custom_call_target="tpu_custom_call" | custom-call | tf_op jit(solution)/shard_map/radiate/pallas_call | solution.py:320
  90.2 33.7 %all_to_all.15.in_ref = f32[32,4,128]{2,1,0:T(4,128)S(1)} all-to-all(f32[32,4,128]{2,1,0:T(4,128)S(1)} %bitcast.35), channel_id=1, replica_groups=mesh['rows'=16,'cols'=32] {'cols'}, dimensions={0} | all-to-all | bytes 131072 | tf_op jit(solution)/shard_map/all_to_all | solution.py:420
  123.9 0.8 finish.1
  (15 shorter events, 0.1 us)
Async XLA Ops:
  3.1 38.5 %collective-permute-start.2 = (f32[13,8,16,128]{3,2,1,0:T(8,128)S(1)}, f32[13,8,16,128]{3,2,1,0:T(8,128)S(1)}, u32[]{:S(2)}, u32[]{:S(2)}) collective-permute-start(f32[13,8,16,128]{3,2,1,0:T(8,128)S(1)} %get-tuple-element.18.own_ref), channel_id=1, source_target_pairs={{0,32},{32,64},{64,96},{96,128},{128,160},{160,192},{192,224},{224... | collective-permute-start | bytes 2555912 | tf_op jit(solution)/shard_map/ppermute | solution.py:28
  7.7 34.0 %collective-permute-start.3 = (f32[13,8,16,128]{3,2,1,0:T(8,128)S(1)}, f32[13,8,16,128]{3,2,1,0:T(8,128)S(1)}, u32[]{:S(2)}, u32[]{:S(2)}) collective-permute-start(f32[13,8,16,128]{3,2,1,0:T(8,128)S(1)} %get-tuple-element.18.own_ref), channel_id=1, source_target_pairs={{32,0},{64,32},{96,64},{128,96},{160,128},{192,160},{224,192},{256... | collective-permute-start | bytes 2555912 | tf_op jit(solution)/shard_map/ppermute | solution.py:28
  13.3 10.8 %collective-permute-start = (f32[13,8,8,128]{3,2,1,0:T(8,128)}, f32[13,8,8,128]{3,2,1,0:T(8,128)S(1)}, u32[]{:S(2)}, u32[]{:S(2)}) collective-permute-start(f32[13,8,8,128]{3,2,1,0:T(8,128)} %get-tuple-element.19), channel_id=1, source_target_pairs={{0,1},{1,2},{2,3},{3,4},{4,5},{5,6},{6,7},{7,8},{8,9},{9,10},{10,1... | collective-permute-start | bytes 1277960 | tf_op jit(solution)/shard_map/ppermute | solution.py:28
  14.6 13.9 %collective-permute-start.1 = (f32[13,8,8,128]{3,2,1,0:T(8,128)}, f32[13,8,8,128]{3,2,1,0:T(8,128)S(1)}, u32[]{:S(2)}, u32[]{:S(2)}) collective-permute-start(f32[13,8,8,128]{3,2,1,0:T(8,128)} %get-tuple-element.20), channel_id=1, source_target_pairs={{1,0},{2,1},{3,2},{4,3},{5,4},{6,5},{7,6},{8,7},{9,8},{10,9},{11,1... | collective-permute-start | bytes 1277960 | tf_op jit(solution)/shard_map/ppermute | solution.py:28
  16.8 0.7 copy-start.2
  17.7 0.7 copy-start.3
  17.7 0.7 copy-start.4
  18.4 0.7 copy-start.5
  18.4 0.7 copy-start.6
  24.0 8.1 %collective-permute-start.4 = (f32[13,8,8,128]{3,2,1,0:T(8,128)S(1)}, f32[13,8,8,128]{3,2,1,0:T(8,128)S(1)}, u32[]{:S(2)}, u32[]{:S(2)}) collective-permute-start(f32[13,8,8,128]{3,2,1,0:T(8,128)S(1)} %collective-permute-done.ylo_ref), channel_id=1, source_target_pairs={{0,32},{32,64},{64,96},{96,128},{128,160},{160,192},{192,224},{224... | collective-permute-start | bytes 1277960 | tf_op jit(solution)/shard_map/ppermute | solution.py:28
  26.5 10.6 %collective-permute-start.6 = (f32[13,8,8,128]{3,2,1,0:T(8,128)S(1)}, f32[13,8,8,128]{3,2,1,0:T(8,128)S(1)}, u32[]{:S(2)}, u32[]{:S(2)}) collective-permute-start(f32[13,8,8,128]{3,2,1,0:T(8,128)S(1)} %collective-permute-done.ylo_ref), channel_id=1, source_target_pairs={{32,0},{64,32},{96,64},{128,96},{160,128},{192,160},{224,192},{256... | collective-permute-start | bytes 1277960 | tf_op jit(solution)/shard_map/ppermute | solution.py:28
  28.5 8.7 %collective-permute-start.5 = (f32[13,8,8,128]{3,2,1,0:T(8,128)S(1)}, f32[13,8,8,128]{3,2,1,0:T(8,128)S(1)}, u32[]{:S(2)}, u32[]{:S(2)}) collective-permute-start(f32[13,8,8,128]{3,2,1,0:T(8,128)S(1)} %collective-permute-done.1.yhi_ref), channel_id=1, source_target_pairs={{0,32},{32,64},{64,96},{96,128},{128,160},{160,192},{192,224},{224... | collective-permute-start | bytes 1277960 | tf_op jit(solution)/shard_map/ppermute | solution.py:28
  32.1 9.6 %collective-permute-start.7 = (f32[13,8,8,128]{3,2,1,0:T(8,128)S(1)}, f32[13,8,8,128]{3,2,1,0:T(8,128)S(1)}, u32[]{:S(2)}, u32[]{:S(2)}) collective-permute-start(f32[13,8,8,128]{3,2,1,0:T(8,128)S(1)} %collective-permute-done.1.yhi_ref), channel_id=1, source_target_pairs={{32,0},{64,32},{96,64},{128,96},{160,128},{192,160},{224,192},{256... | collective-permute-start | bytes 1277960 | tf_op jit(solution)/shard_map/ppermute | solution.py:28
  58.2 0.7 copy-start.1
  58.9 15.5 %all-to-all-start = ((f32[16,32,128]{2,1,0:T(8,128)}), f32[16,32,128]{2,1,0:T(8,128)S(1)}, u32[]{:S(2)}, u32[]{:S(2)}) async-start(f32[16,32,128]{2,1,0:T(8,128)} %bitcast.34), calls=%async_computation | async-start | bytes 524288 | tf_op jit(solution)/shard_map/all_to_all | solution.py:356
  75.1 11.5 %copy-start = (f32[8,8,16,128]{3,2,1,0:T(8,128)S(1)}, f32[8,8,16,128]{3,2,1,0:T(8,128)}, u32[]{:S(2)}) copy-start(f32[8,8,16,128]{3,2,1,0:T(8,128)} %acc_ref.1) | copy-start | bytes 1572868
  75.1 11.5 %all-to-all-start.1 = ((f32[16,32,128]{2,1,0:T(8,128)}), f32[16,32,128]{2,1,0:T(8,128)S(1)}, u32[]{:S(2)}, u32[]{:S(2)}) async-start(f32[16,32,128]{2,1,0:T(8,128)} %broadcast_in_dim.8), calls=%async_computation.1 | async-start | bytes 524288 | tf_op jit(solution)/shard_map/all_to_all | solution.py:359

commit v4 on v3

--- a/solution.py
+++ b/solution.py
@@ -12,6 +12,7 @@
 HALO = 8
 G = 64
 FINE = 16
+LEVEL_BITS = 3
 
 COURANT = 0.5
 OMEGA_LO = 2.0 * math.pi / 24.0
@@ -32,10 +33,7 @@
     half_damp = 0.5 * damping
     keep = (1.0 - half_damp) / (1.0 + half_damp)
     drive = pole_freq * pole_freq / COURANT / (1.0 + half_damp)
-    table = jnp.stack([keep, 0.5 * drive, 4.0 * delta_eps, 0.5 * (COURANT / eps_inf)])
-    return jnp.broadcast_to(
-        jnp.pad(table, ((0, 0), (0, 128 - table.shape[1])))[:, None, :], (4, 8, 128)
-    )
+    return jnp.stack([keep, 0.5 * drive, 4.0 * delta_eps, 0.5 * (COURANT / eps_inf)])
 
 
 def pack_kernel(e_ref, h_ref, p_ref, j_ref, m_ref, own, first, final, mats, sems):
@@ -87,7 +85,7 @@
 
 
 def yee_kernel(
-    where_ref, table_ref, own_ref, ylo_ref, yhi_ref, xlo_ref, xhi_ref, ll_ref, lh_ref, hl_ref, hh_ref,
+    where_ref, table_ref, own_ref, ylo_ref, yhi_ref, xlo_ref, xhi_ref, clo_ref, chi_ref,
     e_out, h_out, p_out, j_out, sample_out, even, odd, coef,
 ):
     cells_x, cells_y, cells_z = own_ref.shape[1:]
@@ -97,14 +95,13 @@
     x_spans = ((0, HALO), inner_x, (inner_x[1], wide_x))
     y_spans = ((0, HALO), inner_y, (inner_y[1], wide_y))
     parts = (
-        (ll_ref, xlo_ref, lh_ref),
+        (clo_ref.at[0], xlo_ref, clo_ref.at[1]),
         (ylo_ref, own_ref, yhi_ref),
-        (hl_ref, xhi_ref, hh_ref),
+        (chi_ref.at[0], xhi_ref, chi_ref.at[1]),
     )
     gains = (1.0, 2.0, 4.0, 2.0)
     whole = slice(0, wide_y)
     zeros = jnp.zeros((HALO, cells_z), jnp.float32)
-    tables = [table_ref[c] for c in range(4)]
     for i, (x0, x1) in enumerate(x_spans):
         for k, (y0, y1) in enumerate(y_spans):
             part = parts[i][k]
@@ -117,14 +114,20 @@
             def fill(x, carry, part=part, inside=inside, x0=x0, y0=y0, y1=y1):
                 for comp in range(12):
                     even[comp, x0 + x, y0:y1, :] = part[comp, x] * gains[comp // 3]
-                for y in range(y0, y1, 8):
-                    ids = part[12, x, y - y0 : y - y0 + 8, :].astype(jnp.int32)
-                    for c in range(4):
-                        value = jnp.take_along_axis(tables[c], ids, axis=1)
-                        coef[c, x0 + x, y : y + 8, :] = value * inside if c == 3 else value
+                ids = part[12, x].astype(jnp.int32)
+                bits = [(ids & (1 << k)) != 0 for k in range(LEVEL_BITS)]
+                for c in range(4):
+                    values = [table_ref[c, level] for level in range(1 << LEVEL_BITS)]
+                    for bit in bits:
+                        values = [
+                            jnp.where(bit, odd_one, even_one)
+                            for even_one, odd_one in zip(values[::2], values[1::2])
+                        ]
+                    value = values[0]
+                    coef[c, x0 + x, y0:y1, :] = value * inside if c == 3 else value
                 return carry
 
-            lax.fori_loop(0, x1 - x0, fill, 0, unroll=2)
+            lax.fori_loop(0, x1 - x0, fill, 0, unroll=8)
     for buffer in (even, odd):
         for comp in (0, 2):
             for x in range(wide_x):
@@ -188,7 +191,8 @@
 
         put(step, magnetic(step))
         put(step + 1, magnetic(step + 1))
-        lax.fori_loop(step + 1, wide_x - 2 - step, both, 0)
+        both(step + 1, 0)
+        lax.fori_loop(step + 2, wide_x - 2 - step, both, 0, unroll=4)
         electric(wide_x - 2 - step)
         for slot, (comp, gain) in enumerate(((1, 1.0), (2, 1.0), (4, 0.5), (5, 0.5))):
             sample_out[step, slot] = new[comp, plane, inner_y[0] : inner_y[1], :] * gain
@@ -212,7 +216,7 @@
     return pl.pallas_call(
         yee_kernel,
         out_shape=[block] * 4 + [jax.ShapeDtypeStruct((STEPS, 4) + cells[1:], jnp.float32)],
-        in_specs=[SMEM, VMEM] + [VMEM] * len(blocks),
+        in_specs=[SMEM, SMEM] + [VMEM] * len(blocks),
         out_specs=[VMEM] * 5,
         scratch_shapes=[state, state, pltpu.VMEM((4,) + wide, jnp.float32)],
         compiler_params=pltpu.CompilerParams(vmem_limit_bytes=20 * 1024 * 1024),
@@ -292,7 +296,9 @@
         def mul(a, b):
             return jnp.dot(a, b, preferred_element_type=jnp.float32)
 
-        table = mul(left_high, high) + (mul(left_high, low) + mul(left_low, high))
+        table = mul(
+            jnp.concatenate([left_high, left_low], axis=1), jnp.concatenate([high, high], axis=0)
+        ) + mul(left_high, low)
         part_real = table[:half, :count] - table[half:, count:]
         part_imag = table[:half, count:] + table[half:, :count]
         cos_y, sin_y = cosy_ref[f], siny_ref[f]
@@ -305,7 +311,7 @@
             rows_ref[4 + c, pl.ds(f, 1), :] = sign * out_imag
         return carry
 
-    lax.fori_loop(0, freqs, one, 0)
+    lax.fori_loop(0, freqs, one, 0, unroll=8)
     half_count = count // 2
     rows = jnp.concatenate(
         [rows_ref[c, :, k * half_count : (k + 1) * half_count] for k in range(2) for c in range(8)],
@@ -370,14 +376,13 @@
     rows, cols = lax.axis_size("rows"), lax.axis_size("cols")
 
     own, first, final = pack(e_field, h_field, polar, polar_rate, material_id)
+    yhi = shifted(first, "cols", -1)
     ylo = shifted(final, "cols", 1)
-    yhi = shifted(first, "cols", -1)
     xhi = shifted(own, "rows", -1)
     xlo = shifted(own, "rows", 1)
-    corner_hl = shifted(ylo, "rows", -1)
-    corner_ll = shifted(ylo, "rows", 1)
-    corner_hh = shifted(yhi, "rows", -1)
-    corner_lh = shifted(yhi, "rows", 1)
+    sides = jnp.stack([ylo, yhi])
+    chi = shifted(sides, "rows", -1)
+    clo = shifted(sides, "rows", 1)
 
     plane_row = plane_index[0]
     root_row = plane_row // cells_x
@@ -410,7 +415,7 @@
     )
     cos_y, sin_y, cos_a, sin_a = waves
     e_out, h_out, p_out, j_out, samples = yee_steps(
-        where, table, own, ylo, yhi, xlo, xhi, corner_ll, corner_lh, corner_hl, corner_hh
+        where, table, own, ylo, yhi, xlo, xhi, clo, chi
     )
     received = spread_rows(samples, root_row)
     dft_out, partial_sum = radiate(

time: 125 us -> 117 us (0.936)
  waiting for transfers between devices: 25 us -> 33.5 us
  starting transfers between devices: 35 us -> 27.5 us
  Pallas kernels: 23.9 us -> 16.5 us
  blocking collectives: 33.7 us -> 31.7 us
    ppermute x8 -> x6, waiting for transfers between devices: 12.5 us -> 21 us  [shifted(): lax.ppermute(value, axis, [(source, source + steps) for source in range(f...]
    pallas_call x1, Pallas kernels: 16.5 us -> 10.4 us  [yee_steps(): pl.pallas_call(yee_kernel, out_shape=[block] * 4 + [jax.ShapeDtypeStruct(...]
    ppermute x8 -> x6, starting transfers between devices: 22.6 us -> 17.1 us  [shifted(): lax.ppermute(value, axis, [(source, source + steps) for source in range(f...]
    all_to_all x1, starting transfers between devices: 8.27 us -> 6.27 us  [spread_rows(): lax.all_to_all(pieces, 'rows', split_axis=0, concat_axis=0, tiled=True)]
    all_to_all x1, blocking collectives: 33.7 us -> 31.7 us  [local(): lax.all_to_all(pieces, 'cols', split_axis=0, concat_axis=0, tiled=True)]
    pallas_call x1, Pallas kernels: 3.64 us -> 2.29 us  [radiate(): pl.pallas_call(radiation_kernel, out_shape=[jax.ShapeDtypeStruct(acc.shap...]
  transfers between devices with their start and end apart: 10 -> 8, of which waited for: 5 -> 6; matrix products, arithmetic and copies ran while one was open for 2% -> 2% of each run, Pallas kernels for 0% -> 0%
where the time goes in v4:
time: 117 us; the launch traced here: 116 us
  waiting for transfers between devices  33.5 us (29%)
  blocking collectives  31.7 us (27%)
  starting transfers between devices  27.5 us (24%)
  Pallas kernels  16.5 us (14%)
  local copies, waits for them, and re-layouts  3.86 us (3%)
  other arithmetic  1.69 us (1%)
  between operations  1.55 us (1%)
    all_to_all x1, blocking collectives, local(): lax.all_to_all(pieces, 'cols', split_axis=0, concat_axis=0, tiled=True)  31.7 us
    ppermute x6, waiting for transfers between devices, shifted(): lax.ppermute(value, axis, [(source, source + steps) for source in range(f...  21 us
    ppermute x6, starting transfers between devices, shifted(): lax.ppermute(value, axis, [(source, source + steps) for source in range(f...  17.1 us
    pallas_call x1, Pallas kernels, yee_steps(): pl.pallas_call(yee_kernel, out_shape=[block] * 4 + [jax.ShapeDtypeStruct(...  10.4 us
    all_to_all x1, waiting for transfers between devices, spread_rows(): lax.all_to_all(copies, 'rows', split_axis=0, concat_axis=0, tiled=True)  6.35 us
    all_to_all x1, starting transfers between devices, spread_rows(): lax.all_to_all(pieces, 'rows', split_axis=0, concat_axis=0, tiled=True)  6.27 us
    all_to_all x1, waiting for transfers between devices, spread_rows(): lax.all_to_all(pieces, 'rows', split_axis=0, concat_axis=0, tiled=True)  6.17 us
    all_to_all x1, starting transfers between devices, spread_rows(): lax.all_to_all(copies, 'rows', split_axis=0, concat_axis=0, tiled=True)  4.2 us
  transfers between devices with their start and end apart: 8, of which 6 were waited for; matrix products, arithmetic and copies ran while one was open for 2% of the time, Pallas kernels for 0%

profile of v4, /device:TPU:1, one launch (start us, length us, event | category | flops | bytes accessed | tf_op | source)
XLA Modules:
  0.0 116.3 jit_solution(1278118877139776748)
XLA Ops:
  0.6 2.5 %pack.1 = (f32[13,8,16,128]{3,2,1,0:T(8,128)S(1)}, f32[13,8,8,128]{3,2,1,0:T(8,128)}, f32[13,8,8,128]{3,2,1,0:T(8,128)}) custom-call(f32[3,8,16,128]{3,2,1,0:T(8,128)} %e_ref.1, f32[3,8,16,128]{3,2,1,0:T(8,128)} %h_ref.1, f32[3,8,16,128]{3,2,1,0:T(8,128)} %p_ref.1, f32[3,8,16,128]{3,2,1,0:T(8,128)} %j_ref.1, s32[8,16,128]{2,1,0:T(8,128)} %m_ref.1), custom_call_target="tpu_custom_call" | custom-call | tf_op jit(solution)/shard_map/pack/pallas_call | solution.py:66
  3.2 4.5 %collective-permute-start.2 = (f32[13,8,16,128]{3,2,1,0:T(8,128)S(1)}, f32[13,8,16,128]{3,2,1,0:T(8,128)S(1)}, u32[]{:S(2)}, u32[]{:S(2)}) collective-permute-start(f32[13,8,16,128]{3,2,1,0:T(8,128)S(1)} %get-tuple-element.18.own_ref), channel_id=1, source_target_pairs={{0,32},{32,64},{64,96},{96,128},{128,160},{160,192},{192,224},{224... | collective-permute-start | bytes 2555912 | tf_op jit(solution)/shard_map/ppermute | solution.py:29
  7.7 5.6 %collective-permute-start.3 = (f32[13,8,16,128]{3,2,1,0:T(8,128)S(1)}, f32[13,8,16,128]{3,2,1,0:T(8,128)S(1)}, u32[]{:S(2)}, u32[]{:S(2)}) collective-permute-start(f32[13,8,16,128]{3,2,1,0:T(8,128)S(1)} %get-tuple-element.18.own_ref), channel_id=1, source_target_pairs={{32,0},{64,32},{96,64},{128,96},{160,128},{192,160},{224,192},{256... | collective-permute-start | bytes 2555912 | tf_op jit(solution)/shard_map/ppermute | solution.py:29
  13.3 1.3 %collective-permute-start = (f32[13,8,8,128]{3,2,1,0:T(8,128)}, f32[13,8,8,128]{3,2,1,0:T(8,128)S(1)}, u32[]{:S(2)}, u32[]{:S(2)}) collective-permute-start(f32[13,8,8,128]{3,2,1,0:T(8,128)} %get-tuple-element.19), channel_id=1, source_target_pairs={{0,1},{1,2},{2,3},{3,4},{4,5},{5,6},{6,7},{7,8},{8,9},{9,10},{10,1... | collective-permute-start | bytes 1277960 | tf_op jit(solution)/shard_map/ppermute | solution.py:29
  14.6 1.3 %collective-permute-start.1 = (f32[13,8,8,128]{3,2,1,0:T(8,128)}, f32[13,8,8,128]{3,2,1,0:T(8,128)S(1)}, u32[]{:S(2)}, u32[]{:S(2)}) collective-permute-start(f32[13,8,8,128]{3,2,1,0:T(8,128)} %get-tuple-element.20), channel_id=1, source_target_pairs={{1,0},{2,1},{3,2},{4,3},{5,4},{6,5},{7,6},{8,7},{9,8},{10,9},{11,1... | collective-permute-start | bytes 1277960 | tf_op jit(solution)/shard_map/ppermute | solution.py:29
  16.6 0.1 stack.64
  16.7 0.1 reshape.197.where_ref
  16.8 0.0 copy-start.2
  16.8 0.7 copy-done.2
  17.5 0.1 convert_element_type.62
  17.6 0.1 convert_element_type.64
  17.7 0.0 copy-start.3
  17.8 0.0 copy-start.4
  17.8 0.6 copy-done.3
  18.4 0.0 copy-done.4
  18.4 0.0 copy-start.5
  18.4 0.0 copy-start.6
  18.5 0.6 copy-done.5
  19.1 0.0 copy-done.6
  19.1 4.9 %collective-permute-done.ylo_ref = f32[13,8,8,128]{3,2,1,0:T(8,128)S(1)} collective-permute-done((f32[13,8,8,128]{3,2,1,0:T(8,128)}, f32[13,8,8,128]{3,2,1,0:T(8,128)S(1)}, u32[]{:S(2)}, u32[]{:S(2)}) %collective-permute-start) | collective-permute-done | bytes 426016 | tf_op jit(solution)/shard_map/ppermute | solution.py:29
  24.1 4.2 %collective-permute-done.1.yhi_ref = f32[13,8,8,128]{3,2,1,0:T(8,128)S(1)} collective-permute-done((f32[13,8,8,128]{3,2,1,0:T(8,128)}, f32[13,8,8,128]{3,2,1,0:T(8,128)S(1)}, u32[]{:S(2)}, u32[]{:S(2)}) %collective-permute-start.1) | collective-permute-done | bytes 426016 | tf_op jit(solution)/shard_map/ppermute | solution.py:29
  28.2 0.1 pad_maximum_fusion
  28.3 2.5 %collective-permute-start.4 = (f32[2,13,8,8,128]{4,3,2,1,0:T(8,128)S(1)}, f32[2,13,8,8,128]{4,3,2,1,0:T(8,128)S(1)}, u32[]{:S(2)}, u32[]{:S(2)}) collective-permute-start(f32[2,13,8,8,128]{4,3,2,1,0:T(8,128)S(1)} %pad_maximum_fusion), channel_id=1, source_target_pairs={{0,32},{32,64},{64,96},{96,128},{128,160},{160,192},{192,224},{224... | collective-permute-start | bytes 2555912 | tf_op jit(solution)/shard_map/ppermute | solution.py:29
  30.8 1.9 %collective-permute-start.5 = (f32[2,13,8,8,128]{4,3,2,1,0:T(8,128)S(1)}, f32[2,13,8,8,128]{4,3,2,1,0:T(8,128)S(1)}, u32[]{:S(2)}, u32[]{:S(2)}) collective-permute-start(f32[2,13,8,8,128]{4,3,2,1,0:T(8,128)S(1)} %pad_maximum_fusion), channel_id=1, source_target_pairs={{32,0},{64,32},{96,64},{128,96},{160,128},{192,160},{224,192},{256... | collective-permute-start | bytes 2555912 | tf_op jit(solution)/shard_map/ppermute | solution.py:29
  32.7 0.1 broadcast_multiply_fusion.1
  32.8 0.1 multiply_add_fusion
  32.9 0.0 collective-permute-done.2.xlo_ref
  32.9 0.0 collective-permute-done.3.xhi_ref
  32.9 7.5 %collective-permute-done.4.clo_ref = f32[2,13,8,8,128]{4,3,2,1,0:T(8,128)S(1)} collective-permute-done((f32[2,13,8,8,128]{4,3,2,1,0:T(8,128)S(1)}, f32[2,13,8,8,128]{4,3,2,1,0:T(8,128)S(1)}, u32[]{:S(2)}, u32[]{:S(2)}) %collective-permute-start.4) | collective-permute-done | bytes 852000 | tf_op jit(solution)/shard_map/ppermute | solution.py:29
  40.4 4.4 %collective-permute-done.5.chi_ref = f32[2,13,8,8,128]{4,3,2,1,0:T(8,128)S(1)} collective-permute-done((f32[2,13,8,8,128]{4,3,2,1,0:T(8,128)S(1)}, f32[2,13,8,8,128]{4,3,2,1,0:T(8,128)S(1)}, u32[]{:S(2)}, u32[]{:S(2)}) %collective-permute-start.5) | collective-permute-done | bytes 852000 | tf_op jit(solution)/shard_map/ppermute | solution.py:29
  44.8 10.4 %yee_steps.1 = (f32[3,8,16,128]{3,2,1,0:T(8,128)}, f32[3,8,16,128]{3,2,1,0:T(8,128)}, f32[3,8,16,128]{3,2,1,0:T(8,128)}, f32[3,8,16,128]{3,2,1,0:T(8,128)}, f32[8,4,16,128]{3,2,1,0:T(8,128)S(1)}) custom-call(s32[3,2]{1,0:T(4,128)S(1)} %reshape.197.where_ref, f32[4,8]{1,0:T(4,128)S(1)} %pad_maximum_fusion.1.table_ref, ...), custom_call_target="tpu_custom_call" | custom-call | tf_op jit(solution)/shard_map/yee_steps/pallas_call | solution.py:216
  55.1 0.0 copy-start.1
  55.1 0.7 copy-done.1
  55.9 6.3 %all-to-all-start = ((f32[16,32,128]{2,1,0:T(8,128)}), f32[16,32,128]{2,1,0:T(8,128)S(1)}, u32[]{:S(2)}, u32[]{:S(2)}) async-start(f32[16,32,128]{2,1,0:T(8,128)} %bitcast.38), calls=%async_computation | async-start | bytes 524288 | tf_op jit(solution)/shard_map/all_to_all | solution.py:362
  62.2 1.0 multiply_sine_fusion
  63.1 6.2 %all-to-all-done = f32[16,32,128]{2,1,0:T(8,128)S(1)} async-done(((f32[16,32,128]{2,1,0:T(8,128)}), f32[16,32,128]{2,1,0:T(8,128)S(1)}, u32[]{:S(2)}, u32[]{:S(2)}) %all-to-all-start) | async-done | bytes 262176 | tf_op jit(solution)/shard_map/all_to_all | solution.py:362
  69.3 0.7 broadcast_in_dim.5
  70.1 0.0 copy-start
  70.1 4.2 %all-to-all-start.1 = ((f32[16,32,128]{2,1,0:T(8,128)}), f32[16,32,128]{2,1,0:T(8,128)S(1)}, u32[]{:S(2)}, u32[]{:S(2)}) async-start(f32[16,32,128]{2,1,0:T(8,128)} %broadcast_in_dim.5), calls=%async_computation.1 | async-start | bytes 524288 | tf_op jit(solution)/shard_map/all_to_all | solution.py:365
  74.3 0.3 multiply_sine_fusion.2
  74.6 0.5 z_phases.1
  75.1 0.1 multiply_sine_fusion.3
  75.2 6.3 %all-to-all-done.1 = f32[16,32,128]{2,1,0:T(8,128)S(1)} async-done(((f32[16,32,128]{2,1,0:T(8,128)}), f32[16,32,128]{2,1,0:T(8,128)S(1)}, u32[]{:S(2)}, u32[]{:S(2)}) %all-to-all-start.1) | async-done | bytes 262176 | tf_op jit(solution)/shard_map/all_to_all | solution.py:365
  81.5 0.0 copy-done
  81.5 2.3 %radiate.1 = (f32[8,8,16,128]{3,2,1,0:T(8,128)}, f32[128,128]{1,0:T(8,128)S(1)}) custom-call(f32[8,8]{1,0:T(8,128)S(1)} %get-tuple-element.39.cos_ref, f32[8,8]{1,0:T(8,128)S(1)} %get-tuple-element.38.sin_ref, f32[8,4,16,128]{3,2,1,0:T(8,128)S(1)} %bitcast.37, f32[8,8,16,128]{3,2,1,0:T(8,128)S(1)} %copy-done, ...), custom_call_target="tpu_custom_call" | custom-call | tf_op jit(solution)/shard_map/radiate/pallas_call | solution.py:326
  83.8 31.7 %all_to_all.15.in_ref = f32[32,4,128]{2,1,0:T(4,128)S(1)} all-to-all(f32[32,4,128]{2,1,0:T(4,128)S(1)} %bitcast.39), channel_id=1, replica_groups=mesh['rows'=16,'cols'=32] {'cols'}, dimensions={0} | all-to-all | bytes 131072 | tf_op jit(solution)/shard_map/all_to_all | solution.py:425
  115.5 0.8 finish.1
  (12 shorter events, 0.1 us)
Async XLA Ops:
  3.2 29.7 %collective-permute-start.2 = (f32[13,8,16,128]{3,2,1,0:T(8,128)S(1)}, f32[13,8,16,128]{3,2,1,0:T(8,128)S(1)}, u32[]{:S(2)}, u32[]{:S(2)}) collective-permute-start(f32[13,8,16,128]{3,2,1,0:T(8,128)S(1)} %get-tuple-element.18.own_ref), channel_id=1, source_target_pairs={{0,32},{32,64},{64,96},{96,128},{128,160},{160,192},{192,224},{224... | collective-permute-start | bytes 2555912 | tf_op jit(solution)/shard_map/ppermute | solution.py:29
  7.7 25.2 %collective-permute-start.3 = (f32[13,8,16,128]{3,2,1,0:T(8,128)S(1)}, f32[13,8,16,128]{3,2,1,0:T(8,128)S(1)}, u32[]{:S(2)}, u32[]{:S(2)}) collective-permute-start(f32[13,8,16,128]{3,2,1,0:T(8,128)S(1)} %get-tuple-element.18.own_ref), channel_id=1, source_target_pairs={{32,0},{64,32},{96,64},{128,96},{160,128},{192,160},{224,192},{256... | collective-permute-start | bytes 2555912 | tf_op jit(solution)/shard_map/ppermute | solution.py:29
  13.3 10.8 %collective-permute-start = (f32[13,8,8,128]{3,2,1,0:T(8,128)}, f32[13,8,8,128]{3,2,1,0:T(8,128)S(1)}, u32[]{:S(2)}, u32[]{:S(2)}) collective-permute-start(f32[13,8,8,128]{3,2,1,0:T(8,128)} %get-tuple-element.19), channel_id=1, source_target_pairs={{0,1},{1,2},{2,3},{3,4},{4,5},{5,6},{6,7},{7,8},{8,9},{9,10},{10,1... | collective-permute-start | bytes 1277960 | tf_op jit(solution)/shard_map/ppermute | solution.py:29
  14.6 13.6 %collective-permute-start.1 = (f32[13,8,8,128]{3,2,1,0:T(8,128)}, f32[13,8,8,128]{3,2,1,0:T(8,128)S(1)}, u32[]{:S(2)}, u32[]{:S(2)}) collective-permute-start(f32[13,8,8,128]{3,2,1,0:T(8,128)} %get-tuple-element.20), channel_id=1, source_target_pairs={{1,0},{2,1},{3,2},{4,3},{5,4},{6,5},{7,6},{8,7},{9,8},{10,9},{11,1... | collective-permute-start | bytes 1277960 | tf_op jit(solution)/shard_map/ppermute | solution.py:29
  16.8 0.7 copy-start.2
  17.7 0.7 copy-start.3
  17.8 0.7 copy-start.4
  18.4 0.7 copy-start.5
  18.4 0.7 copy-start.6
  28.3 12.1 %collective-permute-start.4 = (f32[2,13,8,8,128]{4,3,2,1,0:T(8,128)S(1)}, f32[2,13,8,8,128]{4,3,2,1,0:T(8,128)S(1)}, u32[]{:S(2)}, u32[]{:S(2)}) collective-permute-start(f32[2,13,8,8,128]{4,3,2,1,0:T(8,128)S(1)} %pad_maximum_fusion), channel_id=1, source_target_pairs={{0,32},{32,64},{64,96},{96,128},{128,160},{160,192},{192,224},{224... | collective-permute-start | bytes 2555912 | tf_op jit(solution)/shard_map/ppermute | solution.py:29
  30.8 14.0 %collective-permute-start.5 = (f32[2,13,8,8,128]{4,3,2,1,0:T(8,128)S(1)}, f32[2,13,8,8,128]{4,3,2,1,0:T(8,128)S(1)}, u32[]{:S(2)}, u32[]{:S(2)}) collective-permute-start(f32[2,13,8,8,128]{4,3,2,1,0:T(8,128)S(1)} %pad_maximum_fusion), channel_id=1, source_target_pairs={{32,0},{64,32},{96,64},{128,96},{160,128},{192,160},{224,192},{256... | collective-permute-start | bytes 2555912 | tf_op jit(solution)/shard_map/ppermute | solution.py:29
  55.1 0.7 copy-start.1
  55.9 13.5 %all-to-all-start = ((f32[16,32,128]{2,1,0:T(8,128)}), f32[16,32,128]{2,1,0:T(8,128)S(1)}, u32[]{:S(2)}, u32[]{:S(2)}) async-start(f32[16,32,128]{2,1,0:T(8,128)} %bitcast.38), calls=%async_computation | async-start | bytes 524288 | tf_op jit(solution)/shard_map/all_to_all | solution.py:362
  70.1 11.5 %copy-start = (f32[8,8,16,128]{3,2,1,0:T(8,128)S(1)}, f32[8,8,16,128]{3,2,1,0:T(8,128)}, u32[]{:S(2)}) copy-start(f32[8,8,16,128]{3,2,1,0:T(8,128)} %acc_ref.1) | copy-start | bytes 1572868
  70.1 11.5 %all-to-all-start.1 = ((f32[16,32,128]{2,1,0:T(8,128)}), f32[16,32,128]{2,1,0:T(8,128)S(1)}, u32[]{:S(2)}, u32[]{:S(2)}) async-start(f32[16,32,128]{2,1,0:T(8,128)} %broadcast_in_dim.5), calls=%async_computation.1 | async-start | bytes 524288 | tf_op jit(solution)/shard_map/all_to_all | solution.py:365

commit v5 on v4

--- a/solution.py
+++ b/solution.py
@@ -38,26 +38,20 @@
 
 def pack_kernel(e_ref, h_ref, p_ref, j_ref, m_ref, own, first, final, mats, sems):
     cells_y = e_ref.shape[2]
-    spans = ((own, 0, cells_y), (first, 0, HALO), (final, cells_y - HALO, HALO))
-    copies = [pltpu.make_async_copy(m_ref, mats, sems.at[0])]
-    for i, ref in enumerate((e_ref, h_ref, p_ref, j_ref)):
-        for k, (out, start, size) in enumerate(spans):
-            copies.append(
-                pltpu.make_async_copy(
-                    ref.at[:, :, pl.ds(start, size), :],
-                    out.at[pl.ds(3 * i, 3)],
-                    sems.at[1 + 3 * i + k],
-                )
-            )
+    copies = [
+        pltpu.make_async_copy(ref, own.at[pl.ds(3 * i, 3)], sems.at[i])
+        for i, ref in enumerate((e_ref, h_ref, p_ref, j_ref))
+    ]
+    copies.append(pltpu.make_async_copy(m_ref, mats, sems.at[4]))
     for copy in copies:
         copy.start()
-    copies[0].wait()
-    ids = mats[...].astype(jnp.float32)
-    own[12] = ids
-    first[12] = ids[:, :HALO]
-    final[12] = ids[:, cells_y - HALO :]
-    for copy in copies[1:]:
+    for i, copy in enumerate(copies):
         copy.wait()
+        span = pl.ds(3 * i, 3) if i < 4 else pl.ds(12, 1)
+        if i == 4:
+            own[span] = mats[...].astype(jnp.float32)[None]
+        first[span] = own[span, :, :HALO, :]
+        final[span] = own[span, :, cells_y - HALO :, :]
 
 
 def pack(e_field, h_field, polar, polar_rate, material_id):
@@ -72,7 +66,7 @@
         out_specs=[VMEM] * 3,
         scratch_shapes=[
             pltpu.VMEM(material_id.shape, jnp.int32),
-            pltpu.SemaphoreType.DMA((13,)),
+            pltpu.SemaphoreType.DMA((5,)),
         ],
         compiler_params=pltpu.CompilerParams(vmem_limit_bytes=8 * 1024 * 1024),
         name="pack",
@@ -356,14 +350,15 @@
     )(arrived)
 
 
-def spread_rows(samples, root):
+def spread_rows(samples, root, beside):
     count = lax.axis_size("rows")
     pieces = samples.reshape(count, -1, samples.shape[-1])
     arrived = lax.all_to_all(pieces, "rows", split_axis=0, concat_axis=0, tiled=True)
     mine = lax.dynamic_index_in_dim(arrived, root, 0, keepdims=True)
+    mine, beside = lax.optimization_barrier((mine, beside))
     copies = jnp.broadcast_to(mine, pieces.shape)
     gathered = lax.all_to_all(copies, "rows", split_axis=0, concat_axis=0, tiled=True)
-    return gathered.reshape(samples.shape)
+    return gathered.reshape(samples.shape), beside
 
 
 def local(
@@ -406,18 +401,21 @@
     dir_x = jnp.sqrt(1.0 - dir_y * dir_y - dir_z * dir_z)
     pos_y = (col * cells_y + jnp.arange(cells_y, dtype=jnp.int32)).astype(jnp.float32)
     plane_x = plane_row.astype(jnp.float32)
+    e_out, h_out, p_out, j_out, samples = yee_steps(
+        where, table, own, ylo, yhi, xlo, xhi, clo, chi
+    )
+    samples, pos_y, omegas, dir_x, dir_y, dir_z, angles = lax.optimization_barrier(
+        (samples, pos_y, omegas, dir_x, dir_y, dir_z, angles)
+    )
     phase_y = (
         omegas[:, None, None] * (pos_y[:, None] * dir_y[None, :] + plane_x * dir_x[None, :])[None]
     )
     high, low = z_phases(omegas, dir_z, cells_z)
     waves = (
-        jnp.cos(phase_y), jnp.sin(phase_y), jnp.cos(angles), jnp.sin(angles),
-    )
-    cos_y, sin_y, cos_a, sin_a = waves
-    e_out, h_out, p_out, j_out, samples = yee_steps(
-        where, table, own, ylo, yhi, xlo, xhi, clo, chi
-    )
-    received = spread_rows(samples, root_row)
+        high, low, jnp.cos(phase_y), jnp.sin(phase_y), jnp.cos(angles), jnp.sin(angles),
+    )
+    received, waves = spread_rows(samples, root_row, waves)
+    high, low, cos_y, sin_y, cos_a, sin_a = waves
     dft_out, partial_sum = radiate(
         cos_a, sin_a, received, dft_acc, high, low, cos_y, sin_y,
     )

time: 117 us -> 115 us (0.983)
  blocking collectives: 31.7 us -> 42.1 us
  waiting for transfers between devices: 33.5 us -> 25.7 us
  starting transfers between devices: 27.5 us -> 23.3 us
    all_to_all x0 -> x1, blocking collectives: none -> 10.4 us  [spread_rows(): lax.all_to_all(copies, 'rows', split_axis=0, concat_axis=0, tiled=True)]
    all_to_all x1 -> x0, waiting for transfers between devices: 6.35 us -> none  [spread_rows(): lax.all_to_all(copies, 'rows', split_axis=0, concat_axis=0, tiled=True)]
    all_to_all x1 -> x0, starting transfers between devices: 4.2 us -> none  [spread_rows(): lax.all_to_all(copies, 'rows', split_axis=0, concat_axis=0, tiled=True)]
    unnamed x14 -> x16, local copies, waits for them, and re-layouts: 2.7 us -> 2.75 us
  transfers between devices with their start and end apart: 8 -> 7, of which waited for: 6 -> 5; matrix products, arithmetic and copies ran while one was open for 2% -> 2% of each run, Pallas kernels for 0% -> 0%
where the time goes in v5:
time: 115 us; the launch traced here: 114 us
  blocking collectives  42.1 us (37%)
  waiting for transfers between devices  25.7 us (22%)
  starting transfers between devices  23.3 us (20%)
  Pallas kernels  16.2 us (14%)
  local copies, waits for them, and re-layouts  3.24 us (3%)
  other arithmetic  2.21 us (2%)
  between operations  1.56 us (1%)
    all_to_all x1, blocking collectives, local(): lax.all_to_all(pieces, 'cols', split_axis=0, concat_axis=0, tiled=True)  31.7 us
    ppermute x6, waiting for transfers between devices, shifted(): lax.ppermute(value, axis, [(source, source + steps) for source in range(f...  20.5 us
    ppermute x6, starting transfers between devices, shifted(): lax.ppermute(value, axis, [(source, source + steps) for source in range(f...  17.1 us
    all_to_all x1, blocking collectives, spread_rows(): lax.all_to_all(copies, 'rows', split_axis=0, concat_axis=0, tiled=True)  10.4 us
    pallas_call x1, Pallas kernels, yee_steps(): pl.pallas_call(yee_kernel, out_shape=[block] * 4 + [jax.ShapeDtypeStruct(...  10.4 us
    all_to_all x1, starting transfers between devices, spread_rows(): lax.all_to_all(pieces, 'rows', split_axis=0, concat_axis=0, tiled=True)  6.27 us
    all_to_all x1, waiting for transfers between devices, spread_rows(): lax.all_to_all(pieces, 'rows', split_axis=0, concat_axis=0, tiled=True)  5.26 us
    unnamed x16, local copies, waits for them, and re-layouts  2.75 us
  transfers between devices with their start and end apart: 7, of which 5 were waited for; matrix products, arithmetic and copies ran while one was open for 2% of the time, Pallas kernels for 0%

profile of v5, /device:TPU:1, one launch (start us, length us, event | category | flops | bytes accessed | tf_op | source)
XLA Modules:
  0.0 114.4 jit_solution(698871435069314735)
XLA Ops:
  0.6 2.2 %pack.1 = (f32[13,8,16,128]{3,2,1,0:T(8,128)S(1)}, f32[13,8,8,128]{3,2,1,0:T(8,128)}, f32[13,8,8,128]{3,2,1,0:T(8,128)}) custom-call(f32[3,8,16,128]{3,2,1,0:T(8,128)} %e_ref.1, f32[3,8,16,128]{3,2,1,0:T(8,128)} %h_ref.1, f32[3,8,16,128]{3,2,1,0:T(8,128)} %p_ref.1, f32[3,8,16,128]{3,2,1,0:T(8,128)} %j_ref.1, s32[8,16,128]{2,1,0:T(8,128)} %m_ref.1), custom_call_target="tpu_custom_call" | custom-call | tf_op jit(solution)/shard_map/pack/pallas_call | solution.py:60
  2.8 4.5 %collective-permute-start.2 = (f32[13,8,16,128]{3,2,1,0:T(8,128)S(1)}, f32[13,8,16,128]{3,2,1,0:T(8,128)S(1)}, u32[]{:S(2)}, u32[]{:S(2)}) collective-permute-start(f32[13,8,16,128]{3,2,1,0:T(8,128)S(1)} %get-tuple-element.32.own_ref), channel_id=1, source_target_pairs={{0,32},{32,64},{64,96},{96,128},{128,160},{160,192},{192,224},{224... | collective-permute-start | bytes 2555912 | tf_op jit(solution)/shard_map/ppermute | solution.py:29
  7.3 5.6 %collective-permute-start.3 = (f32[13,8,16,128]{3,2,1,0:T(8,128)S(1)}, f32[13,8,16,128]{3,2,1,0:T(8,128)S(1)}, u32[]{:S(2)}, u32[]{:S(2)}) collective-permute-start(f32[13,8,16,128]{3,2,1,0:T(8,128)S(1)} %get-tuple-element.32.own_ref), channel_id=1, source_target_pairs={{32,0},{64,32},{96,64},{128,96},{160,128},{192,160},{224,192},{256... | collective-permute-start | bytes 2555912 | tf_op jit(solution)/shard_map/ppermute | solution.py:29
  12.9 1.3 %collective-permute-start = (f32[13,8,8,128]{3,2,1,0:T(8,128)}, f32[13,8,8,128]{3,2,1,0:T(8,128)S(1)}, u32[]{:S(2)}, u32[]{:S(2)}) collective-permute-start(f32[13,8,8,128]{3,2,1,0:T(8,128)} %get-tuple-element.33), channel_id=1, source_target_pairs={{0,1},{1,2},{2,3},{3,4},{4,5},{5,6},{6,7},{7,8},{8,9},{9,10},{10,1... | collective-permute-start | bytes 1277960 | tf_op jit(solution)/shard_map/ppermute | solution.py:29
  14.3 1.3 %collective-permute-start.1 = (f32[13,8,8,128]{3,2,1,0:T(8,128)}, f32[13,8,8,128]{3,2,1,0:T(8,128)S(1)}, u32[]{:S(2)}, u32[]{:S(2)}) collective-permute-start(f32[13,8,8,128]{3,2,1,0:T(8,128)} %get-tuple-element.34), channel_id=1, source_target_pairs={{1,0},{2,1},{3,2},{4,3},{5,4},{6,5},{7,6},{8,7},{9,8},{10,9},{11,1... | collective-permute-start | bytes 1277960 | tf_op jit(solution)/shard_map/ppermute | solution.py:29
  16.3 0.1 stack.64
  16.4 0.0 copy-start.2
  16.4 0.1 reshape.161.where_ref
  16.5 0.5 add_multiply_fusion
  17.0 0.1 copy-done.2
  17.1 0.1 convert_element_type.53
  17.2 0.1 convert_element_type.55
  17.3 0.0 copy-start.4
  17.4 0.0 copy-start.5
  17.4 0.6 copy-done.4
  18.0 0.0 copy-done.5
  18.0 0.0 copy-start.6
  18.0 0.0 copy-start.7
  18.0 0.6 copy-done.6
  18.7 0.0 copy-done.7
  18.7 5.0 %collective-permute-done.ylo_ref = f32[13,8,8,128]{3,2,1,0:T(8,128)S(1)} collective-permute-done((f32[13,8,8,128]{3,2,1,0:T(8,128)}, f32[13,8,8,128]{3,2,1,0:T(8,128)S(1)}, u32[]{:S(2)}, u32[]{:S(2)}) %collective-permute-start) | collective-permute-done | bytes 426016 | tf_op jit(solution)/shard_map/ppermute | solution.py:29
  23.7 4.2 %collective-permute-done.1.yhi_ref = f32[13,8,8,128]{3,2,1,0:T(8,128)S(1)} collective-permute-done((f32[13,8,8,128]{3,2,1,0:T(8,128)}, f32[13,8,8,128]{3,2,1,0:T(8,128)S(1)}, u32[]{:S(2)}, u32[]{:S(2)}) %collective-permute-start.1) | collective-permute-done | bytes 426016 | tf_op jit(solution)/shard_map/ppermute | solution.py:29
  27.9 0.1 pad_maximum_fusion
  27.9 2.5 %collective-permute-start.4 = (f32[2,13,8,8,128]{4,3,2,1,0:T(8,128)S(1)}, f32[2,13,8,8,128]{4,3,2,1,0:T(8,128)S(1)}, u32[]{:S(2)}, u32[]{:S(2)}) collective-permute-start(f32[2,13,8,8,128]{4,3,2,1,0:T(8,128)S(1)} %pad_maximum_fusion), channel_id=1, source_target_pairs={{0,32},{32,64},{64,96},{96,128},{128,160},{160,192},{192,224},{224... | collective-permute-start | bytes 2555912 | tf_op jit(solution)/shard_map/ppermute | solution.py:29
  30.4 1.9 %collective-permute-start.5 = (f32[2,13,8,8,128]{4,3,2,1,0:T(8,128)S(1)}, f32[2,13,8,8,128]{4,3,2,1,0:T(8,128)S(1)}, u32[]{:S(2)}, u32[]{:S(2)}) collective-permute-start(f32[2,13,8,8,128]{4,3,2,1,0:T(8,128)S(1)} %pad_maximum_fusion), channel_id=1, source_target_pairs={{32,0},{64,32},{96,64},{128,96},{160,128},{192,160},{224,192},{256... | collective-permute-start | bytes 2555912 | tf_op jit(solution)/shard_map/ppermute | solution.py:29
  32.4 0.0 copy-start.3
  32.4 0.6 copy-done.3
  33.1 0.1 broadcast_multiply_fusion.2
  33.1 0.0 collective-permute-done.2.xlo_ref
  33.1 0.0 collective-permute-done.3.xhi_ref
  33.1 6.9 %collective-permute-done.4.clo_ref = f32[2,13,8,8,128]{4,3,2,1,0:T(8,128)S(1)} collective-permute-done((f32[2,13,8,8,128]{4,3,2,1,0:T(8,128)S(1)}, f32[2,13,8,8,128]{4,3,2,1,0:T(8,128)S(1)}, u32[]{:S(2)}, u32[]{:S(2)}) %collective-permute-start.4) | collective-permute-done | bytes 852000 | tf_op jit(solution)/shard_map/ppermute | solution.py:29
  40.0 4.4 %collective-permute-done.5.chi_ref = f32[2,13,8,8,128]{4,3,2,1,0:T(8,128)S(1)} collective-permute-done((f32[2,13,8,8,128]{4,3,2,1,0:T(8,128)S(1)}, f32[2,13,8,8,128]{4,3,2,1,0:T(8,128)S(1)}, u32[]{:S(2)}, u32[]{:S(2)}) %collective-permute-start.5) | collective-permute-done | bytes 852000 | tf_op jit(solution)/shard_map/ppermute | solution.py:29
  44.4 10.4 %yee_steps.1 = (f32[3,8,16,128]{3,2,1,0:T(8,128)}, f32[3,8,16,128]{3,2,1,0:T(8,128)}, f32[3,8,16,128]{3,2,1,0:T(8,128)}, f32[3,8,16,128]{3,2,1,0:T(8,128)}, f32[8,4,16,128]{3,2,1,0:T(8,128)S(1)}) custom-call(s32[3,2]{1,0:T(4,128)S(1)} %reshape.161.where_ref, f32[4,8]{1,0:T(4,128)S(1)} %pad_maximum_fusion.1.table_ref, ...), custom_call_target="tpu_custom_call" | custom-call | tf_op jit(solution)/shard_map/yee_steps/pallas_call | solution.py:210
  54.8 0.7 copy-done.1
  55.5 0.1 broadcast_multiply_fusion
  55.6 0.1 broadcast_multiply_fusion.1
  55.6 6.3 %all-to-all-start = ((f32[16,32,128]{2,1,0:T(8,128)}), f32[16,32,128]{2,1,0:T(8,128)S(1)}, u32[]{:S(2)}, u32[]{:S(2)}) async-start(f32[16,32,128]{2,1,0:T(8,128)} %bitcast.37), calls=%async_computation | async-start | bytes 524288 | tf_op jit(solution)/shard_map/all_to_all | solution.py:356
  61.9 0.1 multiply_add_fusion
  62.0 1.0 multiply_sine_fusion
  63.0 0.3 multiply_sine_fusion.2
  63.3 0.5 z_phases.1
  63.8 0.0 copy-start
  63.9 5.3 %all-to-all-done = f32[16,32,128]{2,1,0:T(8,128)S(1)} async-done(((f32[16,32,128]{2,1,0:T(8,128)}), f32[16,32,128]{2,1,0:T(8,128)S(1)}, u32[]{:S(2)}, u32[]{:S(2)}) %all-to-all-start) | async-done | bytes 262176 | tf_op jit(solution)/shard_map/all_to_all | solution.py:356
  69.1 10.4 %all_to_all.15 = f32[16,32,128]{2,1,0:T(8,128)S(1)} all-to-all(f32[16,32,128]{2,1,0:T(8,128)S(1)} %broadcast_in_dim.5), channel_id=1, replica_groups=mesh['rows'=16,'cols'=32] {'rows'}, dimensions={0} | all-to-all | bytes 524288 | tf_op jit(solution)/shard_map/all_to_all | solution.py:360
  79.6 0.0 copy-done
  79.6 2.3 %radiate.1 = (f32[8,8,16,128]{3,2,1,0:T(8,128)}, f32[128,128]{1,0:T(8,128)S(1)}) custom-call(f32[8,8]{1,0:T(8,128)S(1)} %get-tuple-element.49.cos_ref, f32[8,8]{1,0:T(8,128)S(1)} %get-tuple-element.50.sin_ref, f32[8,4,16,128]{3,2,1,0:T(8,128)S(1)} %bitcast.36, f32[8,8,16,128]{3,2,1,0:T(8,128)S(1)} %copy-done, ...), custom_call_target="tpu_custom_call" | custom-call | tf_op jit(solution)/shard_map/radiate/pallas_call | solution.py:320
  81.9 31.7 %all_to_all.16.in_ref = f32[32,4,128]{2,1,0:T(4,128)S(1)} all-to-all(f32[32,4,128]{2,1,0:T(4,128)S(1)} %bitcast.38), channel_id=1, replica_groups=mesh['rows'=16,'cols'=32] {'cols'}, dimensions={0} | all-to-all | bytes 131072 | tf_op jit(solution)/shard_map/all_to_all | solution.py:423
  113.6 0.8 finish.1
  (15 shorter events, 0.1 us)
Async XLA Ops:
  2.8 30.3 %collective-permute-start.2 = (f32[13,8,16,128]{3,2,1,0:T(8,128)S(1)}, f32[13,8,16,128]{3,2,1,0:T(8,128)S(1)}, u32[]{:S(2)}, u32[]{:S(2)}) collective-permute-start(f32[13,8,16,128]{3,2,1,0:T(8,128)S(1)} %get-tuple-element.32.own_ref), channel_id=1, source_target_pairs={{0,32},{32,64},{64,96},{96,128},{128,160},{160,192},{192,224},{224... | collective-permute-start | bytes 2555912 | tf_op jit(solution)/shard_map/ppermute | solution.py:29
  7.3 25.8 %collective-permute-start.3 = (f32[13,8,16,128]{3,2,1,0:T(8,128)S(1)}, f32[13,8,16,128]{3,2,1,0:T(8,128)S(1)}, u32[]{:S(2)}, u32[]{:S(2)}) collective-permute-start(f32[13,8,16,128]{3,2,1,0:T(8,128)S(1)} %get-tuple-element.32.own_ref), channel_id=1, source_target_pairs={{32,0},{64,32},{96,64},{128,96},{160,128},{192,160},{224,192},{256... | collective-permute-start | bytes 2555912 | tf_op jit(solution)/shard_map/ppermute | solution.py:29
  12.9 10.8 %collective-permute-start = (f32[13,8,8,128]{3,2,1,0:T(8,128)}, f32[13,8,8,128]{3,2,1,0:T(8,128)S(1)}, u32[]{:S(2)}, u32[]{:S(2)}) collective-permute-start(f32[13,8,8,128]{3,2,1,0:T(8,128)} %get-tuple-element.33), channel_id=1, source_target_pairs={{0,1},{1,2},{2,3},{3,4},{4,5},{5,6},{6,7},{7,8},{8,9},{9,10},{10,1... | collective-permute-start | bytes 1277960 | tf_op jit(solution)/shard_map/ppermute | solution.py:29
  14.3 13.6 %collective-permute-start.1 = (f32[13,8,8,128]{3,2,1,0:T(8,128)}, f32[13,8,8,128]{3,2,1,0:T(8,128)S(1)}, u32[]{:S(2)}, u32[]{:S(2)}) collective-permute-start(f32[13,8,8,128]{3,2,1,0:T(8,128)} %get-tuple-element.34), channel_id=1, source_target_pairs={{1,0},{2,1},{3,2},{4,3},{5,4},{6,5},{7,6},{8,7},{9,8},{10,9},{11,1... | collective-permute-start | bytes 1277960 | tf_op jit(solution)/shard_map/ppermute | solution.py:29
  16.4 0.7 copy-start.2
  17.3 0.7 copy-start.4
  17.4 0.7 copy-start.5
  18.0 0.7 copy-start.6
  18.0 0.7 copy-start.7
  27.9 12.1 %collective-permute-start.4 = (f32[2,13,8,8,128]{4,3,2,1,0:T(8,128)S(1)}, f32[2,13,8,8,128]{4,3,2,1,0:T(8,128)S(1)}, u32[]{:S(2)}, u32[]{:S(2)}) collective-permute-start(f32[2,13,8,8,128]{4,3,2,1,0:T(8,128)S(1)} %pad_maximum_fusion), channel_id=1, source_target_pairs={{0,32},{32,64},{64,96},{96,128},{128,160},{160,192},{192,224},{224... | collective-permute-start | bytes 2555912 | tf_op jit(solution)/shard_map/ppermute | solution.py:29
  30.4 14.0 %collective-permute-start.5 = (f32[2,13,8,8,128]{4,3,2,1,0:T(8,128)S(1)}, f32[2,13,8,8,128]{4,3,2,1,0:T(8,128)S(1)}, u32[]{:S(2)}, u32[]{:S(2)}) collective-permute-start(f32[2,13,8,8,128]{4,3,2,1,0:T(8,128)S(1)} %pad_maximum_fusion), channel_id=1, source_target_pairs={{32,0},{64,32},{96,64},{128,96},{160,128},{192,160},{224,192},{256... | collective-permute-start | bytes 2555912 | tf_op jit(solution)/shard_map/ppermute | solution.py:29
  32.4 0.7 copy-start.3
  54.8 0.7 copy-start.1
  55.6 13.5 %all-to-all-start = ((f32[16,32,128]{2,1,0:T(8,128)}), f32[16,32,128]{2,1,0:T(8,128)S(1)}, u32[]{:S(2)}, u32[]{:S(2)}) async-start(f32[16,32,128]{2,1,0:T(8,128)} %bitcast.37), calls=%async_computation | async-start | bytes 524288 | tf_op jit(solution)/shard_map/all_to_all | solution.py:356
  63.8 15.8 %copy-start = (f32[8,8,16,128]{3,2,1,0:T(8,128)S(1)}, f32[8,8,16,128]{3,2,1,0:T(8,128)}, u32[]{:S(2)}) copy-start(f32[8,8,16,128]{3,2,1,0:T(8,128)} %acc_ref.1) | copy-start | bytes 1572868
